TPU v7x, 128 devices: a whole 4x4x4 slice. The times are simulated.
128 devices in a mesh: tile: 16 (over y_lo, z, core), mem: 8 (over y_hi, x).
Axes of the slice: x: 4, y: 4 (y_hi: 2, y_lo: 2; y = y_hi * 2 + y_lo), z: 4, core: 2. Of those that a mesh axis runs over, the one named last changes fastest.
Arguments:
- anomalies: bfloat16 [64, 2, 32, 65536], P('mem', None, None, 'tile'), may hold values from -0.75 to 0.75
- alpha0: float32 [64, 32, 65536], P('mem', None, 'tile'), may hold values from -33 to 33
- chi0: float32 [32, 65536], P('mem', 'tile'), may hold values from -5 to 5
- sigma: float32 [32, 65536], P('mem', 'tile'), may hold values from 0.3 to 1.5
- innov: float32 [2, 32, 65536], P(None, None, 'tile'), may hold values from -6 to 6
- rinv: float32 [2, 32, 65536], P(None, None, 'tile'), may hold values from 0.25 to 4
- taper_cols: int32 [512, 6], P('tile'), may hold values from 0 to 511, as said below
- taper_coef: bfloat16 [512, 6, 128, 128], P('tile'), may hold values from -0.21875 to 0.21875
Outputs:
- alpha_next: float32 [64, 32, 65536], P('mem', None, 'tile')
- chi_next: float32 [32, 65536], P('mem', 'tile')
- grad_alpha: float32 [64, 32, 65536], P('mem', None, 'tile')
- grad_chi: float32 [32, 65536], P('mem', 'tile')
Inputs may be any that keep to these rules, and one draw needn't show every extreme that they name: `taper_cols`: block row i lists block i itself and 5 other distinct blocks whose cyclic distance from i (modulo 512) is at most 4, in no set order; on every device the first of its block rows lists the block 4 before it and the last lists the block 4 after it.
All inputs are finite; a program needn't handle non-finite values.
Results may differ from a plain program's by a relative error of at most 0.0085.
Values may be sent and summed in bfloat16 or wider, within the bound.
No kernel may reach another device: no remote copies, remote signals or barrier semaphores. Data moves between devices by JAX's collectives and lax.ppermute only.
A program may use at most 128 MiB of HBM per device.

v0:
```python
import jax
import jax.numpy as jnp
from jax import lax
from jax.sharding import PartitionSpec as P

W = 4


def extended(block, sides, width):
    for axis, dim in sides:
        count = lax.axis_size(axis)
        forward = [(i, i + 1) for i in range(count - 1)]
        forward.append((count - 1, 0))
        backward = [(target, source) for source, target in forward]
        low = lax.ppermute(
            lax.slice_in_dim(block, block.shape[dim] - width, None, axis=dim), axis, forward
        )
        high = lax.ppermute(lax.slice_in_dim(block, 0, width, axis=dim), axis, backward)
        block = jnp.concatenate([low, block, high], axis=dim)
    return block


def passed_along(array, axis, by):
    size = lax.axis_size(axis)
    return lax.ppermute(array, axis, [(i, (i + by) % size) for i in range(size)])


def body(anomalies, alpha0, chi0, sigma, innov, rinv, taper_cols, taper_coef):
    members, levels, columns = alpha0.shape
    block_size = taper_coef.shape[2]
    slot_count = taper_coef.shape[1]
    nblocks = columns // block_size
    rim_width = W
    padded_width = nblocks + 2 * rim_width
    first_block = lax.axis_index("tile") * nblocks
    total_blocks = nblocks * lax.axis_size("tile")
    local_cols = (taper_cols - first_block + rim_width) % total_blocks
    onehot = (
        local_cols[:, :, None] == jnp.arange(padded_width, dtype=jnp.int32)[None, None]
    ).astype(jnp.float32)
    lev_share = chi0.shape[0]
    level_start = lax.axis_index("mem") * lev_share

    def localize(alpha):
        rounded = alpha.astype(jnp.bfloat16).reshape(members, levels, nblocks, block_size)
        padded = extended(rounded, (("tile", 2),), rim_width)
        picked = jnp.take(padded, local_cols, axis=2)
        result = jnp.einsum(
            "ijpq,mlijq->mlip", taper_coef, picked, preferred_element_type=jnp.float32
        )
        return result.reshape(members, levels, columns)

    def adjoint(weighted):
        blocks = weighted.reshape(members, levels, nblocks, block_size)
        accumulated = jnp.zeros((members, levels, padded_width, block_size), jnp.float32)
        for column_slot in range(slot_count):
            part_term = jnp.einsum(
                "ipq,mlip->mliq",
                taper_coef[:, column_slot],
                blocks,
                preferred_element_type=jnp.float32,
            )
            accumulated = accumulated + jnp.einsum(
                "mliq,is->mlsq", part_term, onehot[:, column_slot], precision=lax.Precision.HIGHEST
            )
        interior = accumulated[:, :, rim_width : rim_width + nblocks]
        from_next = passed_along(
            accumulated[:, :, :rim_width].astype(jnp.bfloat16), "tile", -1
        ).astype(jnp.float32)
        from_prev = passed_along(
            accumulated[:, :, nblocks + rim_width :].astype(jnp.bfloat16), "tile", 1
        ).astype(jnp.float32)
        interior = interior.at[:, :, :rim_width].add(from_prev)
        interior = interior.at[:, :, nblocks - rim_width :].add(from_next)
        return interior.reshape(members, levels, columns)

    def evaluate(alpha, chi):
        localized = localize(alpha)
        ensemble_part = jnp.sum(anomalies.astype(jnp.float32) * localized[:, None], axis=0)
        static_part = sigma * chi
        spread_static = jnp.broadcast_to(
            static_part[None], (ensemble_part.shape[0], lev_share, columns)
        )
        placed = lax.dynamic_update_slice_in_dim(
            jnp.zeros_like(ensemble_part), spread_static, level_start, 1
        )
        combined = lax.psum(ensemble_part + placed, "mem")
        residual = (rinv * (combined - innov)).astype(jnp.bfloat16)
        own_resid = lax.dynamic_slice_in_dim(residual, level_start, lev_share, 1)
        weighted = jnp.einsum(
            "mtlc,tlc->mlc", anomalies, residual, preferred_element_type=jnp.float32
        ).astype(jnp.bfloat16)
        grad_alpha = alpha + adjoint(weighted)
        grad_chi = chi + sigma * jnp.sum(
            lax.optimization_barrier(own_resid).astype(jnp.float32), axis=0
        )
        return (grad_alpha, grad_chi)

    g_alpha, g_chi = evaluate(alpha0, chi0)
    local_norm = jnp.sum(g_alpha * g_alpha) + jnp.sum(g_chi * g_chi)
    grad_norm = lax.psum(local_norm, ("tile", "mem"))
    h_alpha, h_chi = evaluate(alpha0 - g_alpha, chi0 - g_chi)
    change_alpha = g_alpha - h_alpha
    change_chi = g_chi - h_chi
    local_change = jnp.sum(g_alpha * change_alpha) + jnp.sum(g_chi * change_chi)
    grad_change = lax.psum(local_change, ("tile", "mem"))
    step_length = grad_norm / grad_change
    return (
        alpha0 - step_length * g_alpha,
        chi0 - step_length * g_chi,
        g_alpha - step_length * change_alpha,
        g_chi - step_length * change_chi,
    )


def solution(mesh):
    placed = (
        P("mem", None, None, "tile"),
        P("mem", None, "tile"),
        P("mem", "tile"),
        P("mem", "tile"),
        P(None, None, "tile"),
        P(None, None, "tile"),
        P("tile", None),
        P("tile", None, None, None),
    )
    return jax.shard_map(
        body,
        mesh=mesh,
        in_specs=placed,
        out_specs=(
            P("mem", None, "tile"),
            P("mem", "tile"),
            P("mem", None, "tile"),
            P("mem", "tile"),
        ),
        check_vma=False,
    )
```

profile of v0, /device:TPU:1, one launch (start us, length us, event | category | flops | bytes accessed | tf_op | source)
XLA Modules:
  0.0 525.1 jit_solution(12769493760197025704)
XLA Ops:
  7.2 2.6 copy_bitcast_fusion.3
  11.2 3.1 collective-permute-start
  14.7 2.9 collective-permute-done
  17.6 2.8 collective-permute-done.1
  20.4 1.9 pad_maximum_fusion
  22.3 8.2 %gather_fusion = bf16[192,8,32,128]{3,2,1,0:T(8,128)(2,1)} fusion(bf16[8,32,40,128]{3,1,2,0:T(8,128)(2,1)S(1)} %pad_maximum_fusion, s32[1024]{0:T(1024)S(1)} %pad_clamp_fusion), kind=kCustom, calls=%fused_computation.clone | custom fusion | bytes 25166592 | tf_op jit(solution)/shard_map/jit(_take)/gather | solution.py:47
  30.6 11.8 %fusion.44 = f32[32,8,4,8,128]{4,3,2,1,0:T(8,128)} fusion(bf16[32,6,128,128]{3,2,1,0:T(8,128)(2,1)} %param.25, bf16[32,6,8,32,128]{4,3,2,1,0:T(8,128)(2,1)} %bitcast.237, pred[32,6]{1,0:T(8,128)(4,1)S(1)} %copy.54), kind=kOutput, calls=%fused_computation.69 | convolution fusion | flops 1616904192 | bytes 23068864 | tf_op jit(solution)/shard_map/ijpq,mlijq->mlip/dot_general | solution.py:48
  42.4 2.8 copy.202
  48.2 83.5 %all-reduce.4.cloned.1.call-done = f32[2,32,4096]{2,1,0:T(8,128)} async-done(((f32[2,32,4096]{2,1,0:T(8,128)}), f32[2,32,4096]{2,1,0:T(8,128)}) %all-reduce.4.cloned.1.call-update) | async-done | bytes 1048592 | tf_op jit(solution)/shard_map/psum | solution.py:87
  131.7 2.4 bitcast_convert_fusion.1
  138.2 3.4 convolution_bitcast_fusion.9
  145.7 3.4 convolution_bitcast_fusion.11
  149.0 5.6 %fusion.36 = f32[40,8,32,128]{3,0,2,1:T(8,128)S(1)} fusion(f32[8,32,32,128]{3,0,1,2:T(8,128)S(1)} %convolution_bitcast_fusion.10, pred[32,6,40]{2,0,1:T(32,128)(4,1)S(1)} %iota_compare_fusion), kind=kOutput, calls=%fused_computation.46 | convolution fusion | flops 503316480 | bytes 9441280 | tf_op jit(solution)/shard_map/mliq,is->mlsq/dot_general | solution.py:63
  154.7 5.2 fusion.34
  159.9 6.2 %fusion.32 = f32[40,8,32,128]{3,0,2,1:T(8,128)} fusion(f32[8,32,32,128]{3,0,1,2:T(8,128)S(1)} %convolution_bitcast_fusion.8, pred[32,6,40]{2,0,1:T(32,128)(4,1)S(1)} %iota_compare_fusion), kind=kOutput, calls=%fused_computation.42 | convolution fusion | flops 503316480 | bytes 9441280 | tf_op jit(solution)/shard_map/mliq,is->mlsq/dot_general | solution.py:63
  166.2 6.2 %fusion.30 = f32[40,8,32,128]{3,0,2,1:T(8,128)} fusion(f32[8,32,32,128]{3,0,1,2:T(8,128)S(1)} %convolution_bitcast_fusion.7, pred[32,6,40]{2,0,1:T(32,128)(4,1)S(1)} %iota_compare_fusion), kind=kOutput, calls=%fused_computation.40 | convolution fusion | flops 503316480 | bytes 9441280 | tf_op jit(solution)/shard_map/mliq,is->mlsq/dot_general | solution.py:63
  172.3 6.3 %fusion.28 = f32[40,8,32,128]{3,0,2,1:T(8,128)} fusion(f32[8,32,32,128]{3,0,1,2:T(8,128)S(1)} %convolution_bitcast_fusion.6, pred[32,6,40]{2,0,1:T(32,128)(4,1)S(1)} %iota_compare_fusion), kind=kOutput, calls=%fused_computation.38 | convolution fusion | flops 503316480 | bytes 9441280 | tf_op jit(solution)/shard_map/mliq,is->mlsq/dot_general | solution.py:63
  178.6 15.9 %fusion.102 = (bf16[8,32,40,128]{3,2,1,0:T(8,128)(2,1)S(1)}, f32[8,32,40,128]{3,2,1,0:T(8,128)}) fusion(f32[40,8,32,128]{3,0,2,1:T(8,128)} %fusion.28, f32[40,8,32,128]{3,0,2,1:T(8,128)} %fusion.30, f32[40,8,32,128]{3,0,2,1:T(8,128)} %fusion.32, f32[40,8,32,128]{3,0,2,1:T(8,128)S(1)} %fusion.34, f32[40,8,32,128]{3,0,2,1:T(8,128)S(1)} %fusion.36, ...), kind=kOutput, calls=%fused_computation.156 | convolution fusion | flops 511180800 | bytes 38277120 | tf_op jit(solution)/shard_map/mliq,is->mlsq/dot_general | solution.py:63
  194.7 7.7 %collective-permute-start.2 = (bf16[8,32,4,128]{3,2,1,0:T(4,128)(2,1)S(1)}, bf16[8,32,4,128]{3,2,1,0:T(4,128)(2,1)S(1)}, u32[]{:S(2)}, u32[]{:S(2)}) collective-permute-start(bf16[8,32,4,128]{3,2,1,0:T(4,128)(2,1)S(1)} %get-tuple-element.76), channel_id=1, source_target_pairs={{0,8},{8,16},{16,24},{24,32},{32,40},{40,48},{48,56},{56,64},{64,7... | collective-permute-start | bytes 786440 | tf_op jit(solution)/shard_map/ppermute | solution.py:25
  203.4 5.2 slice.238
  208.6 2.2 fusion.93
  210.8 2.2 fusion.92
  213.0 4.9 reshape.174
  217.9 8.6 %convert_bitcast_fusion = (bf16[8,4,32,8,128]{4,3,2,1,0:T(8,128)(2,1)S(1)}, f32[8,32,4096]{2,1,0:T(8,128)}, f32[8,32,4096]{2,1,0:T(8,128)}) fusion(f32[8,32,4096]{2,1,0:T(8,128)} %param.19, f32[8,32,4096]{2,1,0:T(8,128)} %reshape.174), kind=kLoop, calls=%fused_computation.73 | loop fusion | flops 3145728 | bytes 18874368
  229.8 2.2 collective-permute-done.4
  232.0 2.8 collective-permute-done.5
  235.1 8.4 %gather_fusion.1 = bf16[192,8,32,128]{3,2,1,0:T(8,128)(2,1)} fusion(bf16[8,32,40,128]{3,1,2,0:T(8,128)(2,1)S(1)} %pad_maximum_fusion.1, s32[1024]{0:T(1024)S(1)} %pad_clamp_fusion), kind=kCustom, calls=%fused_computation.1.clone | custom fusion | bytes 25166592 | tf_op jit(solution)/shard_map/jit(_take)/gather | solution.py:47
  243.6 11.8 %fusion.49 = f32[32,8,4,8,128]{4,3,2,1,0:T(8,128)} fusion(bf16[32,6,128,128]{3,2,1,0:T(8,128)(2,1)} %param.25, bf16[32,6,8,32,128]{4,3,2,1,0:T(8,128)(2,1)} %bitcast.236, pred[32,6]{1,0:T(8,128)(4,1)S(1)} %copy.54), kind=kOutput, calls=%fused_computation.70 | convolution fusion | flops 1616904192 | bytes 23068864 | tf_op jit(solution)/shard_map/ijpq,mlijq->mlip/dot_general | solution.py:48
  255.3 2.8 copy.201
  260.8 82.8 %all-reduce.6.cloned.1.call-done = f32[2,32,4096]{2,1,0:T(8,128)} async-done(((f32[2,32,4096]{2,1,0:T(8,128)}), f32[2,32,4096]{2,1,0:T(8,128)}) %all-reduce.6.cloned.1.call-update) | async-done | bytes 1048592 | tf_op jit(solution)/shard_map/psum | solution.py:87
  343.6 2.3 bitcast_convert_fusion
  350.1 3.3 convolution_bitcast_fusion.3
  356.2 1.8 convolution_bitcast_fusion
  358.0 3.3 convolution_bitcast_fusion.5
  361.3 5.2 fusion.24
  366.5 5.2 fusion.22
  371.8 6.4 %fusion.20 = f32[40,8,32,128]{3,0,2,1:T(8,128)} fusion(f32[8,32,32,128]{3,0,1,2:T(8,128)S(1)} %convolution_bitcast_fusion.2, pred[32,6,40]{2,0,1:T(32,128)(4,1)S(1)} %iota_compare_fusion), kind=kOutput, calls=%fused_computation.30 | convolution fusion | flops 503316480 | bytes 9441280 | tf_op jit(solution)/shard_map/mliq,is->mlsq/dot_general | solution.py:63
  378.2 6.2 %fusion.18 = f32[40,8,32,128]{3,0,2,1:T(8,128)} fusion(f32[8,32,32,128]{3,0,1,2:T(8,128)S(1)} %convolution_bitcast_fusion.1, pred[32,6,40]{2,0,1:T(32,128)(4,1)S(1)} %iota_compare_fusion), kind=kOutput, calls=%fused_computation.28 | convolution fusion | flops 503316480 | bytes 9441280 | tf_op jit(solution)/shard_map/mliq,is->mlsq/dot_general | solution.py:63
  384.3 6.1 %fusion.16 = f32[40,8,32,128]{3,0,2,1:T(8,128)} fusion(f32[8,32,32,128]{3,0,1,2:T(8,128)S(1)} %convolution_bitcast_fusion, pred[32,6,40]{2,0,1:T(32,128)(4,1)S(1)} %iota_compare_fusion), kind=kOutput, calls=%fused_computation.26 | convolution fusion | flops 503316480 | bytes 9441280 | tf_op jit(solution)/shard_map/mliq,is->mlsq/dot_general | solution.py:63
  390.5 15.9 %fusion.103 = (bf16[8,32,40,128]{3,2,1,0:T(8,128)(2,1)S(1)}, f32[8,32,40,128]{3,2,1,0:T(8,128)}) fusion(f32[40,8,32,128]{3,0,2,1:T(8,128)} %fusion.16, f32[40,8,32,128]{3,0,2,1:T(8,128)} %fusion.18, f32[40,8,32,128]{3,0,2,1:T(8,128)} %fusion.20, f32[40,8,32,128]{3,0,2,1:T(8,128)S(1)} %fusion.22, f32[40,8,32,128]{3,0,2,1:T(8,128)S(1)} %fusion.24, ...), kind=kOutput, calls=%fused_computation.157 | convolution fusion | flops 511180800 | bytes 38277120 | tf_op jit(solution)/shard_map/mliq,is->mlsq/dot_general | solution.py:63
  406.6 7.7 %collective-permute-start.6 = (bf16[8,32,4,128]{3,2,1,0:T(4,128)(2,1)S(1)}, bf16[8,32,4,128]{3,2,1,0:T(4,128)(2,1)S(1)}, u32[]{:S(2)}, u32[]{:S(2)}) collective-permute-start(bf16[8,32,4,128]{3,2,1,0:T(4,128)(2,1)S(1)} %get-tuple-element.74), channel_id=1, source_target_pairs={{0,8},{8,16},{16,24},{24,32},{32,40},{40,48},{48,56},{56,64},{64,7... | collective-permute-start | bytes 786440 | tf_op jit(solution)/shard_map/ppermute | solution.py:25
  415.3 5.1 slice.245
  421.1 2.2 fusion.91
  423.3 2.2 fusion.90
  425.6 5.0 reshape.177
  430.5 6.6 %multiply_reduce_fusion = (f32[]{:T(128)}, f32[]{:T(128)}) fusion(f32[8,32,4096]{2,1,0:T(8,128)} %get-tuple-element.66, f32[8,32,4096]{2,1,0:T(8,128)} %get-tuple-element.65, f32[8,32,4096]{2,1,0:T(8,128)} %reshape.177), kind=kLoop, calls=%fused_computation.52 | loop fusion | flops 6291454 | bytes 12582920 | tf_op jit(solution)/shard_map/reduce_sum | solution.py:105
  439.6 64.6 %all-reduce = (f32[]{:T(128)}, f32[]{:T(128)}) all-reduce(f32[]{:T(128)S(6)} %add.143, f32[]{:T(128)S(6)} %add.155), channel_id=1, replica_groups=mesh['tile'=16,'mem'=8] {'tile','mem'}, use_global_device_ids=true, to_apply=%region_5.7 | all-reduce | flops 2 | bytes 16 | tf_op jit(solution)/shard_map/psum | solution.py:101
  505.5 11.8 %multiply_subtract_fusion = (f32[8,32,4096]{2,1,0:T(8,128)}, f32[8,32,4096]{2,1,0:T(8,128)}) fusion(f32[8,32,4096]{2,1,0:T(8,128)} %get-tuple-element.66, f32[8,32,4096]{2,1,0:T(8,128)} %get-tuple-element.65, f32[8,32,4096]{2,1,0:T(8,128)} %reshape.177, f32[]{:T(128)S(6)} %div.3, f32[8,32,4096]{2,1,0:T(8,128)} %param.19), kind=kLoop, calls=%fused_computation.50 | loop fusion | flops 6291456 | bytes 25165828 | tf_op jit(solution)/shard_map/sub | solution.py:111
  (91 shorter events, 29.9 us)
Async XLA Ops:
  7.2 7.2 %copy-start.15 = (s32[32,6]{0,1:T(8,128)S(1)}, s32[32,6]{0,1:T(8,128)}, u32[]{:S(2)}) copy-start(s32[32,6]{0,1:T(8,128)} %param.24) | copy-start | bytes 2308
  7.2 7.5 %copy-start.13 = (f32[4,4096]{1,0:T(4,128)S(1)}, f32[4,4096]{1,0:T(4,128)}, u32[]{:S(2)}) copy-start(f32[4,4096]{1,0:T(4,128)} %param.21) | copy-start | bytes 196612
  7.2 7.5 %copy-start.14 = (f32[4,4096]{1,0:T(4,128)S(1)}, f32[4,4096]{1,0:T(4,128)}, u32[]{:S(2)}) copy-start(f32[4,4096]{1,0:T(4,128)} %param.20) | copy-start | bytes 196612
  7.2 124.5 %all-reduce.4.cloned.1.call-start = ((), (), s32[]{:S(2)}) async-start(), calls=%async_computation | async-start | bytes 2097152 | tf_op jit(solution)/shard_map/psum | solution.py:87
  9.9 1.3 copy-start.6
  11.2 6.4 %collective-permute-start = (bf16[8,32,4,128]{3,1,2,0:T(8,128)(2,1)S(1)}, bf16[8,32,4,128]{3,1,2,0:T(8,128)(2,1)S(1)}, u32[]{:S(2)}, u32[]{:S(2)}) collective-permute-start(bf16[8,32,4,128]{3,1,2,0:T(8,128)(2,1)S(1)} %get-tuple-element.79), channel_id=1, source_target_pairs={{0,8},{8,16},{16,24},{24,32},{32,40},{40,48},{48,56},{56,64},{64,7... | collective-permute-start | bytes 786440 | tf_op jit(solution)/shard_map/ppermute | solution.py:15
  14.3 6.1 %collective-permute-start.1 = (bf16[8,32,4,128]{3,1,2,0:T(8,128)(2,1)S(1)}, bf16[8,32,4,128]{3,1,2,0:T(8,128)(2,1)S(1)}, u32[]{:S(2)}, u32[]{:S(2)}) collective-permute-start(bf16[8,32,4,128]{3,1,2,0:T(8,128)(2,1)S(1)} %get-tuple-element.80), channel_id=1, source_target_pairs={{8,0},{16,8},{24,16},{32,24},{40,32},{48,40},{56,48},{64,56},{72,6... | collective-permute-start | bytes 786440 | tf_op jit(solution)/shard_map/ppermute | solution.py:18
  42.4 3.4 copy-start
  45.9 85.8 %copy-start.9 = (f32[2,32,4096]{2,1,0:T(8,128)S(1)}, f32[2,32,4096]{2,1,0:T(8,128)}, u32[]{:S(2)}) copy-start(f32[2,32,4096]{2,1,0:T(8,128)} %param.23) | copy-start | bytes 3145732
  45.9 85.8 %copy-start.11 = (f32[2,32,4096]{2,1,0:T(8,128)S(1)}, f32[2,32,4096]{2,1,0:T(8,128)}, u32[]{:S(2)}) copy-start(f32[2,32,4096]{2,1,0:T(8,128)} %param.22) | copy-start | bytes 3145732
  46.9 1.0 copy-start.7
  47.9 295.7 %all-reduce.6.cloned.1.call-start = ((), (), s32[]{:S(2)}) async-start(), calls=%async_computation.1 | async-start | bytes 2097152 | tf_op jit(solution)/shard_map/psum | solution.py:87
  131.7 2.6 copy-start.1
  134.1 2.2 slice-start
  134.2 2.6 slice-start.1
  149.0 5.6 %copy-start.4 = (f32[8,32,32,128]{3,0,1,2:T(8,128)S(1)}, f32[8,32,32,128]{3,0,1,2:T(8,128)}, u32[]{:S(2)}) copy-start(f32[8,32,32,128]{3,0,1,2:T(8,128)} %convolution_bitcast_fusion.9) | copy-start | bytes 12582916
  194.7 13.9 %collective-permute-start.2 = (bf16[8,32,4,128]{3,2,1,0:T(4,128)(2,1)S(1)}, bf16[8,32,4,128]{3,2,1,0:T(4,128)(2,1)S(1)}, u32[]{:S(2)}, u32[]{:S(2)}) collective-permute-start(bf16[8,32,4,128]{3,2,1,0:T(4,128)(2,1)S(1)} %get-tuple-element.76), channel_id=1, source_target_pairs={{0,8},{8,16},{16,24},{24,32},{32,40},{40,48},{48,56},{56,64},{64,7... | collective-permute-start | bytes 786440 | tf_op jit(solution)/shard_map/ppermute | solution.py:25
  203.3 7.5 %collective-permute-start.3 = (bf16[8,32,4,128]{3,2,1,0:T(4,128)(2,1)S(1)}, bf16[8,32,4,128]{3,2,1,0:T(4,128)(2,1)S(1)}, u32[]{:S(2)}, u32[]{:S(2)}) collective-permute-start(bf16[8,32,4,128]{3,2,1,0:T(4,128)(2,1)S(1)} %get-tuple-element.75), channel_id=1, source_target_pairs={{0,120},{8,0},{16,8},{24,16},{32,24},{40,32},{48,40},{56,48},{64,5... | collective-permute-start | bytes 786440 | tf_op jit(solution)/shard_map/ppermute | solution.py:25
  226.9 5.1 collective-permute-start.4
  228.7 6.1 %collective-permute-start.5 = (bf16[8,32,4,128]{3,1,2,0:T(8,128)(2,1)S(1)}, bf16[8,32,4,128]{3,1,2,0:T(8,128)(2,1)S(1)}, u32[]{:S(2)}, u32[]{:S(2)}) collective-permute-start(bf16[8,32,4,128]{3,1,2,0:T(8,128)(2,1)S(1)} %get-tuple-element.78), channel_id=1, source_target_pairs={{8,0},{16,8},{24,16},{32,24},{40,32},{48,40},{56,48},{64,56},{72,6... | collective-permute-start | bytes 786440 | tf_op jit(solution)/shard_map/ppermute | solution.py:18
  255.3 3.4 copy-start.2
  258.8 84.8 %copy-start.10 = (f32[2,32,4096]{2,1,0:T(8,128)S(1)}, f32[2,32,4096]{2,1,0:T(8,128)}, u32[]{:S(2)}) copy-start(f32[2,32,4096]{2,1,0:T(8,128)} %param.23) | copy-start | bytes 3145732
  258.8 84.8 %copy-start.12 = (f32[2,32,4096]{2,1,0:T(8,128)S(1)}, f32[2,32,4096]{2,1,0:T(8,128)}, u32[]{:S(2)}) copy-start(f32[2,32,4096]{2,1,0:T(8,128)} %param.22) | copy-start | bytes 3145732
  259.8 1.0 copy-start.8
  343.6 2.6 copy-start.3
  346.0 2.2 slice-start.2
  346.2 2.6 slice-start.3
  361.3 5.2 copy-start.5
  406.6 14.5 %collective-permute-start.6 = (bf16[8,32,4,128]{3,2,1,0:T(4,128)(2,1)S(1)}, bf16[8,32,4,128]{3,2,1,0:T(4,128)(2,1)S(1)}, u32[]{:S(2)}, u32[]{:S(2)}) collective-permute-start(bf16[8,32,4,128]{3,2,1,0:T(4,128)(2,1)S(1)} %get-tuple-element.74), channel_id=1, source_target_pairs={{0,8},{8,16},{16,24},{24,32},{32,40},{40,48},{48,56},{56,64},{64,7... | collective-permute-start | bytes 786440 | tf_op jit(solution)/shard_map/ppermute | solution.py:25
  415.2 8.1 %collective-permute-start.7 = (bf16[8,32,4,128]{3,2,1,0:T(4,128)(2,1)S(1)}, bf16[8,32,4,128]{3,2,1,0:T(4,128)(2,1)S(1)}, u32[]{:S(2)}, u32[]{:S(2)}) collective-permute-start(bf16[8,32,4,128]{3,2,1,0:T(4,128)(2,1)S(1)} %get-tuple-element.73), channel_id=1, source_target_pairs={{0,120},{8,0},{16,8},{24,16},{32,24},{40,32},{48,40},{56,48},{64,5... | collective-permute-start | bytes 786440 | tf_op jit(solution)/shard_map/ppermute | solution.py:25
Sparse Core Ops, SparseCore 0:
  48.0 83.6 all-reduce.3
  260.9 82.6 all-reduce.5
where the time goes:
time: 531 us; the launch traced here: 525 us
  waiting for transfers between devices  177 us (33%)
  matrix products  139 us (26%)
  blocking collectives  64.6 us (12%)
  local copies, waits for them, and re-layouts  53.9 us (10%)
  other arithmetic  50.8 us (10%)
  starting transfers between devices  21.6 us (4%)
  between operations  18.5 us (3%)
    psum x2, waiting for transfers between devices, evaluate(): combined = lax.psum(ensemble_part + placed, 'mem')  166 us
    dot_general x12, matrix products, adjoint(): jnp.einsum('mliq,is->mlsq', part_term, onehot[:, column_slot], precision=...  90.4 us
    psum x1, blocking collectives, body(): grad_norm = lax.psum(local_norm, ('tile', 'mem'))  64.6 us
    dot_general x12, matrix products, adjoint(): jnp.einsum('ipq,mlip->mliq', taper_coef[:, column_slot], blocks, preferre...  24.7 us
    dot_general x2, matrix products, localize(): jnp.einsum('ijpq,mlijq->mlip', taper_coef, picked, preferred_element_type...  23.6 us
    gather x2, local copies, waits for them, and re-layouts, localize(): picked = jnp.take(padded, local_cols, axis=2)  16.7 us
    ppermute x4, starting transfers between devices, passed_along(): lax.ppermute(array, axis, [(i, (i + by) % size) for i in range(size)])  15.5 us
    unnamed x5, other arithmetic  13.3 us
  transfers between devices with their start and end apart: 10, of which 6 were waited for; matrix products, arithmetic and copies ran while one was open for 3% of the time, Pallas kernels for 0%

commit v1 on v0

v1 whole, which is shorter than its diff:
```python
import functools
import jax
import jax.numpy as jnp
from jax import lax
from jax.experimental import pallas as pl
from jax.experimental.pallas import tpu as pltpu
from jax.sharding import PartitionSpec as P

W = 4
B = 128
F32 = jnp.float32
BF16 = jnp.bfloat16


def shifted(array, axis, by):
    size = lax.axis_size(axis)
    return lax.ppermute(array, axis, [(i, (i + by) % size) for i in range(size)])


def masked(full, me, share):
    level = lax.broadcasted_iota(jnp.int32, full.shape, 0)
    mine = jnp.logical_and(level >= me * share, level < (me + 1) * share)
    return jnp.where(mine, full, 0.0)


def spread(own, me, levels):
    share = own.shape[0]
    return masked(jnp.concatenate([own] * (levels // share), axis=0), me, share)


def gathered(full, share):
    parts = [full[g * share : (g + 1) * share] for g in range(full.shape[0] // share)]
    return functools.reduce(jnp.add, parts)


def localize_rows(cols, xs, coef_ref, anom_ref, base, out_store, static):
    rows, slots = coef_ref.shape[:2]
    members, slot_count, levels = anom_ref.shape[:3]
    for r in range(rows):
        lhs = jnp.concatenate([xs[cols[base + r, s]] for s in range(slots)], axis=1)
        rhs = jnp.concatenate([coef_ref[r, s] for s in range(slots)], axis=1)
        loc = lax.dot_general(
            lhs, rhs, (((1,), (1,)), ((), ())), preferred_element_type=F32
        ).reshape(members, levels, B)
        for t in range(slot_count):
            a = anom_ref[:, t, :, r * B : (r + 1) * B].astype(F32)
            inc = jnp.sum(a * loc, axis=0) + static[:, r * B : (r + 1) * B]
            out_store(t, r, inc)


def forward_first(scal, cols, alpha_ref, low_ref, high_ref, coef_ref, anom_ref, chi_ref, sig_ref, out_ref, xs):
    d = pl.program_id(0)
    members, levels, columns = alpha_ref.shape
    n = columns // B

    @pl.when(d == 0)
    def _():
        for b in range(W):
            xs[b] = low_ref[:, :, b * B : (b + 1) * B].reshape(members * levels, B)
            xs[W + n + b] = high_ref[:, :, b * B : (b + 1) * B].reshape(members * levels, B)
        for b in range(n):
            xs[W + b] = alpha_ref[:, :, b * B : (b + 1) * B].astype(BF16).reshape(members * levels, B)

    static = spread(sig_ref[...] * chi_ref[...], scal[0], levels)

    def store(t, r, inc):
        out_ref[0, t, :, r * B : (r + 1) * B] = inc.astype(BF16)

    localize_rows(cols, xs, coef_ref, anom_ref, d * coef_ref.shape[0], store, static)


def forward_second(
    scal, cols, alpha_ref, acc_ref, prev_ref, next_ref, coef_ref, anom_ref, chi_ref, sig_ref, res_ref,
    out_ref, norm_ref, xs, tot,
):
    d = pl.program_id(0)
    rows = coef_ref.shape[0]
    members, _, levels = anom_ref.shape[:3]
    n = acc_ref.shape[0] - 2 * W

    @pl.when(d == 0)
    def _():
        for b in range(n + 2 * W):
            v = acc_ref[b]
            if b < 2 * W:
                v = v + prev_ref[b].astype(F32)
            if b >= n:
                v = v + next_ref[b - n].astype(F32)
            xs[b] = (-v).astype(BF16)
        tot[...] = jnp.zeros_like(tot)

    rsum = res_ref[0, 0].astype(F32) + res_ref[0, 1].astype(F32)
    sig = spread(sig_ref[...], scal[0], levels)
    chi = spread(chi_ref[...], scal[0], levels)
    sr = sig * rsum
    static = -(sig * sr)
    gc = chi + sr
    sq = jnp.zeros((levels, B), F32)
    for r in range(rows):
        sq = sq + gc[:, r * B : (r + 1) * B] * gc[:, r * B : (r + 1) * B]
    tot[...] += sq

    def own_square(r, extra):
        adj = acc_ref[W + d * rows + r]
        if extra is not None:
            adj = adj + extra.astype(F32)
        g = alpha_ref[:, :, r * B : (r + 1) * B] + adj.reshape(members, levels, B)
        tot[...] += jnp.sum(g * g, axis=0)

    last = pl.num_programs(0) - 1
    edge = W // rows

    @pl.when(d == 0)
    def _():
        for r in range(rows):
            own_square(r, prev_ref[W + r])

    @pl.when(d == last)
    def _():
        for r in range(rows):
            own_square(r, next_ref[r])

    @pl.when(jnp.logical_and(d > 0, d < last))
    def _():
        for r in range(rows):
            own_square(r, None)

    def store(t, r, inc):
        out_ref[0, t, :, r * B : (r + 1) * B] = inc.astype(BF16)

    localize_rows(cols, xs, coef_ref, anom_ref, d * rows, store, static)

    @pl.when(d == last)
    def _():
        norm_ref[...] = tot[...]


def residual_first(scal, y_ref, rinv_ref, innov_ref, out_ref, inc_ref):
    y = jnp.sum(y_ref[...].astype(F32), axis=0)
    inc_ref[...] = y
    r = (rinv_ref[...] * (y - innov_ref[...])).astype(BF16)
    for k in range(out_ref.shape[0]):
        out_ref[k] = r


def residual_second(scal, y_ref, rinv_ref, innov_ref, inc_ref, old_ref, norm_ref, out_ref, sum_ref):
    y = jnp.sum(y_ref[...].astype(F32), axis=0)
    r = (rinv_ref[...] * (y - innov_ref[...])).astype(BF16)
    for k in range(out_ref.shape[0]):
        out_ref[k] = r
    change = (old_ref[0].astype(F32) - r.astype(F32)) * (inc_ref[...] - y)
    change = jnp.sum(change.reshape(-1, 8, change.shape[-1]), axis=0)
    norm = norm_ref[...].reshape(-1, 8, B).sum(axis=0)
    total_n = jnp.sum(norm)
    total_p = jnp.sum(change)
    lane = lax.broadcasted_iota(jnp.int32, sum_ref.shape, 1)
    sum_ref[...] = jnp.where(lane == 0, total_n, jnp.where(lane == 1, total_p, 0.0))


def adjoint_kernel(cols, res_ref, anom_ref, coef_ref, acc_ref, low_ref, high_ref):
    d = pl.program_id(0)
    rows, slots = coef_ref.shape[:2]
    members, slot_count, levels = anom_ref.shape[:3]
    n = acc_ref.shape[0] - 2 * W

    @pl.when(d == 0)
    def _():
        for b in range(n + 2 * W):
            acc_ref[b] = jnp.zeros(acc_ref.shape[1:], F32)

    for r in range(rows):
        sl = slice(r * B, (r + 1) * B)
        w = functools.reduce(
            jnp.add,
            [
                anom_ref[:, t, :, sl].astype(F32) * res_ref[0, t, :, sl].astype(F32)[None]
                for t in range(slot_count)
            ],
        )
        w = w.astype(BF16).reshape(members * levels, B)
        rhs = jnp.concatenate([coef_ref[r, s] for s in range(slots)], axis=1)
        part = jnp.dot(w, rhs, preferred_element_type=F32)
        for s in range(slots):
            c = cols[d * rows + r, s]
            acc_ref[c] += part[:, s * B : (s + 1) * B]

    @pl.when(d == pl.num_programs(0) - 1)
    def _():
        for b in range(low_ref.shape[0]):
            low_ref[b] = acc_ref[b].astype(BF16)
            high_ref[b] = acc_ref[n + 2 * W - high_ref.shape[0] + b].astype(BF16)


def final_kernel(
    scal, sums_ref, alpha_ref, acc1_ref, acc2_ref, prev1_ref, next1_ref, prev2_ref, next2_ref,
    chi_ref, sig_ref, res1_ref, res2_ref, an_ref, cn_ref, ga_ref, gc_ref,
):
    d = pl.program_id(0)
    rows = acc1_ref.shape[0]
    members, levels = alpha_ref.shape[:2]
    share = chi_ref.shape[0]
    totals = jnp.sum(sums_ref[...], axis=0, keepdims=True)
    lane = lax.broadcasted_iota(jnp.int32, totals.shape, 1)
    norm = jnp.sum(jnp.where(lane == 0, totals, 0.0), axis=1, keepdims=True)
    prod = norm + jnp.sum(jnp.where(lane == 1, totals, 0.0), axis=1, keepdims=True)
    step = norm / prod

    def rows_out(extra1, extra2):
        for r in range(rows):
            sl = slice(r * B, (r + 1) * B)
            a1 = acc1_ref[r]
            a2 = acc2_ref[r]
            if extra1 is not None:
                a1 = a1 + extra1(r).astype(F32)
                a2 = a2 + extra2(r).astype(F32)
            a1 = a1.reshape(members, levels, B)
            a2 = a2.reshape(members, levels, B)
            a0 = alpha_ref[:, :, sl]
            g = a0 + a1
            q = g + (a1 - a2)
            an_ref[:, :, sl] = a0 - step[None] * g
            ga_ref[:, :, sl] = g - step[None] * q

    last = pl.num_programs(0) - 1

    @pl.when(d == 0)
    def _():
        rows_out(lambda r: prev1_ref[W + r], lambda r: prev2_ref[r])

    @pl.when(d == last)
    def _():
        rows_out(lambda r: next1_ref[r], lambda r: next2_ref[r])

    @pl.when(jnp.logical_and(d > 0, d < last))
    def _():
        rows_out(None, None)

    s1 = res1_ref[0, 0].astype(F32) + res1_ref[0, 1].astype(F32)
    s2 = res2_ref[0, 0].astype(F32) + res2_ref[0, 1].astype(F32)
    s1 = gathered(masked(s1, scal[0], share), share)
    s2 = gathered(masked(s2, scal[0], share), share)
    chi = chi_ref[...]
    sg = sig_ref[...]
    g = chi + sg * s1
    q = g + (sg * s1 - sg * s2)
    cn_ref[...] = chi - step * g
    gc_ref[...] = g - step * q


def body(anomalies, alpha0, chi0, sigma, innov, rinv, taper_cols, taper_coef):
    members, levels, columns = alpha0.shape
    slot_count = anomalies.shape[1]
    nblocks, slots = taper_cols.shape
    share = chi0.shape[0]
    groups = lax.axis_size("mem")
    tiles = lax.axis_size("tile")
    me = lax.axis_index("mem")
    scal = me.astype(jnp.int32).reshape(1)
    rows = nblocks // groups
    width = rows * B
    ml = members * levels
    padded = nblocks + 2 * W
    cols = (taper_cols - lax.axis_index("tile") * nblocks + W) % (nblocks * tiles)

    whole = pl.BlockSpec(memory_space=pltpu.VMEM)
    coef_spec = pl.BlockSpec((rows, slots, B, B), lambda d, *_: (d, 0, 0, 0))
    anom_spec = pl.BlockSpec((members, slot_count, levels, width), lambda d, *_: (0, 0, 0, d))
    chi_spec = pl.BlockSpec((share, width), lambda d, *_: (0, d))
    alpha_spec = pl.BlockSpec((members, levels, width), lambda d, *_: (0, 0, d))
    piece_spec = pl.BlockSpec((1, slot_count, levels, width), lambda d, *_: (d, 0, 0, 0))
    pieces = jax.ShapeDtypeStruct((groups, slot_count, levels, width), BF16)
    own_spec = pl.BlockSpec((slot_count, levels, width), lambda d, s: (0, 0, s[0]))
    params = pltpu.CompilerParams(dimension_semantics=("arbitrary",), vmem_limit_bytes=60 * 2**20)

    low = shifted(alpha0[:, :, columns - W * B :].astype(BF16), "tile", 1)
    high = shifted(alpha0[:, :, : W * B].astype(BF16), "tile", -1)

    part1 = pl.pallas_call(
        forward_first,
        grid_spec=pltpu.PrefetchScalarGridSpec(
            num_scalar_prefetch=2,
            grid=(groups,),
            in_specs=[whole, whole, whole, coef_spec, anom_spec, chi_spec, chi_spec],
            out_specs=piece_spec,
            scratch_shapes=[pltpu.VMEM((padded, ml, B), BF16)],
        ),
        out_shape=pieces,
        compiler_params=params,
        name="forward_first",
    )(scal, cols, alpha0, low, high, taper_coef, anomalies, chi0, sigma)

    got1 = lax.all_to_all(part1, "mem", 0, 0)
    r1b, inc1 = pl.pallas_call(
        residual_first,
        grid_spec=pltpu.PrefetchScalarGridSpec(
            num_scalar_prefetch=1,
            grid=(1,),
            in_specs=[whole, own_spec, own_spec],
            out_specs=[whole, whole],
        ),
        out_shape=[pieces, jax.ShapeDtypeStruct((slot_count, levels, width), F32)],
        compiler_params=params,
        name="residual_first",
    )(scal, got1, rinv, innov)
    res1 = lax.all_to_all(r1b, "mem", 0, 0)

    def adjoint(res, halo, low_from):
        return pl.pallas_call(
            adjoint_kernel,
            grid_spec=pltpu.PrefetchScalarGridSpec(
                num_scalar_prefetch=1,
                grid=(groups,),
                in_specs=[piece_spec, anom_spec, coef_spec],
                out_specs=[whole, whole, whole],
            ),
            out_shape=[
                jax.ShapeDtypeStruct((padded, ml, B), F32),
                jax.ShapeDtypeStruct((halo, ml, B), BF16),
                jax.ShapeDtypeStruct((halo, ml, B), BF16),
            ],
            compiler_params=params,
            name="adjoint",
        )(cols, res, anomalies, taper_coef)

    acc1, low1, high1 = adjoint(res1, 2 * W, 0)
    prev1 = shifted(high1, "tile", 1)
    next1 = shifted(low1, "tile", -1)

    part2, norm = pl.pallas_call(
        forward_second,
        grid_spec=pltpu.PrefetchScalarGridSpec(
            num_scalar_prefetch=2,
            grid=(groups,),
            in_specs=[
                alpha_spec, whole, whole, whole, coef_spec, anom_spec, chi_spec, chi_spec, piece_spec,
            ],
            out_specs=[piece_spec, whole],
            scratch_shapes=[pltpu.VMEM((padded, ml, B), BF16), pltpu.VMEM((levels, B), F32)],
        ),
        out_shape=[pieces, jax.ShapeDtypeStruct((levels, B), F32)],
        compiler_params=params,
        name="forward_second",
    )(scal, cols, alpha0, acc1, prev1, next1, taper_coef, anomalies, chi0, sigma, res1)

    got2 = lax.all_to_all(part2, "mem", 0, 0)
    r2b, sums = pl.pallas_call(
        residual_second,
        grid_spec=pltpu.PrefetchScalarGridSpec(
            num_scalar_prefetch=1,
            grid=(1,),
            in_specs=[whole, own_spec, own_spec, whole, pl.BlockSpec((1, slot_count, levels, width), lambda d, s: (0, 0, 0, 0)), whole],
            out_specs=[whole, whole],
        ),
        out_shape=[pieces, jax.ShapeDtypeStruct((groups * tiles, B), F32)],
        compiler_params=params,
        name="residual_second",
    )(scal, got2, rinv, innov, inc1, r1b, norm)
    res2 = lax.all_to_all(r2b, "mem", 0, 0)
    sums = lax.all_to_all(sums, ("tile", "mem"), 0, 0, tiled=True)

    acc2, low2, high2 = adjoint(res2, W, 0)
    prev2 = shifted(high2, "tile", 1)
    next2 = shifted(low2, "tile", -1)

    acc_spec = pl.BlockSpec((rows, ml, B), lambda d, *_: (d + W // rows, 0, 0))
    out = pl.pallas_call(
        final_kernel,
        grid_spec=pltpu.PrefetchScalarGridSpec(
            num_scalar_prefetch=1,
            grid=(groups,),
            in_specs=[
                whole, alpha_spec, acc_spec, acc_spec, whole, whole, whole, whole,
                chi_spec, chi_spec, piece_spec, piece_spec,
            ],
            out_specs=[alpha_spec, chi_spec, alpha_spec, chi_spec],
        ),
        out_shape=[
            jax.ShapeDtypeStruct(alpha0.shape, F32),
            jax.ShapeDtypeStruct(chi0.shape, F32),
            jax.ShapeDtypeStruct(alpha0.shape, F32),
            jax.ShapeDtypeStruct(chi0.shape, F32),
        ],
        compiler_params=params,
        name="final",
    )(scal, sums, alpha0, acc1, acc2, prev1, next1, prev2, next2, chi0, sigma, res1, res2)
    return tuple(out)


def solution(mesh):
    placed = (
        P("mem", None, None, "tile"),
        P("mem", None, "tile"),
        P("mem", "tile"),
        P("mem", "tile"),
        P(None, None, "tile"),
        P(None, None, "tile"),
        P("tile", None),
        P("tile", None, None, None),
    )
    return jax.shard_map(
        body,
        mesh=mesh,
        in_specs=placed,
        out_specs=(
            P("mem", None, "tile"),
            P("mem", "tile"),
            P("mem", None, "tile"),
            P("mem", "tile"),
        ),
        check_vma=False,
    )
```

time: 531 us -> 176 us (0.33)
  waiting for transfers between devices: 177 us -> 11.1 us
  matrix products: 139 us -> 0 us
  Pallas kernels: 0 us -> 67.7 us
  local copies, waits for them, and re-layouts: 53.9 us -> 2.56 us
  other arithmetic: 50.8 us -> 3.09 us
  between operations: 18.5 us -> 0.69 us
  blocking collectives: 64.6 us -> 71 us
    psum x2 -> x0, waiting for transfers between devices: 166 us -> none  [evaluate(): combined = lax.psum(ensemble_part + placed, 'mem')]
    dot_general x26 -> x0, matrix products: 139 us -> none  [the longest x12 90.4 us: adjoint(): jnp.einsum('mliq,is->mlsq', part_term, onehot[:, column_slot], precision=...]
    all_to_all x0 -> x5, blocking collectives: none -> 71 us  [the longest x1 15.8 us: body(): got1 = lax.all_to_all(part1, 'mem', 0, 0)]
    pallas_call x0 -> x7, Pallas kernels: none -> 67.7 us  [the longest x2 25.8 us: adjoint(): pl.pallas_call(adjoint_kernel, grid_spec=pltpu.PrefetchScalarGridSpec(num...]
    psum x1 -> x0, blocking collectives: 64.6 us -> none  [body(): grad_norm = lax.psum(local_norm, ('tile', 'mem'))]
    gather x2 -> x0, local copies, waits for them, and re-layouts: 16.7 us -> none  [localize(): picked = jnp.take(padded, local_cols, axis=2)]
    unnamed x5 -> x0, other arithmetic: 13.3 us -> none
    sub x2 -> x0, other arithmetic: 12.5 us -> none  [the longest x1 11.8 us: body(): g_alpha - step_length * change_alpha]
  transfers between devices with their start and end apart: 10 -> 6, of which waited for: 6 -> 3; matrix products, arithmetic and copies ran while one was open for 3% -> 0% of each run, Pallas kernels for 0% -> 0%
where the time goes in v1:
time: 176 us; the launch traced here: 175 us
  blocking collectives  71 us (40%)
  Pallas kernels  67.7 us (38%)
  starting transfers between devices  18.8 us (11%)
  waiting for transfers between devices  11.1 us (6%)
  other arithmetic  3.09 us (2%)
  local copies, waits for them, and re-layouts  2.56 us (1%)
    pallas_call x2, Pallas kernels, adjoint(): pl.pallas_call(adjoint_kernel, grid_spec=pltpu.PrefetchScalarGridSpec(num...  25.8 us
    ppermute x6, starting transfers between devices, shifted(): lax.ppermute(array, axis, [(i, (i + by) % size) for i in range(size)])  18.8 us
    all_to_all x1, blocking collectives, body(): got1 = lax.all_to_all(part1, 'mem', 0, 0)  15.8 us
    all_to_all x1, blocking collectives, body(): sums = lax.all_to_all(sums, ('tile', 'mem'), 0, 0, tiled=True)  15.7 us
    pallas_call x1, Pallas kernels, body(): pl.pallas_call(forward_second, grid_spec=pltpu.PrefetchScalarGridSpec(num...  14.1 us
    all_to_all x1, blocking collectives, body(): got2 = lax.all_to_all(part2, 'mem', 0, 0)  13.2 us
    all_to_all x1, blocking collectives, body(): res2 = lax.all_to_all(r2b, 'mem', 0, 0)  13.2 us
    all_to_all x1, blocking collectives, body(): res1 = lax.all_to_all(r1b, 'mem', 0, 0)  13.2 us
  transfers between devices with their start and end apart: 6, of which 3 were waited for; matrix products, arithmetic and copies ran while one was open for 0% of the time, Pallas kernels for 0%

profile of v1, /device:TPU:1, one launch (start us, length us, event | category | flops | bytes accessed | tf_op | source)
XLA Modules:
  0.0 174.9 jit_solution(16707072119142289599)
XLA Ops:
  0.6 0.0 copy-start.7
  0.6 2.5 %convert.4 = bf16[8,32,4096]{2,1,0:T(8,128)(2,1)S(1)} convert(f32[8,32,4096]{2,1,0:T(8,128)} %alpha_ref.5) | non-fusion elementwise | flops 1048576 | bytes 6291456 | tf_op jit(solution)/shard_map/convert.1
  3.1 0.1 fusion.1
  3.2 1.5 collective-permute-start.1
  4.6 1.7 collective-permute-start
  6.3 0.0 copy-done.7
  6.3 0.1 copy.13
  6.4 0.6 add_select_fusion.cols
  7.1 3.3 %collective-permute-done.1.high_ref = bf16[8,32,512]{2,1,0:T(8,128)(2,1)S(1)} collective-permute-done((bf16[8,32,512]{2,1,0:T(8,128)(2,1)S(1)}, bf16[8,32,512]{2,1,0:T(8,128)(2,1)S(1)}, u32[]{:S(2)}, u32[]{:S(2)}) %collective-permute-start.1) | collective-permute-done | bytes 262176 | tf_op jit(solution)/shard_map/ppermute | solution.py:17
  10.3 0.0 copy-start.2
  10.3 0.0 collective-permute-done.low_ref
  10.3 0.0 copy-start.3
  10.3 0.7 copy-done.2
  11.0 0.1 copy-done.3
  11.1 12.0 %forward_first.1 = bf16[8,2,32,512]{3,2,1,0:T(8,128)(2,1)} custom-call(s32[1]{0:T(128)} %bitcast.scal, s32[32,6]{1,0:T(8,128)} %add_select_fusion.cols, f32[8,32,4096]{2,1,0:T(8,128)} %alpha_ref.5, bf16[8,32,512]{2,1,0:T(8,128)(2,1)} %copy-done.3, bf16[8,32,512]{2,1,0:T(8,128)(2,1)} %copy-done.2, bf16[32,6,128,128]{3,2,1,0:T(8,128)(2,1)} %coef_ref.7, ...), custom_call_target="tpu_custom_call" | custom-call | tf_op jit(solution)/shard_map/forward_first/pallas_call | solution.py:278
  23.1 15.8 %all_to_all.31.y_ref = bf16[8,2,32,512]{3,2,1,0:T(8,128)(2,1)} all-to-all(bf16[8,2,32,512]{3,2,1,0:T(8,128)(2,1)} %forward_first.1), channel_id=1, replica_groups=mesh['tile'=16,'mem'=8] {'mem'}, dimensions={0} | all-to-all | bytes 1048576 | tf_op jit(solution)/shard_map/all_to_all | solution.py:292
  38.9 2.1 %residual_first.1 = (bf16[8,2,32,512]{3,2,1,0:T(8,128)(2,1)}, f32[2,32,512]{2,1,0:T(8,128)}) custom-call(s32[1]{0:T(128)} %bitcast.scal, bf16[8,2,32,512]{3,2,1,0:T(8,128)(2,1)} %all_to_all.31.y_ref, f32[2,32,4096]{2,1,0:T(8,128)} %rinv_ref.3, f32[2,32,4096]{2,1,0:T(8,128)} %innov_ref.3), custom_call_target="tpu_custom_call" | custom-call | tf_op jit(solution)/shard_map/residual_first/pallas_call | solution.py:293
  41.0 13.2 %all_to_all.32.res_ref.res1_ref = bf16[8,2,32,512]{3,2,1,0:T(8,128)(2,1)} all-to-all(bf16[8,2,32,512]{3,2,1,0:T(8,128)(2,1)} %get-tuple-element.16.old_ref), channel_id=1, replica_groups=mesh['tile'=16,'mem'=8] {'mem'}, dimensions={0} | all-to-all | bytes 1048576 | tf_op jit(solution)/shard_map/all_to_all | solution.py:305
  54.1 13.0 %adjoint.2 = (f32[40,256,128]{2,1,0:T(8,128)}, bf16[8,256,128]{2,1,0:T(8,128)(2,1)}, bf16[8,256,128]{2,1,0:T(8,128)(2,1)}) custom-call(s32[32,6]{1,0:T(8,128)} %add_select_fusion.cols, bf16[8,2,32,512]{3,2,1,0:T(8,128)(2,1)} %all_to_all.32.res_ref.res1_ref, bf16[8,2,32,4096]{3,2,1,0:T(8,128)(2,1)} %anom_ref.7, bf16[32,6,128,128]{3,2,1,0:T(8,128)(2,1)} %coef_ref.7), custom_call_target="tpu_custom_call" | custom-call | tf_op jit(solution)/shard_map/adjoint/pallas_call | solution.py:308
  67.1 7.7 %collective-permute-start.2 = (bf16[8,256,128]{2,1,0:T(8,128)(2,1)}, bf16[8,256,128]{2,1,0:T(8,128)(2,1)S(1)}, u32[]{:S(2)}, u32[]{:S(2)}) collective-permute-start(bf16[8,256,128]{2,1,0:T(8,128)(2,1)} %get-tuple-element.18), channel_id=1, source_target_pairs={{0,8},{8,16},{16,24},{24,32},{32,40},{40,48},{48,56},{56,64},{64,7... | collective-permute-start | bytes 1572872 | tf_op jit(solution)/shard_map/ppermute | solution.py:17
  74.8 1.3 collective-permute-start.3
  76.1 5.1 %collective-permute-done.2.prev_ref.prev1_ref = bf16[8,256,128]{2,1,0:T(8,128)(2,1)S(1)} collective-permute-done((bf16[8,256,128]{2,1,0:T(8,128)(2,1)}, bf16[8,256,128]{2,1,0:T(8,128)(2,1)S(1)}, u32[]{:S(2)}, u32[]{:S(2)}) %collective-permute-start.2) | collective-permute-done | bytes 524320 | tf_op jit(solution)/shard_map/ppermute | solution.py:17
  81.3 0.0 copy-start
  81.3 2.7 %collective-permute-done.3.next_ref.next1_ref = bf16[8,256,128]{2,1,0:T(8,128)(2,1)S(1)} collective-permute-done((bf16[8,256,128]{2,1,0:T(8,128)(2,1)}, bf16[8,256,128]{2,1,0:T(8,128)(2,1)S(1)}, u32[]{:S(2)}, u32[]{:S(2)}) %collective-permute-start.3) | collective-permute-done | bytes 524320 | tf_op jit(solution)/shard_map/ppermute | solution.py:17
  83.9 0.0 copy-start.1
  83.9 0.0 copy-done
  83.9 0.8 copy-done.1
  84.7 14.1 %forward_second.1 = (bf16[8,2,32,512]{3,2,1,0:T(8,128)(2,1)}, f32[32,128]{1,0:T(8,128)}) custom-call(s32[1]{0:T(128)} %bitcast.scal, s32[32,6]{1,0:T(8,128)} %add_select_fusion.cols, f32[8,32,4096]{2,1,0:T(8,128)} %alpha_ref.5, f32[40,256,128]{2,1,0:T(8,128)} %get-tuple-element.17.acc_ref.acc1_ref, bf16[8,256,128]{2,1,0:T(8,128)(2,1)} %copy-done, ...), custom_call_target="tpu_custom_call" | custom-call | tf_op jit(solution)/shard_map/forward_second/pallas_call | solution.py:329
  98.8 13.2 %all_to_all.33.y_ref = bf16[8,2,32,512]{3,2,1,0:T(8,128)(2,1)} all-to-all(bf16[8,2,32,512]{3,2,1,0:T(8,128)(2,1)} %get-tuple-element.20), channel_id=1, replica_groups=mesh['tile'=16,'mem'=8] {'mem'}, dimensions={0} | all-to-all | bytes 1048576 | tf_op jit(solution)/shard_map/all_to_all | solution.py:345
  112.0 2.2 %residual_second.1 = (bf16[8,2,32,512]{3,2,1,0:T(8,128)(2,1)}, f32[128,128]{1,0:T(8,128)}) custom-call(s32[1]{0:T(128)} %bitcast.scal, bf16[8,2,32,512]{3,2,1,0:T(8,128)(2,1)} %all_to_all.33.y_ref, f32[2,32,4096]{2,1,0:T(8,128)} %rinv_ref.3, f32[2,32,4096]{2,1,0:T(8,128)} %innov_ref.3, f32[2,32,512]{2,1,0:T(8,128)} %get-tuple-element.21.inc_ref, ...), custom_call_target="tpu_custom_call" | custom-call | tf_op jit(solution)/shard_map/residual_second/pallas_call | solution.py:346
  114.2 13.2 %all_to_all.34.res_ref.res2_ref = bf16[8,2,32,512]{3,2,1,0:T(8,128)(2,1)} all-to-all(bf16[8,2,32,512]{3,2,1,0:T(8,128)(2,1)} %get-tuple-element.24), channel_id=1, replica_groups=mesh['tile'=16,'mem'=8] {'mem'}, dimensions={0} | all-to-all | bytes 1048576 | tf_op jit(solution)/shard_map/all_to_all | solution.py:358
  127.4 0.0 copy-start.6
  127.4 12.8 %adjoint.3 = (f32[40,256,128]{2,1,0:T(8,128)}, bf16[4,256,128]{2,1,0:T(8,128)(2,1)}, bf16[4,256,128]{2,1,0:T(8,128)(2,1)}) custom-call(s32[32,6]{1,0:T(8,128)} %add_select_fusion.cols, bf16[8,2,32,512]{3,2,1,0:T(8,128)(2,1)} %all_to_all.34.res_ref.res2_ref, bf16[8,2,32,4096]{3,2,1,0:T(8,128)(2,1)} %anom_ref.7, bf16[32,6,128,128]{3,2,1,0:T(8,128)(2,1)} %coef_ref.7), custom_call_target="tpu_custom_call" | custom-call | tf_op jit(solution)/shard_map/adjoint/pallas_call | solution.py:308
  140.2 6.6 %collective-permute-start.4 = (bf16[4,256,128]{2,1,0:T(8,128)(2,1)}, bf16[4,256,128]{2,1,0:T(8,128)(2,1)S(1)}, u32[]{:S(2)}, u32[]{:S(2)}) collective-permute-start(bf16[4,256,128]{2,1,0:T(8,128)(2,1)} %get-tuple-element.26), channel_id=1, source_target_pairs={{0,8},{8,16},{16,24},{24,32},{32,40},{40,48},{48,56},{56,64},{64,7... | collective-permute-start | bytes 786440 | tf_op jit(solution)/shard_map/ppermute | solution.py:17
  146.8 0.0 collective-permute-start.5
  146.8 0.0 copy-done.6
  146.8 15.7 %all_to_all.35 = f32[128,1,128]{2,1,0:T(1,128)} all-to-all(f32[128,1,128]{2,1,0:T(1,128)S(1)} %bitcast.6), channel_id=1, replica_groups=mesh['tile'=16,'mem'=8] {'tile','mem'}, dimensions={0} | all-to-all | bytes 131072 | tf_op jit(solution)/shard_map/all_to_all | solution.py:359
  162.4 0.0 collective-permute-done.4.prev2_ref
  162.4 0.0 copy-start.4
  162.4 0.0 collective-permute-done.5.next2_ref
  162.5 0.0 copy-start.5
  162.5 0.7 copy-done.4
  163.2 0.1 copy-done.5
  163.3 11.6 %final.1 = (f32[8,32,4096]{2,1,0:T(8,128)}, f32[4,4096]{1,0:T(4,128)}, f32[8,32,4096]{2,1,0:T(8,128)}, f32[4,4096]{1,0:T(4,128)}) custom-call(s32[1]{0:T(128)} %bitcast.scal, f32[128,128]{1,0:T(8,128)} %bitcast.5, f32[8,32,4096]{2,1,0:T(8,128)} %alpha_ref.5, f32[40,256,128]{2,1,0:T(8,128)} %get-tuple-element.17.acc_ref.acc1_ref, ...), custom_call_target="tpu_custom_call" | custom-call | tf_op jit(solution)/shard_map/final/pallas_call | solution.py:366
Async XLA Ops:
  0.6 5.7 %copy-start.7 = (s32[32,6]{0,1:T(8,128)S(1)}, s32[32,6]{0,1:T(8,128)}, u32[]{:S(2)}) copy-start(s32[32,6]{0,1:T(8,128)} %param.14) | copy-start | bytes 2308
  3.2 7.1 %collective-permute-start.1 = (bf16[8,32,512]{2,1,0:T(8,128)(2,1)S(1)}, bf16[8,32,512]{2,1,0:T(8,128)(2,1)S(1)}, u32[]{:S(2)}, u32[]{:S(2)}) collective-permute-start(bf16[8,32,512]{2,1,0:T(8,128)(2,1)S(1)} %get-tuple-element.28), channel_id=1, source_target_pairs={{0,120},{8,0},{16,8},{24,16},{32,24},{40,32},{48,40},{56,48},{64,5... | collective-permute-start | bytes 786440 | tf_op jit(solution)/shard_map/ppermute | solution.py:17
  4.6 5.7 %collective-permute-start = (bf16[8,32,512]{2,1,0:T(8,128)(2,1)S(1)}, bf16[8,32,512]{2,1,0:T(8,128)(2,1)S(1)}, u32[]{:S(2)}, u32[]{:S(2)}) collective-permute-start(bf16[8,32,512]{2,1,0:T(8,128)(2,1)S(1)} %get-tuple-element.29), channel_id=1, source_target_pairs={{0,8},{8,16},{16,24},{24,32},{32,40},{40,48},{48,56},{56,64},{64,7... | collective-permute-start | bytes 786440 | tf_op jit(solution)/shard_map/ppermute | solution.py:17
  10.3 0.7 copy-start.2
  10.3 0.8 copy-start.3
  67.1 14.2 %collective-permute-start.2 = (bf16[8,256,128]{2,1,0:T(8,128)(2,1)}, bf16[8,256,128]{2,1,0:T(8,128)(2,1)S(1)}, u32[]{:S(2)}, u32[]{:S(2)}) collective-permute-start(bf16[8,256,128]{2,1,0:T(8,128)(2,1)} %get-tuple-element.18), channel_id=1, source_target_pairs={{0,8},{8,16},{16,24},{24,32},{32,40},{40,48},{48,56},{56,64},{64,7... | collective-permute-start | bytes 1572872 | tf_op jit(solution)/shard_map/ppermute | solution.py:17
  74.8 9.1 %collective-permute-start.3 = (bf16[8,256,128]{2,1,0:T(8,128)(2,1)}, bf16[8,256,128]{2,1,0:T(8,128)(2,1)S(1)}, u32[]{:S(2)}, u32[]{:S(2)}) collective-permute-start(bf16[8,256,128]{2,1,0:T(8,128)(2,1)} %get-tuple-element.19), channel_id=1, source_target_pairs={{0,120},{8,0},{16,8},{24,16},{32,24},{40,32},{48,40},{56,48},{64,5... | collective-permute-start | bytes 1572872 | tf_op jit(solution)/shard_map/ppermute | solution.py:17
  81.3 2.7 %copy-start = (bf16[8,256,128]{2,1,0:T(8,128)(2,1)}, bf16[8,256,128]{2,1,0:T(8,128)(2,1)S(1)}, u32[]{:S(2)}) copy-start(bf16[8,256,128]{2,1,0:T(8,128)(2,1)S(1)} %collective-permute-done.2.prev_ref.prev1_ref) | copy-start | bytes 1572868
  83.9 0.8 copy-start.1
  127.4 19.4 %copy-start.6 = (f32[128,128]{1,0:T(8,128)S(1)}, f32[128,128]{1,0:T(8,128)}, u32[]{:S(2)}) copy-start(f32[128,128]{1,0:T(8,128)} %get-tuple-element.23) | copy-start | bytes 196612
  140.2 22.3 %collective-permute-start.4 = (bf16[4,256,128]{2,1,0:T(8,128)(2,1)}, bf16[4,256,128]{2,1,0:T(8,128)(2,1)S(1)}, u32[]{:S(2)}, u32[]{:S(2)}) collective-permute-start(bf16[4,256,128]{2,1,0:T(8,128)(2,1)} %get-tuple-element.26), channel_id=1, source_target_pairs={{0,8},{8,16},{16,24},{24,32},{32,40},{40,48},{48,56},{56,64},{64,7... | collective-permute-start | bytes 786440 | tf_op jit(solution)/shard_map/ppermute | solution.py:17
  146.8 15.7 %collective-permute-start.5 = (bf16[4,256,128]{2,1,0:T(8,128)(2,1)}, bf16[4,256,128]{2,1,0:T(8,128)(2,1)S(1)}, u32[]{:S(2)}, u32[]{:S(2)}) collective-permute-start(bf16[4,256,128]{2,1,0:T(8,128)(2,1)} %get-tuple-element.27), channel_id=1, source_target_pairs={{0,120},{8,0},{16,8},{24,16},{32,24},{40,32},{48,40},{56,48},{64,5... | collective-permute-start | bytes 786440 | tf_op jit(solution)/shard_map/ppermute | solution.py:17
  162.4 0.7 copy-start.4
  162.5 0.8 copy-start.5

commit v2 on v0

v2 whole, which is shorter than its diff:
```python
import functools
import jax
import jax.numpy as jnp
from jax import lax
from jax.experimental import pallas as pl
from jax.experimental.pallas import tpu as pltpu
from jax.sharding import PartitionSpec as P

W = 4
B = 128
STREAMS = 1
F32 = jnp.float32
BF16 = jnp.bfloat16
MIB = 2**20


def shifted(array, axis, by):
    size = lax.axis_size(axis)
    return lax.ppermute(array, axis, [(i, (i + by) % size) for i in range(size)])


def resident(array):
    return pltpu.with_memory_space_constraint(array, pltpu.VMEM)


def masked(full, me, share, first):
    level = first + lax.broadcasted_iota(jnp.int32, full.shape, 0)
    mine = jnp.logical_and(level >= me * share, level < (me + 1) * share)
    return jnp.where(mine, full, 0.0)


def spread(own, me, levels, first):
    share = own.shape[0]
    return masked(jnp.concatenate([own] * (levels // share), axis=0), me, share, first)


def gathered(full, share):
    parts = [full[g * share : (g + 1) * share] for g in range(full.shape[0] // share)]
    return functools.reduce(jnp.add, parts)


def lanes(start, size):
    return pl.ds(pl.multiple_of(start, B), size)


def localize(first, levels, cols, xs, coef_ref, anom_ref, out_ref, static_of):
    groups = out_ref.shape[0]
    nblocks, slots = coef_ref.shape[:2]
    members, slot_count = anom_ref.shape[:2]
    rows = nblocks // groups
    lv = slice(first, first + levels)

    def step(d, carry):
        static = static_of(d)
        for r in range(rows):
            i = d * rows + r
            sl = slice(r * B, (r + 1) * B)
            lhs = jnp.concatenate([xs[cols[i, s]] for s in range(slots)], axis=1)
            rhs = jnp.concatenate([coef_ref[i, s] for s in range(slots)], axis=1)
            loc = lax.dot_general(
                lhs, rhs, (((1,), (1,)), ((), ())), preferred_element_type=F32
            ).reshape(members, levels, B)
            for t in range(slot_count):
                a = anom_ref[:, t, lv, lanes(i * B, B)].astype(F32)
                inc = jnp.sum(a * loc, axis=0) + static[:, sl]
                out_ref[d, t, :, sl] = inc.astype(BF16)
        return carry

    lax.fori_loop(0, groups, step, 0)


def forward_first(
    first, levels, me_ref, cols, alpha_ref, low_ref, high_ref, coef_ref, anom_ref, chi_ref, sig_ref,
    out_ref, xs,
):
    members, _, columns = alpha_ref.shape
    n = columns // B
    width = columns // out_ref.shape[0]
    ml = members * levels
    lv = slice(first, first + levels)
    for b in range(W):
        xs[b] = low_ref[:, lv, b * B : (b + 1) * B].reshape(ml, B)
        xs[W + n + b] = high_ref[:, lv, b * B : (b + 1) * B].reshape(ml, B)

    def load(b, carry):
        xs[W + b] = alpha_ref[:, lv, lanes(b * B, B)].astype(BF16).reshape(ml, B)
        return carry

    lax.fori_loop(0, n, load, 0, unroll=4)

    def static_of(d):
        cut = lanes(d * width, width)
        return spread(sig_ref[:, cut] * chi_ref[:, cut], me_ref[0], levels, first)

    localize(first, levels, cols, xs, coef_ref, anom_ref, out_ref, static_of)


def forward_second(
    first, levels, me_ref, cols, alpha_ref, acc_ref, prev_ref, next_ref, coef_ref, anom_ref, chi_ref,
    sig_ref, res_ref, out_ref, norm_ref, xs,
):
    members, _, columns = alpha_ref.shape
    n = columns // B
    groups = out_ref.shape[0]
    width = columns // groups
    lv = slice(first, first + levels)
    norm_ref[...] = jnp.zeros_like(norm_ref)

    def block(b, adj):
        xs[b] = (-adj).astype(BF16)

    def own(b, adj):
        block(b, adj)
        g = alpha_ref[:, lv, lanes((b - W) * B, B)] + adj.reshape(members, levels, B)
        norm_ref[...] += jnp.sum(g * g, axis=0)

    for b in range(W):
        block(b, acc_ref[b] + prev_ref[b].astype(F32))
        own(W + b, acc_ref[W + b] + prev_ref[W + b].astype(F32))
        own(n + b, acc_ref[n + b] + next_ref[b].astype(F32))
        block(n + W + b, acc_ref[n + W + b] + next_ref[W + b].astype(F32))

    def inner(b, carry):
        own(b, acc_ref[b])
        return carry

    lax.fori_loop(2 * W, n, inner, 0, unroll=2)

    def static_of(d):
        cut = lanes(d * width, width)
        rsum = res_ref[d, 0].astype(F32) + res_ref[d, 1].astype(F32)
        sig = spread(sig_ref[:, cut], me_ref[0], levels, first)
        chi = spread(chi_ref[:, cut], me_ref[0], levels, first)
        sr = sig * rsum
        gc = chi + sr
        sq = gc * gc
        for r in range(width // B):
            norm_ref[...] += sq[:, r * B : (r + 1) * B]
        return -(sig * sr)

    localize(first, levels, cols, xs, coef_ref, anom_ref, out_ref, static_of)


def residual_first(first, levels, me_ref, y_ref, rinv_ref, innov_ref, out_ref, inc_ref):
    width = y_ref.shape[-1]
    lv = slice(first, first + levels)
    cut = lanes(me_ref[0] * width, width)
    y = jnp.sum(y_ref[...].astype(F32), axis=0)
    inc_ref[...] = y
    r = (rinv_ref[:, lv, cut] * (y - innov_ref[:, lv, cut])).astype(BF16)
    for k in range(out_ref.shape[0]):
        out_ref[k] = r


def residual_second(
    first, levels, me_ref, y_ref, rinv_ref, innov_ref, inc_ref, old_ref, norm_ref, out_ref, sum_ref
):
    width = y_ref.shape[-1]
    lv = slice(first, first + levels)
    cut = lanes(me_ref[0] * width, width)
    y = jnp.sum(y_ref[...].astype(F32), axis=0)
    r = (rinv_ref[:, lv, cut] * (y - innov_ref[:, lv, cut])).astype(BF16)
    for k in range(out_ref.shape[0]):
        out_ref[k] = r
    change = (old_ref[0].astype(F32) - r.astype(F32)) * (inc_ref[...] - y)
    change = jnp.sum(change.reshape(-1, 8, width), axis=0)
    norm = norm_ref[...].reshape(-1, 8, B).sum(axis=0)
    lane = lax.broadcasted_iota(jnp.int32, sum_ref.shape, 1)
    sum_ref[...] = jnp.where(lane == 0, jnp.sum(norm), jnp.where(lane == 1, jnp.sum(change), 0.0))


def adjoint_kernel(first, levels, cols, res_ref, anom_ref, coef_ref, acc_ref, low_ref, high_ref):
    groups = res_ref.shape[0]
    nblocks, slots = coef_ref.shape[:2]
    members, slot_count = anom_ref.shape[:2]
    rows = nblocks // groups
    padded = nblocks + 2 * W
    ml = members * levels
    lv = slice(first, first + levels)

    def clear(b, carry):
        acc_ref[b] = jnp.zeros(acc_ref.shape[1:], F32)
        return carry

    lax.fori_loop(0, padded, clear, 0)

    def step(d, carry):
        for r in range(rows):
            i = d * rows + r
            sl = slice(r * B, (r + 1) * B)
            w = functools.reduce(
                jnp.add,
                [
                    anom_ref[:, t, lv, lanes(i * B, B)].astype(F32)
                    * res_ref[d, t, :, sl].astype(F32)[None]
                    for t in range(slot_count)
                ],
            )
            w = w.astype(BF16).reshape(ml, B)
            rhs = jnp.concatenate([coef_ref[i, s] for s in range(slots)], axis=1)
            part = jnp.dot(w, rhs, preferred_element_type=F32)
            for s in range(slots):
                acc_ref[cols[i, s]] += part[:, s * B : (s + 1) * B]
        return carry

    lax.fori_loop(0, groups, step, 0)
    halo = low_ref.shape[0]
    for b in range(halo):
        low_ref[b] = acc_ref[b].astype(BF16)
        high_ref[b] = acc_ref[padded - halo + b].astype(BF16)


def final_kernel(
    me_ref, sums_ref, alpha_ref, chi_ref, sig_ref, acc1, acc2, prev1, next1, prev2, next2, res1, res2,
    an_ref, cn_ref, ga_ref, gc_ref,
):
    d = pl.program_id(0)
    members, total, width = an_ref.shape
    streams = len(acc1)
    levels = total // streams
    rows = width // B
    share = chi_ref.shape[0]
    cut = lanes(d * width, width)
    totals = sum(jnp.sum(s[...], axis=0, keepdims=True) for s in sums_ref)
    lane = lax.broadcasted_iota(jnp.int32, totals.shape, 1)
    norm = jnp.sum(jnp.where(lane == 0, totals, 0.0), axis=1, keepdims=True)
    prod = norm + jnp.sum(jnp.where(lane == 1, totals, 0.0), axis=1, keepdims=True)
    step = norm / prod

    def rows_out(extra1, extra2):
        for h in range(streams):
            lv = slice(h * levels, (h + 1) * levels)
            for r in range(rows):
                sl = slice(r * B, (r + 1) * B)
                a1 = acc1[h][W + d * rows + r]
                a2 = acc2[h][W + d * rows + r]
                if extra1 is not None:
                    a1 = a1 + extra1(h, r).astype(F32)
                    a2 = a2 + extra2(h, r).astype(F32)
                a1 = a1.reshape(members, levels, B)
                a2 = a2.reshape(members, levels, B)
                a0 = alpha_ref[:, lv, lanes((d * rows + r) * B, B)]
                g = a0 + a1
                q = g + (a1 - a2)
                an_ref[:, lv, sl] = a0 - step[None] * g
                ga_ref[:, lv, sl] = g - step[None] * q

    last = pl.num_programs(0) - 1

    @pl.when(d == 0)
    def _():
        rows_out(lambda h, r: prev1[h][W + r], lambda h, r: prev2[h][r])

    @pl.when(d == last)
    def _():
        rows_out(lambda h, r: next1[h][r], lambda h, r: next2[h][r])

    @pl.when(jnp.logical_and(d > 0, d < last))
    def _():
        rows_out(None, None)

    def own_sum(res):
        parts = []
        for h in range(streams):
            s = res[h][d, 0].astype(F32) + res[h][d, 1].astype(F32)
            parts.append(gathered(masked(s, me_ref[0], share, h * levels), share))
        return functools.reduce(jnp.add, parts)

    s1 = own_sum(res1)
    s2 = own_sum(res2)
    chi = chi_ref[:, cut]
    sg = sig_ref[:, cut]
    g = chi + sg * s1
    q = g + (sg * s1 - sg * s2)
    cn_ref[...] = chi - step * g
    gc_ref[...] = g - step * q


def body(anomalies, alpha0, chi0, sigma, innov, rinv, taper_cols, taper_coef):
    members, all_levels, columns = alpha0.shape
    slot_count = anomalies.shape[1]
    nblocks, slots = taper_cols.shape
    share = chi0.shape[0]
    groups = lax.axis_size("mem")
    tiles = lax.axis_size("tile")
    me = lax.axis_index("mem").astype(jnp.int32).reshape(1)
    width = columns // groups
    levels = all_levels // STREAMS
    ml = members * levels
    padded = nblocks + 2 * W
    cols = (taper_cols - lax.axis_index("tile") * nblocks + W) % (nblocks * tiles)

    vm = pl.BlockSpec(memory_space=pltpu.VMEM)
    sm = pl.BlockSpec(memory_space=pltpu.SMEM)

    def call(kernel, name, scalars, operands, outs, scratch=(), limit=8):
        return pl.pallas_call(
            kernel,
            in_specs=[sm] * len(scalars) + [vm] * len(operands),
            out_specs=[vm] * len(outs),
            out_shape=[pltpu.VMEM(o.shape, o.dtype) for o in outs],
            scratch_shapes=list(scratch),
            compiler_params=pltpu.CompilerParams(vmem_limit_bytes=limit * MIB),
            name=name,
        )(*scalars, *[resident(o) for o in operands])

    pieces = jax.ShapeDtypeStruct((groups, slot_count, levels, width), BF16)
    inc_out = jax.ShapeDtypeStruct((slot_count, levels, width), F32)
    xs = pltpu.VMEM((padded, ml, B), BF16)
    part = functools.partial

    low = shifted(alpha0[:, :, columns - W * B :].astype(BF16), "tile", 1)
    high = shifted(alpha0[:, :, : W * B].astype(BF16), "tile", -1)

    def exchanged(x):
        return lax.all_to_all(x, "mem", 0, 0)

    def adjoint(first, res, halo):
        edge = jax.ShapeDtypeStruct((halo, ml, B), BF16)
        acc, lo, hi = call(
            part(adjoint_kernel, first, levels), "adjoint", [cols], [res, anomalies, taper_coef],
            [jax.ShapeDtypeStruct((padded, ml, B), F32), edge, edge],
        )
        return acc, shifted(hi, "tile", 1), shifted(lo, "tile", -1)

    firsts = [h * levels for h in range(STREAMS)]
    part1 = [
        call(
            part(forward_first, f, levels), "forward_first", [me, cols],
            [alpha0, low, high, taper_coef, anomalies, chi0, sigma], [pieces], [xs],
        )[0]
        for f in firsts
    ]
    got1 = [exchanged(p) for p in part1]
    own1 = [
        call(
            part(residual_first, f, levels), "residual_first", [me], [got, rinv, innov], [pieces, inc_out]
        )
        for f, got in zip(firsts, got1)
    ]
    res1 = [exchanged(o[0]) for o in own1]
    adj1 = [adjoint(f, res, 2 * W) for f, res in zip(firsts, res1)]
    part2 = [
        call(
            part(forward_second, f, levels), "forward_second", [me, cols],
            [alpha0, *adj, taper_coef, anomalies, chi0, sigma, res],
            [pieces, jax.ShapeDtypeStruct((levels, B), F32)], [xs],
        )
        for f, adj, res in zip(firsts, adj1, res1)
    ]
    got2 = [exchanged(p[0]) for p in part2]
    own2 = [
        call(
            part(residual_second, f, levels), "residual_second", [me],
            [got, rinv, innov, own[1], own[0], p[1]],
            [pieces, jax.ShapeDtypeStruct((groups * tiles, B), F32)],
        )
        for f, got, own, p in zip(firsts, got2, own1, part2)
    ]
    res2 = [exchanged(o[0]) for o in own2]
    sums = [lax.all_to_all(o[1], ("tile", "mem"), 0, 0, tiled=True) for o in own2]
    adj2 = [adjoint(f, res, W) for f, res in zip(firsts, res2)]

    operands = [
        sums, alpha0, chi0, sigma,
        [a[0] for a in adj1], [a[0] for a in adj2],
        [a[1] for a in adj1], [a[2] for a in adj1],
        [a[1] for a in adj2], [a[2] for a in adj2],
        res1, res2,
    ]
    flat, tree = jax.tree.flatten(operands)
    count = len(flat)

    def final(me_ref, *refs):
        final_kernel(me_ref, *jax.tree.unflatten(tree, refs[:count]), *refs[count:])

    alpha_spec = pl.BlockSpec((members, all_levels, width), lambda d: (0, 0, d))
    chi_spec = pl.BlockSpec((share, width), lambda d: (0, d))
    out = pl.pallas_call(
        final,
        grid=(groups,),
        in_specs=[sm] + [vm] * count,
        out_specs=[alpha_spec, chi_spec, alpha_spec, chi_spec],
        out_shape=[
            jax.ShapeDtypeStruct(alpha0.shape, F32),
            jax.ShapeDtypeStruct(chi0.shape, F32),
            jax.ShapeDtypeStruct(alpha0.shape, F32),
            jax.ShapeDtypeStruct(chi0.shape, F32),
        ],
        compiler_params=pltpu.CompilerParams(
            dimension_semantics=("arbitrary",), vmem_limit_bytes=8 * MIB
        ),
        name="final",
    )(me, *[resident(o) for o in flat])
    return tuple(out)


def solution(mesh):
    placed = (
        P("mem", None, None, "tile"),
        P("mem", None, "tile"),
        P("mem", "tile"),
        P("mem", "tile"),
        P(None, None, "tile"),
        P(None, None, "tile"),
        P("tile", None),
        P("tile", None, None, None),
    )
    return jax.shard_map(
        body,
        mesh=mesh,
        in_specs=placed,
        out_specs=(
            P("mem", None, "tile"),
            P("mem", "tile"),
            P("mem", None, "tile"),
            P("mem", "tile"),
        ),
        check_vma=False,
    )
```

time: 531 us -> 140 us (0.26); the launches traced: 525 us -> 139 us
  waiting for transfers between devices: 177 us -> 11.2 us
  matrix products: 139 us -> 0 us
  other arithmetic: 50.8 us -> 2.63 us
  local copies, waits for them, and re-layouts: 53.9 us -> 7.34 us
  Pallas kernels: 0 us -> 32.5 us
  between operations: 18.5 us -> 0.78 us
    psum x2 -> x0, waiting for transfers between devices: 166 us -> none  [evaluate(): combined = lax.psum(ensemble_part + placed, 'mem')]
    dot_general x26 -> x0, matrix products: 139 us -> none  [the longest x12 90.4 us: adjoint(): jnp.einsum('mliq,is->mlsq', part_term, onehot[:, column_slot], precision=...]
    all_to_all x0 -> x5, blocking collectives: none -> 66 us  [the longest x4 50.3 us: exchanged(): return lax.all_to_all(x, 'mem', 0, 0)]
    psum x1 -> x0, blocking collectives: 64.6 us -> none  [body(): grad_norm = lax.psum(local_norm, ('tile', 'mem'))]
    pallas_call x0 -> x7, Pallas kernels: none -> 32.5 us  [the longest x6 26.9 us: call(): pl.pallas_call(kernel, in_specs=[sm] * len(scalars) + [vm] * len(operands...]
    gather x2 -> x0, local copies, waits for them, and re-layouts: 16.7 us -> none  [localize(): picked = jnp.take(padded, local_cols, axis=2)]
    unnamed x5 -> x1, other arithmetic: 13.3 us -> 0.01 us
    sub x2 -> x0, other arithmetic: 12.5 us -> none  [the longest x1 11.8 us: body(): g_alpha - step_length * change_alpha]
  transfers between devices with their start and end apart: 10 -> 6, of which waited for: 6 -> 3; matrix products, arithmetic and copies ran while one was open for 3% -> 0% of each run, Pallas kernels for 0% -> 0%
where the time goes in v2:
time: 140 us; the launch traced here: 139 us
  blocking collectives  66 us (47%)
  Pallas kernels  32.5 us (23%)
  starting transfers between devices  19.1 us (14%)
  waiting for transfers between devices  11.2 us (8%)
  local copies, waits for them, and re-layouts  7.34 us (5%)
  other arithmetic  2.63 us (2%)
    all_to_all x4, blocking collectives, exchanged(): return lax.all_to_all(x, 'mem', 0, 0)  50.3 us
    pallas_call x6, Pallas kernels, call(): pl.pallas_call(kernel, in_specs=[sm] * len(scalars) + [vm] * len(operands...  26.9 us
    ppermute x6, starting transfers between devices, shifted(): lax.ppermute(array, axis, [(i, (i + by) % size) for i in range(size)])  19.1 us
    all_to_all x1, blocking collectives, body(): lax.all_to_all(o[1], ('tile', 'mem'), 0, 0, tiled=True)  15.7 us
    ppermute x6, waiting for transfers between devices, shifted(): lax.ppermute(array, axis, [(i, (i + by) % size) for i in range(size)])  11.2 us
    unnamed x25, local copies, waits for them, and re-layouts  7.29 us
    pallas_call x1, Pallas kernels, body(): pl.pallas_call(final, grid=(groups,), in_specs=[sm] + [vm] * count, out_s...  5.61 us
  transfers between devices with their start and end apart: 6, of which 3 were waited for; matrix products, arithmetic and copies ran while one was open for 0% of the time, Pallas kernels for 0%

profile of v2, /device:TPU:1, one launch (start us, length us, event | category | flops | bytes accessed | tf_op | source)
XLA Modules:
  0.0 139.5 jit_solution(13577121572561505349)
XLA Ops:
  0.6 0.0 copy-start.9
  0.6 0.0 copy-start.8
  0.7 0.0 copy-start.7
  0.7 0.0 slice-start
  0.7 2.6 %convert.4 = bf16[8,32,4096]{2,1,0:T(8,128)(2,1)S(1)} convert(f32[8,32,4096]{2,1,0:T(8,128)} %refs_1_.1) | non-fusion elementwise | flops 1048576 | bytes 6291456 | tf_op jit(solution)/shard_map/convert.1
  3.3 0.1 fusion.1
  3.4 1.5 %collective-permute-start.1 = (bf16[8,32,512]{2,1,0:T(8,128)(2,1)S(1)}, bf16[8,32,512]{2,1,0:T(8,128)(2,1)S(1)}, u32[]{:S(2)}, u32[]{:S(2)}) collective-permute-start(bf16[8,32,512]{2,1,0:T(8,128)(2,1)S(1)} %get-tuple-element.28), channel_id=1, source_target_pairs={{0,120},{8,0},{16,8},{24,16},{32,24},{40,32},{48,40},{56,48},{64,5... | collective-permute-start | bytes 786440 | tf_op jit(solution)/shard_map/ppermute | solution.py:19
  4.8 1.7 %collective-permute-start = (bf16[8,32,512]{2,1,0:T(8,128)(2,1)S(1)}, bf16[8,32,512]{2,1,0:T(8,128)(2,1)S(1)}, u32[]{:S(2)}, u32[]{:S(2)}) collective-permute-start(bf16[8,32,512]{2,1,0:T(8,128)(2,1)S(1)} %get-tuple-element.29), channel_id=1, source_target_pairs={{0,8},{8,16},{16,24},{24,32},{32,40},{40,48},{48,56},{56,64},{64,7... | collective-permute-start | bytes 786440 | tf_op jit(solution)/shard_map/ppermute | solution.py:19
  6.5 0.0 copy-done.9
  6.5 0.1 copy.13
  6.6 3.9 %collective-permute-done.1.high_ref = bf16[8,32,512]{2,1,0:T(8,128)(2,1)S(1)} collective-permute-done((bf16[8,32,512]{2,1,0:T(8,128)(2,1)S(1)}, bf16[8,32,512]{2,1,0:T(8,128)(2,1)S(1)}, u32[]{:S(2)}, u32[]{:S(2)}) %collective-permute-start.1) | collective-permute-done | bytes 262176 | tf_op jit(solution)/shard_map/ppermute | solution.py:19
  10.5 0.0 collective-permute-done.low_ref
  10.5 0.0 copy-done.8
  10.5 0.0 copy-done.7
  10.5 0.0 copy-start
  10.5 2.8 %copy-done = bf16[32,6,128,128]{3,2,1,0:T(8,128)(2,1)S(1)} copy-done((bf16[32,6,128,128]{3,2,1,0:T(8,128)(2,1)S(1)}, bf16[32,6,128,128]{3,2,1,0:T(8,128)(2,1)}, u32[]{:S(2)}) %copy-start) | copy-done | bytes 6291480
  13.3 0.0 copy-start.1
  13.3 2.2 %copy-done.1 = f32[8,32,4096]{2,1,0:T(8,128)S(1)} copy-done((f32[8,32,4096]{2,1,0:T(8,128)S(1)}, f32[8,32,4096]{2,1,0:T(8,128)}, u32[]{:S(2)}) %copy-start.1) | copy-done | bytes 4194328
  15.5 0.0 copy-start.3
  15.5 2.2 %copy-done.3 = bf16[8,2,32,4096]{3,2,1,0:T(8,128)(2,1)S(1)} copy-done((bf16[8,2,32,4096]{3,2,1,0:T(8,128)(2,1)S(1)}, bf16[8,2,32,4096]{3,2,1,0:T(8,128)(2,1)}, u32[]{:S(2)}) %copy-start.3) | copy-done | bytes 4194328
  17.7 6.2 %forward_first.1 = bf16[8,2,32,512]{3,2,1,0:T(8,128)(2,1)S(1)} custom-call(s32[1]{0:T(128)} %bitcast.me_ref, s32[32,6]{1,0:T(8,128)S(1)} %add_select_fusion.cols, f32[8,32,4096]{2,1,0:T(8,128)S(1)} %copy-done.1, bf16[8,32,512]{2,1,0:T(8,128)(2,1)S(1)} %collective-permute-done.low_ref, bf16[8,32,512]{2,1,0:T(8,128)(2,1)S(1)} %collective-permute-done.1.high_ref, ...), custom_call_target="tpu_custom_call" | custom-call | tf_op jit(solution)/shard_map/forward_first/pallas_call | solution.py:297
  23.9 0.0 copy-start.4
  23.9 15.8 %all_to_all.31.y_ref = bf16[8,2,32,512]{3,2,1,0:T(8,128)(2,1)S(1)} all-to-all(bf16[8,2,32,512]{3,2,1,0:T(8,128)(2,1)S(1)} %forward_first.1), channel_id=1, replica_groups=mesh['tile'=16,'mem'=8] {'mem'}, dimensions={0} | all-to-all | bytes 1048576 | tf_op jit(solution)/shard_map/all_to_all | solution.py:316
  39.7 0.0 copy-done.5
  39.7 0.0 copy-done.6
  39.7 0.1 residual_first.1
  39.8 11.5 %all_to_all.32.res_ref.refs_10_ = bf16[8,2,32,512]{3,2,1,0:T(8,128)(2,1)S(1)} all-to-all(bf16[8,2,32,512]{3,2,1,0:T(8,128)(2,1)S(1)} %get-tuple-element.16.old_ref), channel_id=1, replica_groups=mesh['tile'=16,'mem'=8] {'mem'}, dimensions={0} | all-to-all | bytes 1048576 | tf_op jit(solution)/shard_map/all_to_all | solution.py:316
  51.2 0.0 slice-done
  51.2 0.0 slice-done.1
  51.2 0.0 copy-done.4
  51.2 0.0 copy-start.2
  51.3 6.8 %adjoint.2 = (f32[40,256,128]{2,1,0:T(8,128)S(1)}, bf16[8,256,128]{2,1,0:T(8,128)(2,1)S(1)}, bf16[8,256,128]{2,1,0:T(8,128)(2,1)S(1)}) custom-call(s32[32,6]{1,0:T(8,128)S(1)} %add_select_fusion.cols, bf16[8,2,32,512]{3,2,1,0:T(8,128)(2,1)S(1)} %all_to_all.32.res_ref.refs_10_, bf16[8,2,32,4096]{3,2,1,0:T(8,128)(2,1)S(1)} %copy-done.4, ...), custom_call_target="tpu_custom_call" | custom-call | tf_op jit(solution)/shard_map/adjoint/pallas_call | solution.py:297
  58.1 7.8 %collective-permute-start.2 = (bf16[8,256,128]{2,1,0:T(8,128)(2,1)S(1)}, bf16[8,256,128]{2,1,0:T(8,128)(2,1)S(1)}, u32[]{:S(2)}, u32[]{:S(2)}) collective-permute-start(bf16[8,256,128]{2,1,0:T(8,128)(2,1)S(1)} %get-tuple-element.18), channel_id=1, source_target_pairs={{0,8},{8,16},{16,24},{24,32},{32,40},{40,48},{48,56},{56,64},{64,7... | collective-permute-start | bytes 1572872 | tf_op jit(solution)/shard_map/ppermute | solution.py:19
  65.9 1.6 %collective-permute-start.3 = (bf16[8,256,128]{2,1,0:T(8,128)(2,1)S(1)}, bf16[8,256,128]{2,1,0:T(8,128)(2,1)S(1)}, u32[]{:S(2)}, u32[]{:S(2)}) collective-permute-start(bf16[8,256,128]{2,1,0:T(8,128)(2,1)S(1)} %get-tuple-element.19), channel_id=1, source_target_pairs={{0,120},{8,0},{16,8},{24,16},{32,24},{40,32},{48,40},{56,48},{64,5... | collective-permute-start | bytes 1572872 | tf_op jit(solution)/shard_map/ppermute | solution.py:19
  67.5 4.6 %collective-permute-done.2.prev_ref.refs_6_ = bf16[8,256,128]{2,1,0:T(8,128)(2,1)S(1)} collective-permute-done((bf16[8,256,128]{2,1,0:T(8,128)(2,1)S(1)}, bf16[8,256,128]{2,1,0:T(8,128)(2,1)S(1)}, u32[]{:S(2)}, u32[]{:S(2)}) %collective-permute-start.2) | collective-permute-done | bytes 524320 | tf_op jit(solution)/shard_map/ppermute | solution.py:19
  72.0 2.8 %collective-permute-done.3.next_ref.refs_7_ = bf16[8,256,128]{2,1,0:T(8,128)(2,1)S(1)} collective-permute-done((bf16[8,256,128]{2,1,0:T(8,128)(2,1)S(1)}, bf16[8,256,128]{2,1,0:T(8,128)(2,1)S(1)}, u32[]{:S(2)}, u32[]{:S(2)}) %collective-permute-start.3) | collective-permute-done | bytes 524320 | tf_op jit(solution)/shard_map/ppermute | solution.py:19
  74.8 0.0 copy-done.2
  74.8 6.7 %forward_second.1 = (bf16[8,2,32,512]{3,2,1,0:T(8,128)(2,1)S(1)}, f32[32,128]{1,0:T(8,128)S(1)}) custom-call(s32[1]{0:T(128)} %bitcast.me_ref, s32[32,6]{1,0:T(8,128)S(1)} %add_select_fusion.cols, f32[8,32,4096]{2,1,0:T(8,128)S(1)} %copy-done.2, f32[40,256,128]{2,1,0:T(8,128)S(1)} %get-tuple-element.17.acc_ref.refs_4_, ...), custom_call_target="tpu_custom_call" | custom-call | tf_op jit(solution)/shard_map/forward_second/pallas_call | solution.py:297
  81.5 11.5 %all_to_all.33.y_ref = bf16[8,2,32,512]{3,2,1,0:T(8,128)(2,1)S(1)} all-to-all(bf16[8,2,32,512]{3,2,1,0:T(8,128)(2,1)S(1)} %get-tuple-element.20), channel_id=1, replica_groups=mesh['tile'=16,'mem'=8] {'mem'}, dimensions={0} | all-to-all | bytes 1048576 | tf_op jit(solution)/shard_map/all_to_all | solution.py:316
  93.0 0.3 residual_second.1
  93.3 11.5 %all_to_all.34.res_ref.refs_11_ = bf16[8,2,32,512]{3,2,1,0:T(8,128)(2,1)S(1)} all-to-all(bf16[8,2,32,512]{3,2,1,0:T(8,128)(2,1)S(1)} %get-tuple-element.24), channel_id=1, replica_groups=mesh['tile'=16,'mem'=8] {'mem'}, dimensions={0} | all-to-all | bytes 1048576 | tf_op jit(solution)/shard_map/all_to_all | solution.py:316
  104.8 6.8 %adjoint.3 = (f32[40,256,128]{2,1,0:T(8,128)S(1)}, bf16[4,256,128]{2,1,0:T(8,128)(2,1)S(1)}, bf16[4,256,128]{2,1,0:T(8,128)(2,1)S(1)}) custom-call(s32[32,6]{1,0:T(8,128)S(1)} %add_select_fusion.cols, bf16[8,2,32,512]{3,2,1,0:T(8,128)(2,1)S(1)} %all_to_all.34.res_ref.refs_11_, bf16[8,2,32,4096]{3,2,1,0:T(8,128)(2,1)S(1)} %copy-done.4, ...), custom_call_target="tpu_custom_call" | custom-call | tf_op jit(solution)/shard_map/adjoint/pallas_call | solution.py:297
  111.6 6.5 %collective-permute-start.4 = (bf16[4,256,128]{2,1,0:T(8,128)(2,1)S(1)}, bf16[4,256,128]{2,1,0:T(8,128)(2,1)S(1)}, u32[]{:S(2)}, u32[]{:S(2)}) collective-permute-start(bf16[4,256,128]{2,1,0:T(8,128)(2,1)S(1)} %get-tuple-element.26), channel_id=1, source_target_pairs={{0,8},{8,16},{16,24},{24,32},{32,40},{40,48},{48,56},{56,64},{64,7... | collective-permute-start | bytes 786440 | tf_op jit(solution)/shard_map/ppermute | solution.py:19
  118.2 0.0 collective-permute-start.5
  118.2 15.7 %all_to_all.35 = f32[128,1,128]{2,1,0:T(1,128)S(1)} all-to-all(f32[128,1,128]{2,1,0:T(1,128)S(1)} %bitcast.8), channel_id=1, replica_groups=mesh['tile'=16,'mem'=8] {'tile','mem'}, dimensions={0} | all-to-all | bytes 131072 | tf_op jit(solution)/shard_map/all_to_all | solution.py:361
  133.9 0.0 collective-permute-done.4.refs_8_
  133.9 0.0 collective-permute-done.5.refs_9_
  133.9 5.6 %final.1 = (f32[8,32,4096]{2,1,0:T(8,128)}, f32[4,4096]{1,0:T(4,128)}, f32[8,32,4096]{2,1,0:T(8,128)}, f32[4,4096]{1,0:T(4,128)}) custom-call(s32[1]{0:T(128)} %bitcast.me_ref, f32[128,128]{1,0:T(8,128)S(1)} %bitcast.7, f32[8,32,4096]{2,1,0:T(8,128)S(1)} %copy-done.2, f32[4,4096]{1,0:T(4,128)S(1)} %copy-done.7, f32[4,4096]{1,0:T(4,128)S(1)} %copy-done.8, ...), custom_call_target="tpu_custom_call" | custom-call | tf_op jit(solution)/shard_map/final/pallas_call | solution.py:379
  (5 shorter events, 0.0 us)
Async XLA Ops:
  0.6 5.9 %copy-start.9 = (s32[32,6]{0,1:T(8,128)S(1)}, s32[32,6]{0,1:T(8,128)}, u32[]{:S(2)}) copy-start(s32[32,6]{0,1:T(8,128)} %param.14) | copy-start | bytes 2308
  0.6 9.9 %copy-start.8 = (f32[4,4096]{1,0:T(4,128)S(1)}, f32[4,4096]{1,0:T(4,128)}, u32[]{:S(2)}) copy-start(f32[4,4096]{1,0:T(4,128)} %refs_3_.1) | copy-start | bytes 196612
  0.7 9.9 %copy-start.7 = (f32[4,4096]{1,0:T(4,128)S(1)}, f32[4,4096]{1,0:T(4,128)}, u32[]{:S(2)}) copy-start(f32[4,4096]{1,0:T(4,128)} %refs_2_.1) | copy-start | bytes 196612
  0.7 50.6 %slice-start = ((s8[6291456]{0:T(1024)(128)(4,1)}), s8[2097152]{0:T(1024)(128)(4,1)S(1)}, s32[]{:S(2)}) async-start(s8[6291456]{0:T(1024)(128)(4,1)} %bitcast.5), calls=%async_computation.5 | async-start | bytes 4194304
  3.4 7.1 %collective-permute-start.1 = (bf16[8,32,512]{2,1,0:T(8,128)(2,1)S(1)}, bf16[8,32,512]{2,1,0:T(8,128)(2,1)S(1)}, u32[]{:S(2)}, u32[]{:S(2)}) collective-permute-start(bf16[8,32,512]{2,1,0:T(8,128)(2,1)S(1)} %get-tuple-element.28), channel_id=1, source_target_pairs={{0,120},{8,0},{16,8},{24,16},{32,24},{40,32},{48,40},{56,48},{64,5... | collective-permute-start | bytes 786440 | tf_op jit(solution)/shard_map/ppermute | solution.py:19
  4.8 5.7 %collective-permute-start = (bf16[8,32,512]{2,1,0:T(8,128)(2,1)S(1)}, bf16[8,32,512]{2,1,0:T(8,128)(2,1)S(1)}, u32[]{:S(2)}, u32[]{:S(2)}) collective-permute-start(bf16[8,32,512]{2,1,0:T(8,128)(2,1)S(1)} %get-tuple-element.29), channel_id=1, source_target_pairs={{0,8},{8,16},{16,24},{24,32},{32,40},{40,48},{48,56},{56,64},{64,7... | collective-permute-start | bytes 786440 | tf_op jit(solution)/shard_map/ppermute | solution.py:19
  10.5 2.8 %copy-start = (bf16[32,6,128,128]{3,2,1,0:T(8,128)(2,1)S(1)}, bf16[32,6,128,128]{3,2,1,0:T(8,128)(2,1)}, u32[]{:S(2)}) copy-start(bf16[32,6,128,128]{3,2,1,0:T(8,128)(2,1)} %coef_ref.7) | copy-start | bytes 18874372
  13.3 2.2 %copy-start.1 = (f32[8,32,4096]{2,1,0:T(8,128)S(1)}, f32[8,32,4096]{2,1,0:T(8,128)}, u32[]{:S(2)}) copy-start(f32[8,32,4096]{2,1,0:T(8,128)} %refs_1_.1) | copy-start | bytes 12582916
  15.5 2.2 %copy-start.3 = (bf16[8,2,32,4096]{3,2,1,0:T(8,128)(2,1)S(1)}, bf16[8,2,32,4096]{3,2,1,0:T(8,128)(2,1)}, u32[]{:S(2)}) copy-start(bf16[8,2,32,4096]{3,2,1,0:T(8,128)(2,1)} %anom_ref.7) | copy-start | bytes 12582916
  17.7 22.0 %copy-start.5 = (f32[2,32,4096]{2,1,0:T(8,128)S(1)}, f32[2,32,4096]{2,1,0:T(8,128)}, u32[]{:S(2)}) copy-start(f32[2,32,4096]{2,1,0:T(8,128)} %rinv_ref.3) | copy-start | bytes 3145732
  17.7 22.0 %copy-start.6 = (f32[2,32,4096]{2,1,0:T(8,128)S(1)}, f32[2,32,4096]{2,1,0:T(8,128)}, u32[]{:S(2)}) copy-start(f32[2,32,4096]{2,1,0:T(8,128)} %innov_ref.3) | copy-start | bytes 3145732
  17.7 33.5 %slice-start.1 = ((s8[6291456]{0:T(1024)(128)(4,1)}), s8[4194304]{0:T(1024)(128)(4,1)S(1)}, s32[]{:S(2)}) async-start(s8[6291456]{0:T(1024)(128)(4,1)} %bitcast.5), calls=%async_computation.6 | async-start | bytes 8388608
  23.9 27.3 %copy-start.4 = (bf16[8,2,32,4096]{3,2,1,0:T(8,128)(2,1)S(1)}, bf16[8,2,32,4096]{3,2,1,0:T(8,128)(2,1)}, u32[]{:S(2)}) copy-start(bf16[8,2,32,4096]{3,2,1,0:T(8,128)(2,1)} %anom_ref.7) | copy-start | bytes 12582916
  51.2 23.6 %copy-start.2 = (f32[8,32,4096]{2,1,0:T(8,128)S(1)}, f32[8,32,4096]{2,1,0:T(8,128)}, u32[]{:S(2)}) copy-start(f32[8,32,4096]{2,1,0:T(8,128)} %refs_1_.1) | copy-start | bytes 12582916
  58.1 13.9 %collective-permute-start.2 = (bf16[8,256,128]{2,1,0:T(8,128)(2,1)S(1)}, bf16[8,256,128]{2,1,0:T(8,128)(2,1)S(1)}, u32[]{:S(2)}, u32[]{:S(2)}) collective-permute-start(bf16[8,256,128]{2,1,0:T(8,128)(2,1)S(1)} %get-tuple-element.18), channel_id=1, source_target_pairs={{0,8},{8,16},{16,24},{24,32},{32,40},{40,48},{48,56},{56,64},{64,7... | collective-permute-start | bytes 1572872 | tf_op jit(solution)/shard_map/ppermute | solution.py:19
  65.9 8.9 %collective-permute-start.3 = (bf16[8,256,128]{2,1,0:T(8,128)(2,1)S(1)}, bf16[8,256,128]{2,1,0:T(8,128)(2,1)S(1)}, u32[]{:S(2)}, u32[]{:S(2)}) collective-permute-start(bf16[8,256,128]{2,1,0:T(8,128)(2,1)S(1)} %get-tuple-element.19), channel_id=1, source_target_pairs={{0,120},{8,0},{16,8},{24,16},{32,24},{40,32},{48,40},{56,48},{64,5... | collective-permute-start | bytes 1572872 | tf_op jit(solution)/shard_map/ppermute | solution.py:19
  111.6 22.3 %collective-permute-start.4 = (bf16[4,256,128]{2,1,0:T(8,128)(2,1)S(1)}, bf16[4,256,128]{2,1,0:T(8,128)(2,1)S(1)}, u32[]{:S(2)}, u32[]{:S(2)}) collective-permute-start(bf16[4,256,128]{2,1,0:T(8,128)(2,1)S(1)} %get-tuple-element.26), channel_id=1, source_target_pairs={{0,8},{8,16},{16,24},{24,32},{32,40},{40,48},{48,56},{56,64},{64,7... | collective-permute-start | bytes 786440 | tf_op jit(solution)/shard_map/ppermute | solution.py:19
  118.2 15.7 %collective-permute-start.5 = (bf16[4,256,128]{2,1,0:T(8,128)(2,1)S(1)}, bf16[4,256,128]{2,1,0:T(8,128)(2,1)S(1)}, u32[]{:S(2)}, u32[]{:S(2)}) collective-permute-start(bf16[4,256,128]{2,1,0:T(8,128)(2,1)S(1)} %get-tuple-element.27), channel_id=1, source_target_pairs={{0,120},{8,0},{16,8},{24,16},{32,24},{40,32},{48,40},{56,48},{64,5... | collective-permute-start | bytes 786440 | tf_op jit(solution)/shard_map/ppermute | solution.py:19

commit v3 on v2

v3 whole, which is shorter than its diff:
```python
import functools
import jax
import jax.numpy as jnp
from jax import lax
from jax.experimental import pallas as pl
from jax.experimental.pallas import tpu as pltpu
from jax.sharding import PartitionSpec as P

W = 4
B = 128
F32 = jnp.float32
BF16 = jnp.bfloat16
MIB = 2**20


def shifted(array, axis, by):
    size = lax.axis_size(axis)
    return lax.ppermute(array, axis, [(i, (i + by) % size) for i in range(size)])


def resident(array):
    return pltpu.with_memory_space_constraint(array, pltpu.VMEM)


def masked(full, me, share, first):
    level = first + lax.broadcasted_iota(jnp.int32, full.shape, 0)
    mine = jnp.logical_and(level >= me * share, level < (me + 1) * share)
    return jnp.where(mine, full, 0.0)


def spread(own, me, levels, first):
    share = own.shape[0]
    return masked(jnp.concatenate([own] * (levels // share), axis=0), me, share, first)


def gathered(full, share):
    parts = [full[g * share : (g + 1) * share] for g in range(full.shape[0] // share)]
    return functools.reduce(jnp.add, parts)


def lanes(start, size):
    return pl.ds(pl.multiple_of(start, B), size)


def localize_group(d, levels, first, cols, xs, coef_ref, anom_ref, out_ref, static):
    groups = out_ref.shape[0]
    nblocks, slots = coef_ref.shape[:2]
    members, slot_count = anom_ref.shape[:2]
    rows = nblocks // groups
    lv = slice(first, first + levels)
    for r in range(rows):
        i = d * rows + r
        sl = slice(r * B, (r + 1) * B)
        lhs = jnp.concatenate([xs[cols[i, s]] for s in range(slots)], axis=1)
        rhs = jnp.concatenate([coef_ref[i, s] for s in range(slots)], axis=1)
        loc = lax.dot_general(
            lhs, rhs, (((1,), (1,)), ((), ())), preferred_element_type=F32
        ).reshape(members, levels, B)
        for t in range(slot_count):
            a = anom_ref[:, t, lv, lanes(i * B, B)].astype(F32)
            inc = jnp.sum(a * loc, axis=0) + static[:, sl]
            out_ref[d, t, :, sl] = inc.astype(BF16)


def first_static(d, width, levels, me_ref, chi_ref, sig_ref):
    cut = lanes(d * width, width)
    return spread(sig_ref[:, cut] * chi_ref[:, cut], me_ref[0], levels, 0)


def second_static(d, width, levels, me_ref, chi_ref, sig_ref, res_ref, norm_ref):
    cut = lanes(d * width, width)
    rsum = res_ref[d, 0].astype(F32) + res_ref[d, 1].astype(F32)
    sig = spread(sig_ref[:, cut], me_ref[0], levels, 0)
    chi = spread(chi_ref[:, cut], me_ref[0], levels, 0)
    sr = sig * rsum
    gc = chi + sr
    sq = gc * gc
    for r in range(width // B):
        norm_ref[...] += sq[:, r * B : (r + 1) * B]
    return -(sig * sr)


def edge_kernel(alpha_hbm, low_ref, high_ref, buf, sem):
    columns = alpha_hbm.shape[-1]
    width = low_ref.shape[-1]
    copies = [
        pltpu.make_async_copy(alpha_hbm.at[:, :, pl.ds(start, width)], buf.at[k], sem.at[k])
        for k, start in enumerate((0, columns - width))
    ]
    for c in copies:
        c.start()
    for c, out in zip(copies, (low_ref, high_ref)):
        c.wait()
        out[...] = buf[0 if out is low_ref else 1].astype(BF16)


def first_inner(
    me_ref, cols, alpha_hbm, coef_hbm, anom_hbm, chi_ref, sig_ref,
    alpha_ref, coef_ref, anom_ref, xs, out_ref, sem,
):
    members, levels, columns = alpha_ref.shape
    groups = out_ref.shape[0]
    width = columns // groups
    rows = width // B
    ml = members * levels

    def copy(kind, d):
        if kind == 0:
            part = (slice(None), slice(None), pl.ds(d * width, width))
            return pltpu.make_async_copy(alpha_hbm.at[part], alpha_ref.at[part], sem.at[kind, d])
        if kind == 1:
            part = pl.ds(d * rows, rows)
            return pltpu.make_async_copy(coef_hbm.at[part], coef_ref.at[part], sem.at[kind, d])
        part = (slice(None), slice(None), slice(None), pl.ds(d * width, width))
        return pltpu.make_async_copy(anom_hbm.at[part], anom_ref.at[part], sem.at[kind, d])

    order = [(0, 0), (0, 1)]
    for d in range(1, groups - 1):
        order += [(0, d + 1), (1, d), (2, d)]
    tail = [(k, d) for d in (0, groups - 1) for k in (1, 2)]
    for kind, d in order + tail:
        copy(kind, d).start()

    def load(d):
        copy(0, d).wait()
        for r in range(rows):
            b = d * rows + r
            xs[W + b] = alpha_ref[:, :, b * B : (b + 1) * B].astype(BF16).reshape(ml, B)

    load(0)
    load(1)
    for d in range(1, groups - 1):
        load(d + 1)
        copy(1, d).wait()
        copy(2, d).wait()
        static = first_static(d, width, levels, me_ref, chi_ref, sig_ref)
        localize_group(d, levels, 0, cols, xs, coef_ref, anom_ref, out_ref, static)
    for kind, d in tail:
        copy(kind, d).wait()


def first_outer(
    me_ref, cols, low_ref, high_ref, coef_ref, anom_ref, chi_ref, sig_ref, xs_in, part_ref, xs, out_ref
):
    members, _, levels, columns = anom_ref.shape
    groups = out_ref.shape[0]
    width = columns // groups
    ml = members * levels
    n = columns // B
    for b in range(W):
        xs[b] = low_ref[:, :, b * B : (b + 1) * B].reshape(ml, B)
        xs[W + n + b] = high_ref[:, :, b * B : (b + 1) * B].reshape(ml, B)

    def step(k, carry):
        d = k * (groups - 1)
        static = first_static(d, width, levels, me_ref, chi_ref, sig_ref)
        localize_group(d, levels, 0, cols, xs, coef_ref, anom_ref, out_ref, static)
        return carry

    lax.fori_loop(0, 2, step, 0)


def adjoint_group(d, cols, res_ref, anom_ref, coef_ref, acc_ref):
    groups = res_ref.shape[0]
    nblocks, slots = coef_ref.shape[:2]
    members, slot_count, levels = anom_ref.shape[:3]
    rows = nblocks // groups
    for r in range(rows):
        i = d * rows + r
        sl = slice(r * B, (r + 1) * B)
        w = functools.reduce(
            jnp.add,
            [
                anom_ref[:, t, :, lanes(i * B, B)].astype(F32) * res_ref[d, t, :, sl].astype(F32)[None]
                for t in range(slot_count)
            ],
        )
        w = w.astype(BF16).reshape(members * levels, B)
        rhs = jnp.concatenate([coef_ref[i, s] for s in range(slots)], axis=1)
        part = jnp.dot(w, rhs, preferred_element_type=F32)
        for s in range(slots):
            acc_ref[cols[i, s]] += part[:, s * B : (s + 1) * B]


def adjoint_edges(outer, cols, res_ref, anom_ref, coef_ref, acc_ref, low_ref, high_ref):
    groups = res_ref.shape[0]
    padded = acc_ref.shape[0]

    def clear(b, carry):
        acc_ref[b] = jnp.zeros(acc_ref.shape[1:], F32)
        return carry

    lax.fori_loop(0, padded, clear, 0)

    def step(k, carry):
        d = jnp.where(k < outer, k, groups - 2 * outer + k)
        adjoint_group(d, cols, res_ref, anom_ref, coef_ref, acc_ref)
        return carry

    lax.fori_loop(0, 2 * outer, step, 0)
    halo = low_ref.shape[0]
    for b in range(halo):
        low_ref[b] = acc_ref[b].astype(BF16)
        high_ref[b] = acc_ref[padded - halo + b].astype(BF16)


def adjoint_all(cols, res_ref, anom_ref, coef_ref, sum_in, acc_ref, low_ref, high_ref, sum_ref):
    adjoint_edges(res_ref.shape[0] // 2, cols, res_ref, anom_ref, coef_ref, acc_ref, low_ref, high_ref)


def adjoint_rest(outer, cols, res_ref, anom_ref, coef_ref, acc_in, acc_ref):
    def step(d, carry):
        adjoint_group(d, cols, res_ref, anom_ref, coef_ref, acc_ref)
        return carry

    lax.fori_loop(outer, res_ref.shape[0] - outer, step, 0)


def second_block(b, adj, alpha_ref, xs, norm_ref, own):
    members, levels = alpha_ref.shape[:2]
    xs[b] = (-adj).astype(BF16)
    if own:
        g = alpha_ref[:, :, lanes((b - W) * B, B)] + adj.reshape(members, levels, B)
        norm_ref[...] += jnp.sum(g * g, axis=0)


def second_inner(
    outer, me_ref, cols, res_ref, anom_ref, coef_ref, alpha_ref, chi_ref, sig_ref, acc_in,
    acc_ref, xs, out_ref, norm_ref,
):
    adjoint_rest(outer, cols, res_ref, anom_ref, coef_ref, acc_in, acc_ref)
    levels = alpha_ref.shape[1]
    groups = out_ref.shape[0]
    padded = acc_ref.shape[0]
    width = out_ref.shape[-1]
    norm_ref[...] = jnp.zeros_like(norm_ref)

    def block(b, carry):
        second_block(b, acc_ref[b], alpha_ref, xs, norm_ref, True)
        return carry

    lax.fori_loop(2 * W, padded - 2 * W, block, 0, unroll=2)

    def step(d, carry):
        static = second_static(d, width, levels, me_ref, chi_ref, sig_ref, res_ref, norm_ref)
        localize_group(d, levels, 0, cols, xs, coef_ref, anom_ref, out_ref, static)
        return carry

    lax.fori_loop(outer, groups - outer, step, 0)


def second_outer(
    outer, me_ref, cols, res_ref, anom_ref, coef_ref, alpha_ref, chi_ref, sig_ref, acc_ref, prev_ref,
    next_ref, xs_in, part_in, norm_in, xs, out_ref, norm_ref,
):
    levels = alpha_ref.shape[1]
    groups = out_ref.shape[0]
    width = out_ref.shape[-1]
    n = acc_ref.shape[0] - 2 * W
    for b in range(2 * W):
        second_block(b, acc_ref[b] + prev_ref[b].astype(F32), alpha_ref, xs, norm_ref, b >= W)
        second_block(n + b, acc_ref[n + b] + next_ref[b].astype(F32), alpha_ref, xs, norm_ref, b < W)

    def step(k, carry):
        d = jnp.where(k < outer, k, groups - 2 * outer + k)
        static = second_static(d, width, levels, me_ref, chi_ref, sig_ref, res_ref, norm_ref)
        localize_group(d, levels, 0, cols, xs, coef_ref, anom_ref, out_ref, static)
        return carry

    lax.fori_loop(0, 2 * outer, step, 0)


def residual_first(me_ref, y_ref, rinv_ref, innov_ref, out_ref, inc_ref):
    width = y_ref.shape[-1]
    cut = lanes(me_ref[0] * width, width)
    y = jnp.sum(y_ref[...].astype(F32), axis=0)
    inc_ref[...] = y
    r = (rinv_ref[:, :, cut] * (y - innov_ref[:, :, cut])).astype(BF16)
    for k in range(out_ref.shape[0]):
        out_ref[k] = r


def residual_second(
    me_ref, y_ref, rinv_ref, innov_ref, inc_ref, old_ref, norm_ref, out_ref, sum_ref
):
    width = y_ref.shape[-1]
    cut = lanes(me_ref[0] * width, width)
    y = jnp.sum(y_ref[...].astype(F32), axis=0)
    r = (rinv_ref[:, :, cut] * (y - innov_ref[:, :, cut])).astype(BF16)
    for k in range(out_ref.shape[0]):
        out_ref[k] = r
    change = (old_ref[0].astype(F32) - r.astype(F32)) * (inc_ref[...] - y)
    change = jnp.sum(change.reshape(-1, 8, width), axis=0)
    norm = norm_ref[...].reshape(-1, 8, B).sum(axis=0)
    lane = lax.broadcasted_iota(jnp.int32, sum_ref.shape, 1)
    sum_ref[...] = jnp.where(lane == 0, jnp.sum(norm), jnp.where(lane == 1, jnp.sum(change), 0.0))


def final_kernel(
    me_ref, sums_ref, alpha_ref, chi_ref, sig_ref, acc1, acc2, prev1, next1, prev2, next2, res1, res2,
    an_ref, cn_ref, ga_ref, gc_ref,
):
    d = pl.program_id(0)
    members, total, width = an_ref.shape
    streams = len(acc1)
    levels = total // streams
    rows = width // B
    share = chi_ref.shape[0]
    cut = lanes(d * width, width)
    totals = sum(jnp.sum(s[...], axis=0, keepdims=True) for s in sums_ref)
    lane = lax.broadcasted_iota(jnp.int32, totals.shape, 1)
    norm = jnp.sum(jnp.where(lane == 0, totals, 0.0), axis=1, keepdims=True)
    prod = norm + jnp.sum(jnp.where(lane == 1, totals, 0.0), axis=1, keepdims=True)
    step = norm / prod

    def rows_out(extra1, extra2):
        for h in range(streams):
            lv = slice(h * levels, (h + 1) * levels)
            for r in range(rows):
                sl = slice(r * B, (r + 1) * B)
                a1 = acc1[h][W + d * rows + r]
                a2 = acc2[h][W + d * rows + r]
                if extra1 is not None:
                    a1 = a1 + extra1(h, r).astype(F32)
                    a2 = a2 + extra2(h, r).astype(F32)
                a1 = a1.reshape(members, levels, B)
                a2 = a2.reshape(members, levels, B)
                a0 = alpha_ref[:, lv, lanes((d * rows + r) * B, B)]
                g = a0 + a1
                q = g + (a1 - a2)
                an_ref[:, lv, sl] = a0 - step[None] * g
                ga_ref[:, lv, sl] = g - step[None] * q

    last = pl.num_programs(0) - 1

    @pl.when(d == 0)
    def _():
        rows_out(lambda h, r: prev1[h][W + r], lambda h, r: prev2[h][r])

    @pl.when(d == last)
    def _():
        rows_out(lambda h, r: next1[h][r], lambda h, r: next2[h][r])

    @pl.when(jnp.logical_and(d > 0, d < last))
    def _():
        rows_out(None, None)

    def own_sum(res):
        parts = []
        for h in range(streams):
            s = res[h][d, 0].astype(F32) + res[h][d, 1].astype(F32)
            parts.append(gathered(masked(s, me_ref[0], share, h * levels), share))
        return functools.reduce(jnp.add, parts)

    s1 = own_sum(res1)
    s2 = own_sum(res2)
    chi = chi_ref[:, cut]
    sg = sig_ref[:, cut]
    g = chi + sg * s1
    q = g + (sg * s1 - sg * s2)
    cn_ref[...] = chi - step * g
    gc_ref[...] = g - step * q


def body(anomalies, alpha0, chi0, sigma, innov, rinv, taper_cols, taper_coef):
    members, all_levels, columns = alpha0.shape
    slot_count = anomalies.shape[1]
    nblocks, slots = taper_cols.shape
    share = chi0.shape[0]
    groups = lax.axis_size("mem")
    tiles = lax.axis_size("tile")
    me = lax.axis_index("mem").astype(jnp.int32).reshape(1)
    width = columns // groups
    levels = all_levels
    ml = members * levels
    padded = nblocks + 2 * W
    cols = (taper_cols - lax.axis_index("tile") * nblocks + W) % (nblocks * tiles)

    vm = pl.BlockSpec(memory_space=pltpu.VMEM)
    sm = pl.BlockSpec(memory_space=pltpu.SMEM)

    anywhere = pl.BlockSpec(memory_space=pltpu.HBM)
    part = functools.partial
    sds = jax.ShapeDtypeStruct
    pieces = sds((groups, slot_count, levels, width), BF16)
    inc_out = sds((slot_count, levels, width), F32)
    norm_out = sds((levels, B), F32)
    xs_out = sds((padded, ml, B), BF16)
    acc_out = sds((padded, ml, B), F32)
    work = 2 * ml * slots * B * B

    def call(kernel, name, scalars, operands, outs, scratch=(), limit=8, alias={}, hbm=0, rows=1):
        return pl.pallas_call(
            kernel,
            in_specs=[sm] * len(scalars) + [anywhere] * hbm + [vm] * (len(operands) - hbm),
            out_specs=[vm] * len(outs),
            out_shape=[pltpu.VMEM(o.shape, o.dtype) for o in outs],
            scratch_shapes=list(scratch),
            input_output_aliases={len(scalars) + k: v for k, v in alias.items()},
            compiler_params=pltpu.CompilerParams(vmem_limit_bytes=limit * MIB),
            cost_estimate=pl.CostEstimate(
                flops=8 * rows * work, transcendentals=0, bytes_accessed=rows * 3 * MIB // 4
            ),
            name=name,
        )(
            *scalars,
            *[pltpu.with_memory_space_constraint(o, pltpu.HBM) for o in operands[:hbm]],
            *[resident(o) for o in operands[hbm:]],
        )

    def exchanged(x):
        return lax.all_to_all(x, "mem", 0, 0)

    rim = sds((members, levels, W * B), BF16)
    high, low = call(
        edge_kernel, "edges", [], [alpha0], [rim, rim],
        [pltpu.VMEM((2, members, levels, W * B), F32), pltpu.SemaphoreType.DMA((2,))], hbm=1,
    )
    low = shifted(low, "tile", 1)
    high = shifted(high, "tile", -1)
    alpha, coef, anom, xs1, part1 = call(
        first_inner, "first_inner", [me, cols], [alpha0, taper_coef, anomalies, chi0, sigma],
        [sds(alpha0.shape, F32), sds(taper_coef.shape, BF16), sds(anomalies.shape, BF16), xs_out, pieces],
        [pltpu.SemaphoreType.DMA((3, groups))], hbm=3, rows=24,
    )
    xs1, part1 = call(
        first_outer, "first_outer", [me, cols], [low, high, coef, anom, chi0, sigma, xs1, part1],
        [xs_out, pieces], alias={6: 0, 7: 1}, rows=8,
    )
    got1 = exchanged(part1)
    r1, inc1 = call(residual_first, "residual_first", [me], [got1, rinv, innov], [pieces, inc_out])
    res1 = exchanged(r1)

    outer = 2 * W // (width // B)
    edge = sds((2 * W, ml, B), BF16)
    acc1, low1, high1 = call(
        part(adjoint_edges, outer), "adjoint_edges", [cols], [res1, anom, coef], [acc_out, edge, edge],
        rows=16,
    )
    prev1 = shifted(high1, "tile", 1)
    next1 = shifted(low1, "tile", -1)
    acc1, xs2, part2, norm = call(
        part(second_inner, outer), "second_inner", [me, cols],
        [res1, anom, coef, alpha, chi0, sigma, acc1], [acc_out, xs_out, pieces, norm_out],
        alias={6: 0}, rows=32,
    )
    xs2, part2, norm = call(
        part(second_outer, outer), "second_outer", [me, cols],
        [res1, anom, coef, alpha, chi0, sigma, acc1, prev1, next1, xs2, part2, norm],
        [xs_out, pieces, norm_out], alias={9: 0, 10: 1, 11: 2}, rows=16,
    )
    got2 = exchanged(part2)
    r2, sums = call(
        residual_second, "residual_second", [me], [got2, rinv, innov, inc1, r1, norm],
        [pieces, sds((groups * tiles, B), F32)],
    )
    res2 = exchanged(r2)
    edge = sds((W, ml, B), BF16)
    acc2, low2, high2, sums = call(
        adjoint_all, "adjoint_all", [cols], [res2, anom, coef, sums],
        [acc_out, edge, edge, sds(sums.shape, F32)], alias={3: 3}, rows=32,
    )
    prev2 = shifted(high2, "tile", 1)
    next2 = shifted(low2, "tile", -1)
    sums = lax.all_to_all(sums, ("tile", "mem"), 0, 0, tiled=True)
    operands = [
        [sums], alpha, chi0, sigma, [acc1], [acc2], [prev1], [next1], [prev2], [next2], [res1], [res2]
    ]
    flat, tree = jax.tree.flatten(operands)
    count = len(flat)

    def final(me_ref, *refs):
        final_kernel(me_ref, *jax.tree.unflatten(tree, refs[:count]), *refs[count:])

    alpha_spec = pl.BlockSpec((members, all_levels, width), lambda d: (0, 0, d))
    chi_spec = pl.BlockSpec((share, width), lambda d: (0, d))
    out = pl.pallas_call(
        final,
        grid=(groups,),
        in_specs=[sm] + [vm] * count,
        out_specs=[alpha_spec, chi_spec, alpha_spec, chi_spec],
        out_shape=[
            jax.ShapeDtypeStruct(alpha0.shape, F32),
            jax.ShapeDtypeStruct(chi0.shape, F32),
            jax.ShapeDtypeStruct(alpha0.shape, F32),
            jax.ShapeDtypeStruct(chi0.shape, F32),
        ],
        compiler_params=pltpu.CompilerParams(
            dimension_semantics=("arbitrary",), vmem_limit_bytes=8 * MIB
        ),
        name="final",
    )(me, *[resident(o) for o in flat])
    return tuple(out)


def solution(mesh):
    placed = (
        P("mem", None, None, "tile"),
        P("mem", None, "tile"),
        P("mem", "tile"),
        P("mem", "tile"),
        P(None, None, "tile"),
        P(None, None, "tile"),
        P("tile", None),
        P("tile", None, None, None),
    )
    return jax.shard_map(
        body,
        mesh=mesh,
        in_specs=placed,
        out_specs=(
            P("mem", None, "tile"),
            P("mem", "tile"),
            P("mem", None, "tile"),
            P("mem", "tile"),
        ),
        check_vma=False,
    )
```

time: 140 us -> 123 us (0.88)
  waiting for transfers between devices: 11.2 us -> 1.91 us
  local copies, waits for them, and re-layouts: 7.34 us -> 0.11 us
  starting transfers between devices: 19.1 us -> 13.2 us
  Pallas kernels: 32.5 us -> 36.9 us
  blocking collectives: 66 us -> 69.8 us
  other arithmetic: 2.63 us -> 0.02 us
    ppermute x6, waiting for transfers between devices: 11.2 us -> 1.91 us  [shifted(): lax.ppermute(array, axis, [(i, (i + by) % size) for i in range(size)])]
    unnamed x25 -> x11, local copies, waits for them, and re-layouts: 7.29 us -> 0.11 us
    ppermute x6, starting transfers between devices: 19.1 us -> 13.2 us  [shifted(): lax.ppermute(array, axis, [(i, (i + by) % size) for i in range(size)])]
    pallas_call x6 -> x9, Pallas kernels: 26.9 us -> 31.3 us  [call(): pl.pallas_call(kernel, in_specs=[sm] * len(scalars) + [anywhere] * hbm +...]
    all_to_all x4, blocking collectives: 50.3 us -> 54.3 us  [exchanged(): return lax.all_to_all(x, 'mem', 0, 0)]
    another operation x1 -> x0, other arithmetic: 2.61 us -> none
  transfers between devices with their start and end apart: 6 -> 6, of which waited for: 3 -> 1; matrix products, arithmetic and copies ran while one was open for 0% -> 0% of each run, Pallas kernels for 0% -> 11%
where the time goes in v3:
time: 123 us
  blocking collectives  69.8 us (57%)
  Pallas kernels  36.9 us (30%)
  starting transfers between devices  13.2 us (11%)
  waiting for transfers between devices  1.91 us (2%)
    all_to_all x4, blocking collectives, exchanged(): return lax.all_to_all(x, 'mem', 0, 0)  54.3 us
    pallas_call x9, Pallas kernels, call(): pl.pallas_call(kernel, in_specs=[sm] * len(scalars) + [anywhere] * hbm +...  31.3 us
    all_to_all x1, blocking collectives, body(): sums = lax.all_to_all(sums, ('tile', 'mem'), 0, 0, tiled=True)  15.5 us
    ppermute x6, starting transfers between devices, shifted(): lax.ppermute(array, axis, [(i, (i + by) % size) for i in range(size)])  13.2 us
    pallas_call x1, Pallas kernels, body(): pl.pallas_call(final, grid=(groups,), in_specs=[sm] + [vm] * count, out_s...  5.61 us
  transfers between devices with their start and end apart: 6, of which 1 were waited for; matrix products, arithmetic and copies ran while one was open for 0% of the time, Pallas kernels for 11%

profile of v3, /device:TPU:1, one launch (start us, length us, event | category | flops | bytes accessed | tf_op | source)
XLA Modules:
  0.0 122.7 jit_solution(7465917343902195350)
XLA Ops:
  0.6 0.0 copy-start.4
  0.6 0.0 copy-start.3
  0.7 0.0 copy-start.2
  0.7 1.3 %edges.1 = (bf16[8,32,512]{2,1,0:T(8,128)(2,1)S(1)}, bf16[8,32,512]{2,1,0:T(8,128)(2,1)S(1)}) custom-call(f32[8,32,4096]{2,1,0:T(8,128)} %alpha_hbm.3), custom_call_target="tpu_custom_call" | custom-call | flops 402653184 | bytes 786432 | tf_op jit(solution)/shard_map/edges/pallas_call | solution.py:393
  2.0 3.1 %collective-permute-start = (bf16[8,32,512]{2,1,0:T(8,128)(2,1)S(1)}, bf16[8,32,512]{2,1,0:T(8,128)(2,1)S(1)}, u32[]{:S(2)}, u32[]{:S(2)}) collective-permute-start(bf16[8,32,512]{2,1,0:T(8,128)(2,1)S(1)} %get-tuple-element.29), channel_id=1, source_target_pairs={{0,8},{8,16},{16,24},{24,32},{32,40},{40,48},{48,56},{56,64},{64,7... | collective-permute-start | bytes 786440 | tf_op jit(solution)/shard_map/ppermute | solution.py:18
  5.0 0.0 collective-permute-start.1
  5.0 0.0 copy-done.4
  5.0 0.1 copy.20
  5.2 0.0 copy-done.3
  5.2 0.0 copy-done.2
  5.2 6.5 %first_inner.1 = (f32[8,32,4096]{2,1,0:T(8,128)S(1)}, bf16[32,6,128,128]{3,2,1,0:T(8,128)(2,1)S(1)}, bf16[8,2,32,4096]{3,2,1,0:T(8,128)(2,1)S(1)}, bf16[40,256,1...) custom-call(s32[1]{0:T(128)} %bitcast.me_ref, s32[32,6]{1,0:T(8,128)S(1)} %add_select_fusion.cols, ...), custom_call_target="tpu_custom_call" | custom-call | flops 9663676416 | bytes 18874368 | tf_op jit(solution)/shard_map/first_inner/pallas_call | solution.py:393
  11.6 0.0 collective-permute-done.low_ref
  11.7 0.0 collective-permute-done.1.high_ref
  11.7 0.0 copy-start
  11.7 0.0 copy-start.1
  11.7 2.1 %first_outer.1 = (bf16[40,256,128]{2,1,0:T(8,128)(2,1)S(1)}, bf16[8,2,32,512]{3,2,1,0:T(8,128)(2,1)S(1)}) custom-call(s32[1]{0:T(128)} %bitcast.me_ref, s32[32,6]{1,0:T(8,128)S(1)} %add_select_fusion.cols, bf16[8,32,512]{2,1,0:T(8,128)(2,1)S(1)} %collective-permute-done.low_ref, ...), custom_call_target="tpu_custom_call", output_to_operand_aliasing={{0}: (8, {}), {1}: (9, {})} | custom-call | flops 3221225472 | bytes 6291456 | tf_op jit(solution)/shard_map/first_outer/pallas_call | solution.py:393
  13.8 15.7 %all_to_all.31.y_ref = bf16[8,2,32,512]{3,2,1,0:T(8,128)(2,1)S(1)} all-to-all(bf16[8,2,32,512]{3,2,1,0:T(8,128)(2,1)S(1)} %get-tuple-element.35), channel_id=1, replica_groups=mesh['tile'=16,'mem'=8] {'mem'}, dimensions={0} | all-to-all | bytes 1048576 | tf_op jit(solution)/shard_map/all_to_all | solution.py:412
  29.5 0.0 copy-done
  29.5 0.0 copy-done.1
  29.5 0.1 residual_first.1
  29.6 11.6 %all_to_all.32.res_ref.refs_10_ = bf16[8,2,32,512]{3,2,1,0:T(8,128)(2,1)S(1)} all-to-all(bf16[8,2,32,512]{3,2,1,0:T(8,128)(2,1)S(1)} %get-tuple-element.36.old_ref), channel_id=1, replica_groups=mesh['tile'=16,'mem'=8] {'mem'}, dimensions={0} | all-to-all | bytes 1048576 | tf_op jit(solution)/shard_map/all_to_all | solution.py:412
  41.2 4.1 %adjoint_edges.1 = (f32[40,256,128]{2,1,0:T(8,128)S(1)}, bf16[8,256,128]{2,1,0:T(8,128)(2,1)S(1)}, bf16[8,256,128]{2,1,0:T(8,128)(2,1)S(1)}) custom-call(s32[32,6]{1,0:T(8,128)S(1)} %add_select_fusion.cols, bf16[8,2,32,512]{3,2,1,0:T(8,128)(2,1)S(1)} %all_to_all.32.res_ref.refs_10_, bf16[8,2,32,4096]{3,2,1,0:T(8,128)(2,1)S(1)} %get-tuple-element.32.anom_ref, ...), custom_call_target="tpu_custom_call" | custom-call | flops 6442450944 | bytes 12582912 | tf_op jit(solution)/shard_map/adjoint_edges/pallas_call | solution.py:393
  45.2 7.5 %collective-permute-start.2 = (bf16[8,256,128]{2,1,0:T(8,128)(2,1)S(1)}, bf16[8,256,128]{2,1,0:T(8,128)(2,1)S(1)}, u32[]{:S(2)}, u32[]{:S(2)}) collective-permute-start(bf16[8,256,128]{2,1,0:T(8,128)(2,1)S(1)} %get-tuple-element.40), channel_id=1, source_target_pairs={{0,8},{8,16},{16,24},{24,32},{32,40},{40,48},{48,56},{56,64},{64,7... | collective-permute-start | bytes 1572872 | tf_op jit(solution)/shard_map/ppermute | solution.py:18
  52.7 0.0 collective-permute-start.3
  52.7 6.7 %second_inner.1 = (f32[40,256,128]{2,1,0:T(8,128)S(1)}, bf16[40,256,128]{2,1,0:T(8,128)(2,1)S(1)}, bf16[8,2,32,512]{3,2,1,0:T(8,128)(2,1)S(1)}, f32[32,128]{1,0:T(8,128)S(1)}) custom-call(s32[1]{0:T(128)} %bitcast.me_ref, s32[32,6]{1,0:T(8,128)S(1)} %add_select_fusion.cols, ...), custom_call_target="tpu_custom_call", output_to_operand_aliasing={{0}: (8, {})} | custom-call | flops 12884901888 | bytes 25165824 | tf_op jit(solution)/shard_map/second_inner/pallas_call | solution.py:393
  59.4 0.0 collective-permute-done.2.prev_ref.refs_6_
  59.4 1.9 %collective-permute-done.3.next_ref.refs_7_ = bf16[8,256,128]{2,1,0:T(8,128)(2,1)S(1)} collective-permute-done((bf16[8,256,128]{2,1,0:T(8,128)(2,1)S(1)}, bf16[8,256,128]{2,1,0:T(8,128)(2,1)S(1)}, u32[]{:S(2)}, u32[]{:S(2)}) %collective-permute-start.3) | collective-permute-done | bytes 524320 | tf_op jit(solution)/shard_map/ppermute | solution.py:18
  61.3 3.6 %second_outer.1 = (bf16[40,256,128]{2,1,0:T(8,128)(2,1)S(1)}, bf16[8,2,32,512]{3,2,1,0:T(8,128)(2,1)S(1)}, f32[32,128]{1,0:T(8,128)S(1)}) custom-call(s32[1]{0:T(128)} %bitcast.me_ref, s32[32,6]{1,0:T(8,128)S(1)} %add_select_fusion.cols, ...), custom_call_target="tpu_custom_call", output_to_operand_aliasing={{0}: (11, {}), {1}: (12, {}), {2}: (13, {})} | custom-call | flops 6442450944 | bytes 12582912 | tf_op jit(solution)/shard_map/second_outer/pallas_call | solution.py:393
  64.9 13.9 %all_to_all.33.y_ref = bf16[8,2,32,512]{3,2,1,0:T(8,128)(2,1)S(1)} all-to-all(bf16[8,2,32,512]{3,2,1,0:T(8,128)(2,1)S(1)} %get-tuple-element.45), channel_id=1, replica_groups=mesh['tile'=16,'mem'=8] {'mem'}, dimensions={0} | all-to-all | bytes 1048576 | tf_op jit(solution)/shard_map/all_to_all | solution.py:412
  78.8 0.3 residual_second.1
  79.1 13.1 %all_to_all.34.res_ref.refs_11_ = bf16[8,2,32,512]{3,2,1,0:T(8,128)(2,1)S(1)} all-to-all(bf16[8,2,32,512]{3,2,1,0:T(8,128)(2,1)S(1)} %get-tuple-element.48), channel_id=1, replica_groups=mesh['tile'=16,'mem'=8] {'mem'}, dimensions={0} | all-to-all | bytes 1048576 | tf_op jit(solution)/shard_map/all_to_all | solution.py:412
  92.1 6.8 %adjoint_all.1 = (f32[40,256,128]{2,1,0:T(8,128)S(1)}, bf16[4,256,128]{2,1,0:T(8,128)(2,1)S(1)}, bf16[4,256,128]{2,1,0:T(8,128)(2,1)S(1)}, f32[128,128]{1,0:T(8,128)S(1)}) custom-call(s32[32,6]{1,0:T(8,128)S(1)} %add_select_fusion.cols, bf16[8,2,32,512]{3,2,1,0:T(8,128)(2,1)S(1)} %all_to_all.34.res_ref.refs_11_, ...), custom_call_target="tpu_custom_call", output_to_operand_aliasing={{3}: (4, {})} | custom-call | flops 12884901888 | bytes 25165824 | tf_op jit(solution)/shard_map/adjoint_all/pallas_call | solution.py:393
  98.9 2.6 %collective-permute-start.4 = (bf16[4,256,128]{2,1,0:T(8,128)(2,1)S(1)}, bf16[4,256,128]{2,1,0:T(8,128)(2,1)S(1)}, u32[]{:S(2)}, u32[]{:S(2)}) collective-permute-start(bf16[4,256,128]{2,1,0:T(8,128)(2,1)S(1)} %get-tuple-element.52), channel_id=1, source_target_pairs={{0,8},{8,16},{16,24},{24,32},{32,40},{40,48},{48,56},{56,64},{64,7... | collective-permute-start | bytes 786440 | tf_op jit(solution)/shard_map/ppermute | solution.py:18
  101.6 0.0 collective-permute-start.5
  101.6 15.5 %all_to_all.35 = f32[128,1,128]{2,1,0:T(1,128)S(1)} all-to-all(f32[128,1,128]{2,1,0:T(1,128)S(1)} %bitcast.6), channel_id=1, replica_groups=mesh['tile'=16,'mem'=8] {'tile','mem'}, dimensions={0} | all-to-all | bytes 131072 | tf_op jit(solution)/shard_map/all_to_all | solution.py:465
  117.0 0.0 collective-permute-done.4.refs_8_
  117.0 0.0 collective-permute-done.5.refs_9_
  117.0 5.6 %final.1 = (f32[8,32,4096]{2,1,0:T(8,128)}, f32[4,4096]{1,0:T(4,128)}, f32[8,32,4096]{2,1,0:T(8,128)}, f32[4,4096]{1,0:T(4,128)}) custom-call(s32[1]{0:T(128)} %bitcast.me_ref, f32[128,128]{1,0:T(8,128)S(1)} %bitcast.5, f32[8,32,4096]{2,1,0:T(8,128)S(1)} %get-tuple-element.37.alpha_ref.refs_1_, f32[4,4096]{1,0:T(4,128)S(1)} %copy-done.2, ...), custom_call_target="tpu_custom_call" | custom-call | tf_op jit(solution)/shard_map/final/pallas_call | solution.py:477
  (1 shorter events, 0.0 us)
Async XLA Ops:
  0.6 4.4 %copy-start.4 = (s32[32,6]{0,1:T(8,128)S(1)}, s32[32,6]{0,1:T(8,128)}, u32[]{:S(2)}) copy-start(s32[32,6]{0,1:T(8,128)} %param.14) | copy-start | bytes 2308
  0.6 4.5 %copy-start.3 = (f32[4,4096]{1,0:T(4,128)S(1)}, f32[4,4096]{1,0:T(4,128)}, u32[]{:S(2)}) copy-start(f32[4,4096]{1,0:T(4,128)} %refs_3_.1) | copy-start | bytes 196612
  0.7 4.5 %copy-start.2 = (f32[4,4096]{1,0:T(4,128)S(1)}, f32[4,4096]{1,0:T(4,128)}, u32[]{:S(2)}) copy-start(f32[4,4096]{1,0:T(4,128)} %refs_2_.1) | copy-start | bytes 196612
  2.0 9.7 %collective-permute-start = (bf16[8,32,512]{2,1,0:T(8,128)(2,1)S(1)}, bf16[8,32,512]{2,1,0:T(8,128)(2,1)S(1)}, u32[]{:S(2)}, u32[]{:S(2)}) collective-permute-start(bf16[8,32,512]{2,1,0:T(8,128)(2,1)S(1)} %get-tuple-element.29), channel_id=1, source_target_pairs={{0,8},{8,16},{16,24},{24,32},{32,40},{40,48},{48,56},{56,64},{64,7... | collective-permute-start | bytes 786440 | tf_op jit(solution)/shard_map/ppermute | solution.py:18
  5.0 6.6 %collective-permute-start.1 = (bf16[8,32,512]{2,1,0:T(8,128)(2,1)S(1)}, bf16[8,32,512]{2,1,0:T(8,128)(2,1)S(1)}, u32[]{:S(2)}, u32[]{:S(2)}) collective-permute-start(bf16[8,32,512]{2,1,0:T(8,128)(2,1)S(1)} %get-tuple-element.30), channel_id=1, source_target_pairs={{0,120},{8,0},{16,8},{24,16},{32,24},{40,32},{48,40},{56,48},{64,5... | collective-permute-start | bytes 786440 | tf_op jit(solution)/shard_map/ppermute | solution.py:18
  11.7 17.8 %copy-start = (f32[2,32,4096]{2,1,0:T(8,128)S(1)}, f32[2,32,4096]{2,1,0:T(8,128)}, u32[]{:S(2)}) copy-start(f32[2,32,4096]{2,1,0:T(8,128)} %rinv_ref.3) | copy-start | bytes 3145732
  11.7 17.8 %copy-start.1 = (f32[2,32,4096]{2,1,0:T(8,128)S(1)}, f32[2,32,4096]{2,1,0:T(8,128)}, u32[]{:S(2)}) copy-start(f32[2,32,4096]{2,1,0:T(8,128)} %innov_ref.3) | copy-start | bytes 3145732
  45.2 14.2 %collective-permute-start.2 = (bf16[8,256,128]{2,1,0:T(8,128)(2,1)S(1)}, bf16[8,256,128]{2,1,0:T(8,128)(2,1)S(1)}, u32[]{:S(2)}, u32[]{:S(2)}) collective-permute-start(bf16[8,256,128]{2,1,0:T(8,128)(2,1)S(1)} %get-tuple-element.40), channel_id=1, source_target_pairs={{0,8},{8,16},{16,24},{24,32},{32,40},{40,48},{48,56},{56,64},{64,7... | collective-permute-start | bytes 1572872 | tf_op jit(solution)/shard_map/ppermute | solution.py:18
  52.7 8.6 %collective-permute-start.3 = (bf16[8,256,128]{2,1,0:T(8,128)(2,1)S(1)}, bf16[8,256,128]{2,1,0:T(8,128)(2,1)S(1)}, u32[]{:S(2)}, u32[]{:S(2)}) collective-permute-start(bf16[8,256,128]{2,1,0:T(8,128)(2,1)S(1)} %get-tuple-element.41), channel_id=1, source_target_pairs={{0,120},{8,0},{16,8},{24,16},{32,24},{40,32},{48,40},{56,48},{64,5... | collective-permute-start | bytes 1572872 | tf_op jit(solution)/shard_map/ppermute | solution.py:18
  98.9 18.1 %collective-permute-start.4 = (bf16[4,256,128]{2,1,0:T(8,128)(2,1)S(1)}, bf16[4,256,128]{2,1,0:T(8,128)(2,1)S(1)}, u32[]{:S(2)}, u32[]{:S(2)}) collective-permute-start(bf16[4,256,128]{2,1,0:T(8,128)(2,1)S(1)} %get-tuple-element.52), channel_id=1, source_target_pairs={{0,8},{8,16},{16,24},{24,32},{32,40},{40,48},{48,56},{56,64},{64,7... | collective-permute-start | bytes 786440 | tf_op jit(solution)/shard_map/ppermute | solution.py:18
  101.6 15.5 %collective-permute-start.5 = (bf16[4,256,128]{2,1,0:T(8,128)(2,1)S(1)}, bf16[4,256,128]{2,1,0:T(8,128)(2,1)S(1)}, u32[]{:S(2)}, u32[]{:S(2)}) collective-permute-start(bf16[4,256,128]{2,1,0:T(8,128)(2,1)S(1)} %get-tuple-element.53), channel_id=1, source_target_pairs={{0,120},{8,0},{16,8},{24,16},{32,24},{40,32},{48,40},{56,48},{64,5... | collective-permute-start | bytes 786440 | tf_op jit(solution)/shard_map/ppermute | solution.py:18

commit v4 on v3

--- a/solution.py
+++ b/solution.py
@@ -20,6 +20,18 @@
 
 def resident(array):
     return pltpu.with_memory_space_constraint(array, pltpu.VMEM)
+
+
+def column(cols, i, s):
+    nblocks = cols.shape[1]
+    total = nblocks * lax.axis_size("tile")
+    c = cols[s, i] - lax.axis_index("tile").astype(jnp.int32) * nblocks + W
+    c = jnp.where(c < 0, c + total, c)
+    return jnp.where(c >= total, c - total, c)
+
+
+def rank():
+    return lax.axis_index("mem").astype(jnp.int32)
 
 
 def masked(full, me, share, first):
@@ -51,7 +63,7 @@
     for r in range(rows):
         i = d * rows + r
         sl = slice(r * B, (r + 1) * B)
-        lhs = jnp.concatenate([xs[cols[i, s]] for s in range(slots)], axis=1)
+        lhs = jnp.concatenate([xs[column(cols, i, s)] for s in range(slots)], axis=1)
         rhs = jnp.concatenate([coef_ref[i, s] for s in range(slots)], axis=1)
         loc = lax.dot_general(
             lhs, rhs, (((1,), (1,)), ((), ())), preferred_element_type=F32
@@ -62,16 +74,16 @@
             out_ref[d, t, :, sl] = inc.astype(BF16)
 
 
-def first_static(d, width, levels, me_ref, chi_ref, sig_ref):
+def first_static(d, width, levels, chi_ref, sig_ref):
     cut = lanes(d * width, width)
-    return spread(sig_ref[:, cut] * chi_ref[:, cut], me_ref[0], levels, 0)
-
-
-def second_static(d, width, levels, me_ref, chi_ref, sig_ref, res_ref, norm_ref):
+    return spread(sig_ref[:, cut] * chi_ref[:, cut], rank(), levels, 0)
+
+
+def second_static(d, width, levels, chi_ref, sig_ref, res_ref, norm_ref):
     cut = lanes(d * width, width)
     rsum = res_ref[d, 0].astype(F32) + res_ref[d, 1].astype(F32)
-    sig = spread(sig_ref[:, cut], me_ref[0], levels, 0)
-    chi = spread(chi_ref[:, cut], me_ref[0], levels, 0)
+    sig = spread(sig_ref[:, cut], rank(), levels, 0)
+    chi = spread(chi_ref[:, cut], rank(), levels, 0)
     sr = sig * rsum
     gc = chi + sr
     sq = gc * gc
@@ -94,35 +106,22 @@
         out[...] = buf[0 if out is low_ref else 1].astype(BF16)
 
 
-def first_inner(
-    me_ref, cols, alpha_hbm, coef_hbm, anom_hbm, chi_ref, sig_ref,
-    alpha_ref, coef_ref, anom_ref, xs, out_ref, sem,
-):
+def first_inner(cols, alpha_hbm, coef_ref, anom_ref, chi_ref, sig_ref, alpha_ref, xs, out_ref, sem):
     members, levels, columns = alpha_ref.shape
     groups = out_ref.shape[0]
     width = columns // groups
     rows = width // B
     ml = members * levels
 
-    def copy(kind, d):
-        if kind == 0:
-            part = (slice(None), slice(None), pl.ds(d * width, width))
-            return pltpu.make_async_copy(alpha_hbm.at[part], alpha_ref.at[part], sem.at[kind, d])
-        if kind == 1:
-            part = pl.ds(d * rows, rows)
-            return pltpu.make_async_copy(coef_hbm.at[part], coef_ref.at[part], sem.at[kind, d])
-        part = (slice(None), slice(None), slice(None), pl.ds(d * width, width))
-        return pltpu.make_async_copy(anom_hbm.at[part], anom_ref.at[part], sem.at[kind, d])
-
-    order = [(0, 0), (0, 1)]
-    for d in range(1, groups - 1):
-        order += [(0, d + 1), (1, d), (2, d)]
-    tail = [(k, d) for d in (0, groups - 1) for k in (1, 2)]
-    for kind, d in order + tail:
-        copy(kind, d).start()
+    def copy(d):
+        part = (slice(None), slice(None), pl.ds(d * width, width))
+        return pltpu.make_async_copy(alpha_hbm.at[part], alpha_ref.at[part], sem.at[d])
+
+    for d in range(groups):
+        copy(d).start()
 
     def load(d):
-        copy(0, d).wait()
+        copy(d).wait()
         for r in range(rows):
             b = d * rows + r
             xs[W + b] = alpha_ref[:, :, b * B : (b + 1) * B].astype(BF16).reshape(ml, B)
@@ -131,16 +130,12 @@
     load(1)
     for d in range(1, groups - 1):
         load(d + 1)
-        copy(1, d).wait()
-        copy(2, d).wait()
-        static = first_static(d, width, levels, me_ref, chi_ref, sig_ref)
+        static = first_static(d, width, levels, chi_ref, sig_ref)
         localize_group(d, levels, 0, cols, xs, coef_ref, anom_ref, out_ref, static)
-    for kind, d in tail:
-        copy(kind, d).wait()
 
 
 def first_outer(
-    me_ref, cols, low_ref, high_ref, coef_ref, anom_ref, chi_ref, sig_ref, xs_in, part_ref, xs, out_ref
+    cols, low_ref, high_ref, coef_ref, anom_ref, chi_ref, sig_ref, xs_in, part_ref, xs, out_ref
 ):
     members, _, levels, columns = anom_ref.shape
     groups = out_ref.shape[0]
@@ -153,7 +148,7 @@
 
     def step(k, carry):
         d = k * (groups - 1)
-        static = first_static(d, width, levels, me_ref, chi_ref, sig_ref)
+        static = first_static(d, width, levels, chi_ref, sig_ref)
         localize_group(d, levels, 0, cols, xs, coef_ref, anom_ref, out_ref, static)
         return carry
 
@@ -176,10 +171,8 @@
             ],
         )
         w = w.astype(BF16).reshape(members * levels, B)
-        rhs = jnp.concatenate([coef_ref[i, s] for s in range(slots)], axis=1)
-        part = jnp.dot(w, rhs, preferred_element_type=F32)
         for s in range(slots):
-            acc_ref[cols[i, s]] += part[:, s * B : (s + 1) * B]
+            acc_ref[column(cols, i, s)] += jnp.dot(w, coef_ref[i, s], preferred_element_type=F32)
 
 
 def adjoint_edges(outer, cols, res_ref, anom_ref, coef_ref, acc_ref, low_ref, high_ref):
@@ -225,7 +218,7 @@
 
 
 def second_inner(
-    outer, me_ref, cols, res_ref, anom_ref, coef_ref, alpha_ref, chi_ref, sig_ref, acc_in,
+    outer, cols, res_ref, anom_ref, coef_ref, alpha_ref, chi_ref, sig_ref, acc_in,
     acc_ref, xs, out_ref, norm_ref,
 ):
     adjoint_rest(outer, cols, res_ref, anom_ref, coef_ref, acc_in, acc_ref)
@@ -242,7 +235,7 @@
     lax.fori_loop(2 * W, padded - 2 * W, block, 0, unroll=2)
 
     def step(d, carry):
-        static = second_static(d, width, levels, me_ref, chi_ref, sig_ref, res_ref, norm_ref)
+        static = second_static(d, width, levels, chi_ref, sig_ref, res_ref, norm_ref)
         localize_group(d, levels, 0, cols, xs, coef_ref, anom_ref, out_ref, static)
         return carry
 
@@ -250,7 +243,7 @@
 
 
 def second_outer(
-    outer, me_ref, cols, res_ref, anom_ref, coef_ref, alpha_ref, chi_ref, sig_ref, acc_ref, prev_ref,
+    outer, cols, res_ref, anom_ref, coef_ref, alpha_ref, chi_ref, sig_ref, acc_ref, prev_ref,
     next_ref, xs_in, part_in, norm_in, xs, out_ref, norm_ref,
 ):
     levels = alpha_ref.shape[1]
@@ -263,16 +256,16 @@
 
     def step(k, carry):
         d = jnp.where(k < outer, k, groups - 2 * outer + k)
-        static = second_static(d, width, levels, me_ref, chi_ref, sig_ref, res_ref, norm_ref)
+        static = second_static(d, width, levels, chi_ref, sig_ref, res_ref, norm_ref)
         localize_group(d, levels, 0, cols, xs, coef_ref, anom_ref, out_ref, static)
         return carry
 
     lax.fori_loop(0, 2 * outer, step, 0)
 
 
-def residual_first(me_ref, y_ref, rinv_ref, innov_ref, out_ref, inc_ref):
+def residual_first(y_ref, rinv_ref, innov_ref, out_ref, inc_ref):
     width = y_ref.shape[-1]
-    cut = lanes(me_ref[0] * width, width)
+    cut = lanes(rank() * width, width)
     y = jnp.sum(y_ref[...].astype(F32), axis=0)
     inc_ref[...] = y
     r = (rinv_ref[:, :, cut] * (y - innov_ref[:, :, cut])).astype(BF16)
@@ -281,10 +274,10 @@
 
 
 def residual_second(
-    me_ref, y_ref, rinv_ref, innov_ref, inc_ref, old_ref, norm_ref, out_ref, sum_ref
+    y_ref, rinv_ref, innov_ref, inc_ref, old_ref, norm_ref, out_ref, sum_ref
 ):
     width = y_ref.shape[-1]
-    cut = lanes(me_ref[0] * width, width)
+    cut = lanes(rank() * width, width)
     y = jnp.sum(y_ref[...].astype(F32), axis=0)
     r = (rinv_ref[:, :, cut] * (y - innov_ref[:, :, cut])).astype(BF16)
     for k in range(out_ref.shape[0]):
@@ -297,7 +290,7 @@
 
 
 def final_kernel(
-    me_ref, sums_ref, alpha_ref, chi_ref, sig_ref, acc1, acc2, prev1, next1, prev2, next2, res1, res2,
+    sums_ref, alpha_ref, chi_ref, sig_ref, acc1, acc2, prev1, next1, prev2, next2, res1, res2,
     an_ref, cn_ref, ga_ref, gc_ref,
 ):
     d = pl.program_id(0)
@@ -349,7 +342,7 @@
         parts = []
         for h in range(streams):
             s = res[h][d, 0].astype(F32) + res[h][d, 1].astype(F32)
-            parts.append(gathered(masked(s, me_ref[0], share, h * levels), share))
+            parts.append(gathered(masked(s, rank(), share, h * levels), share))
         return functools.reduce(jnp.add, parts)
 
     s1 = own_sum(res1)
@@ -369,12 +362,11 @@
     share = chi0.shape[0]
     groups = lax.axis_size("mem")
     tiles = lax.axis_size("tile")
-    me = lax.axis_index("mem").astype(jnp.int32).reshape(1)
     width = columns // groups
     levels = all_levels
     ml = members * levels
     padded = nblocks + 2 * W
-    cols = (taper_cols - lax.axis_index("tile") * nblocks + W) % (nblocks * tiles)
+    cols = taper_cols.T
 
     vm = pl.BlockSpec(memory_space=pltpu.VMEM)
     sm = pl.BlockSpec(memory_space=pltpu.SMEM)
@@ -414,21 +406,22 @@
     rim = sds((members, levels, W * B), BF16)
     high, low = call(
         edge_kernel, "edges", [], [alpha0], [rim, rim],
-        [pltpu.VMEM((2, members, levels, W * B), F32), pltpu.SemaphoreType.DMA((2,))], hbm=1,
+        [pltpu.VMEM((2, members, levels, W * B), F32), pltpu.SemaphoreType.DMA((2,))], hbm=1, rows=96,
     )
     low = shifted(low, "tile", 1)
     high = shifted(high, "tile", -1)
-    alpha, coef, anom, xs1, part1 = call(
-        first_inner, "first_inner", [me, cols], [alpha0, taper_coef, anomalies, chi0, sigma],
-        [sds(alpha0.shape, F32), sds(taper_coef.shape, BF16), sds(anomalies.shape, BF16), xs_out, pieces],
-        [pltpu.SemaphoreType.DMA((3, groups))], hbm=3, rows=24,
-    )
+    alpha, xs1, part1 = call(
+        first_inner, "first_inner", [cols], [alpha0, taper_coef, anomalies, chi0, sigma],
+        [sds(alpha0.shape, F32), xs_out, pieces],
+        [pltpu.SemaphoreType.DMA((groups,))], hbm=1, rows=24,
+    )
+    coef, anom = taper_coef, anomalies
     xs1, part1 = call(
-        first_outer, "first_outer", [me, cols], [low, high, coef, anom, chi0, sigma, xs1, part1],
+        first_outer, "first_outer", [cols], [low, high, coef, anom, chi0, sigma, xs1, part1],
         [xs_out, pieces], alias={6: 0, 7: 1}, rows=8,
     )
     got1 = exchanged(part1)
-    r1, inc1 = call(residual_first, "residual_first", [me], [got1, rinv, innov], [pieces, inc_out])
+    r1, inc1 = call(residual_first, "residual_first", [], [got1, rinv, innov], [pieces, inc_out])
     res1 = exchanged(r1)
 
     outer = 2 * W // (width // B)
@@ -440,18 +433,18 @@
     prev1 = shifted(high1, "tile", 1)
     next1 = shifted(low1, "tile", -1)
     acc1, xs2, part2, norm = call(
-        part(second_inner, outer), "second_inner", [me, cols],
+        part(second_inner, outer), "second_inner", [cols],
         [res1, anom, coef, alpha, chi0, sigma, acc1], [acc_out, xs_out, pieces, norm_out],
         alias={6: 0}, rows=32,
     )
     xs2, part2, norm = call(
-        part(second_outer, outer), "second_outer", [me, cols],
+        part(second_outer, outer), "second_outer", [cols],
         [res1, anom, coef, alpha, chi0, sigma, acc1, prev1, next1, xs2, part2, norm],
         [xs_out, pieces, norm_out], alias={9: 0, 10: 1, 11: 2}, rows=16,
     )
     got2 = exchanged(part2)
     r2, sums = call(
-        residual_second, "residual_second", [me], [got2, rinv, innov, inc1, r1, norm],
+        residual_second, "residual_second", [], [got2, rinv, innov, inc1, r1, norm],
         [pieces, sds((groups * tiles, B), F32)],
     )
     res2 = exchanged(r2)
@@ -469,15 +462,15 @@
     flat, tree = jax.tree.flatten(operands)
     count = len(flat)
 
-    def final(me_ref, *refs):
-        final_kernel(me_ref, *jax.tree.unflatten(tree, refs[:count]), *refs[count:])
+    def final(*refs):
+        final_kernel(*jax.tree.unflatten(tree, refs[:count]), *refs[count:])
 
     alpha_spec = pl.BlockSpec((members, all_levels, width), lambda d: (0, 0, d))
     chi_spec = pl.BlockSpec((share, width), lambda d: (0, d))
     out = pl.pallas_call(
         final,
         grid=(groups,),
-        in_specs=[sm] + [vm] * count,
+        in_specs=[vm] * count,
         out_specs=[alpha_spec, chi_spec, alpha_spec, chi_spec],
         out_shape=[
             jax.ShapeDtypeStruct(alpha0.shape, F32),
@@ -489,7 +482,7 @@
             dimension_semantics=("arbitrary",), vmem_limit_bytes=8 * MIB
         ),
         name="final",
-    )(me, *[resident(o) for o in flat])
+    )(*[resident(o) for o in flat])
     return tuple(out)
 
 

time: 123 us -> 120 us (0.976)
  Pallas kernels: 36.9 us -> 34 us
    pallas_call x9, Pallas kernels: 31.3 us -> 28.4 us  [call(): pl.pallas_call(kernel, in_specs=[sm] * len(scalars) + [anywhere] * hbm +...]
  transfers between devices with their start and end apart: 6 -> 6, of which waited for: 1 -> 2; matrix products, arithmetic and copies ran while one was open for 0% -> 0% of each run, Pallas kernels for 11% -> 10%
where the time goes in v4:
time: 120 us
  blocking collectives  70.1 us (58%)
  Pallas kernels  34 us (28%)
  starting transfers between devices  12.1 us (10%)
  waiting for transfers between devices  2.85 us (2%)
    all_to_all x4, blocking collectives, exchanged(): return lax.all_to_all(x, 'mem', 0, 0)  54.7 us
    pallas_call x9, Pallas kernels, call(): pl.pallas_call(kernel, in_specs=[sm] * len(scalars) + [anywhere] * hbm +...  28.4 us
    all_to_all x1, blocking collectives, body(): sums = lax.all_to_all(sums, ('tile', 'mem'), 0, 0, tiled=True)  15.4 us
    ppermute x6, starting transfers between devices, shifted(): lax.ppermute(array, axis, [(i, (i + by) % size) for i in range(size)])  12.1 us
    pallas_call x1, Pallas kernels, body(): pl.pallas_call(final, grid=(groups,), in_specs=[vm] * count, out_specs=[a...  5.66 us
    ppermute x6, waiting for transfers between devices, shifted(): lax.ppermute(array, axis, [(i, (i + by) % size) for i in range(size)])  2.85 us
  transfers between devices with their start and end apart: 6, of which 2 were waited for; matrix products, arithmetic and copies ran while one was open for 0% of the time, Pallas kernels for 10%

profile of v4, /device:TPU:1, one launch (start us, length us, event | category | flops | bytes accessed | tf_op | source)
XLA Modules:
  0.0 119.9 jit_solution(14555792309578877072)
XLA Ops:
  0.6 0.0 copy-start
  0.6 0.0 copy-start.1
  0.7 0.0 copy-start.5
  0.7 0.0 copy-start.4
  0.7 0.0 copy-start.6
  0.7 1.4 %edges.1 = (bf16[8,32,512]{2,1,0:T(8,128)(2,1)S(1)}, bf16[8,32,512]{2,1,0:T(8,128)(2,1)S(1)}) custom-call(f32[8,32,4096]{2,1,0:T(8,128)} %alpha_hbm.3), custom_call_target="tpu_custom_call" | custom-call | flops 38654705664 | bytes 75497472 | tf_op jit(solution)/shard_map/edges/pallas_call | solution.py:385
  2.1 3.1 %collective-permute-start = (bf16[8,32,512]{2,1,0:T(8,128)(2,1)S(1)}, bf16[8,32,512]{2,1,0:T(8,128)(2,1)S(1)}, u32[]{:S(2)}, u32[]{:S(2)}) collective-permute-start(bf16[8,32,512]{2,1,0:T(8,128)(2,1)S(1)} %get-tuple-element.27), channel_id=1, source_target_pairs={{0,8},{8,16},{16,24},{24,32},{32,40},{40,48},{48,56},{56,64},{64,7... | collective-permute-start | bytes 786440 | tf_op jit(solution)/shard_map/ppermute | solution.py:18
  5.2 0.0 collective-permute-start.1
  5.2 0.0 copy-done
  5.2 0.0 copy-done.1
  5.2 0.0 copy-done.5
  5.2 0.0 copy-done.4
  5.2 0.0 copy-done.6
  5.2 5.6 %first_inner.1 = (f32[8,32,4096]{2,1,0:T(8,128)S(1)}, bf16[40,256,128]{2,1,0:T(8,128)(2,1)S(1)}, bf16[8,2,32,512]{3,2,1,0:T(8,128)(2,1)S(1)}) custom-call(s32[6,32]{1,0:T(8,128)S(1)} %bitcast.7, f32[8,32,4096]{2,1,0:T(8,128)} %alpha_hbm.3, bf16[32,6,128,128]{3,2,1,0:T(8,128)(2,1)S(1)} %copy-done, bf16[8,2,32,4096]{3,2,1,0:T(8,128)(2,1)S(1)} %copy-done.1, ...), custom_call_target="tpu_custom_call" | custom-call | flops 9663676416 | bytes 18874368 | tf_op jit(solution)/shard_map/first_inner/pallas_call | solution.py:385
  10.8 0.0 collective-permute-done.low_ref
  10.8 0.5 collective-permute-done.1.high_ref
  11.3 0.0 copy-start.2
  11.3 0.0 copy-start.3
  11.3 1.9 %first_outer.1 = (bf16[40,256,128]{2,1,0:T(8,128)(2,1)S(1)}, bf16[8,2,32,512]{3,2,1,0:T(8,128)(2,1)S(1)}) custom-call(s32[6,32]{1,0:T(8,128)S(1)} %bitcast.8, bf16[8,32,512]{2,1,0:T(8,128)(2,1)S(1)} %collective-permute-done.low_ref, bf16[8,32,512]{2,1,0:T(8,128)(2,1)S(1)} %collective-permute-done.1.high_ref, ...), custom_call_target="tpu_custom_call", output_to_operand_aliasing={{0}: (7, {}), {1}: (8, {})} | custom-call | flops 3221225472 | bytes 6291456 | tf_op jit(solution)/shard_map/first_outer/pallas_call | solution.py:385
  13.1 15.9 %all_to_all.31.y_ref = bf16[8,2,32,512]{3,2,1,0:T(8,128)(2,1)S(1)} all-to-all(bf16[8,2,32,512]{3,2,1,0:T(8,128)(2,1)S(1)} %get-tuple-element.31), channel_id=1, replica_groups=mesh['tile'=16,'mem'=8] {'mem'}, dimensions={0} | all-to-all | bytes 1048576 | tf_op jit(solution)/shard_map/all_to_all | solution.py:404
  29.1 0.0 copy-done.2
  29.1 0.0 copy-done.3
  29.1 0.1 residual_first.1
  29.2 11.5 %all_to_all.32.res_ref.refs_10_ = bf16[8,2,32,512]{3,2,1,0:T(8,128)(2,1)S(1)} all-to-all(bf16[8,2,32,512]{3,2,1,0:T(8,128)(2,1)S(1)} %get-tuple-element.32.old_ref), channel_id=1, replica_groups=mesh['tile'=16,'mem'=8] {'mem'}, dimensions={0} | all-to-all | bytes 1048576 | tf_op jit(solution)/shard_map/all_to_all | solution.py:404
  40.7 3.6 %adjoint_edges.1 = (f32[40,256,128]{2,1,0:T(8,128)S(1)}, bf16[8,256,128]{2,1,0:T(8,128)(2,1)S(1)}, bf16[8,256,128]{2,1,0:T(8,128)(2,1)S(1)}) custom-call(s32[6,32]{1,0:T(8,128)S(1)} %bitcast.9, bf16[8,2,32,512]{3,2,1,0:T(8,128)(2,1)S(1)} %all_to_all.32.res_ref.refs_10_, bf16[8,2,32,4096]{3,2,1,0:T(8,128)(2,1)S(1)} %copy-done.1, ...), custom_call_target="tpu_custom_call" | custom-call | flops 6442450944 | bytes 12582912 | tf_op jit(solution)/shard_map/adjoint_edges/pallas_call | solution.py:385
  44.3 6.4 %collective-permute-start.2 = (bf16[8,256,128]{2,1,0:T(8,128)(2,1)S(1)}, bf16[8,256,128]{2,1,0:T(8,128)(2,1)S(1)}, u32[]{:S(2)}, u32[]{:S(2)}) collective-permute-start(bf16[8,256,128]{2,1,0:T(8,128)(2,1)S(1)} %get-tuple-element.36), channel_id=1, source_target_pairs={{0,8},{8,16},{16,24},{24,32},{32,40},{40,48},{48,56},{56,64},{64,7... | collective-permute-start | bytes 1572872 | tf_op jit(solution)/shard_map/ppermute | solution.py:18
  50.7 0.0 collective-permute-start.3
  50.7 6.2 %second_inner.1 = (f32[40,256,128]{2,1,0:T(8,128)S(1)}, bf16[40,256,128]{2,1,0:T(8,128)(2,1)S(1)}, bf16[8,2,32,512]{3,2,1,0:T(8,128)(2,1)S(1)}, f32[32,128]{1,0:T(8,128)S(1)}) custom-call(s32[6,32]{1,0:T(8,128)S(1)} %bitcast.10, bf16[8,2,32,512]{3,2,1,0:T(8,128)(2,1)S(1)} %all_to_all.32.res_ref.refs_10_, ...), custom_call_target="tpu_custom_call", output_to_operand_aliasing={{0}: (7, {})} | custom-call | flops 12884901888 | bytes 25165824 | tf_op jit(solution)/shard_map/second_inner/pallas_call | solution.py:385
  56.9 0.0 collective-permute-done.2.prev_ref.refs_6_
  57.0 2.4 %collective-permute-done.3.next_ref.refs_7_ = bf16[8,256,128]{2,1,0:T(8,128)(2,1)S(1)} collective-permute-done((bf16[8,256,128]{2,1,0:T(8,128)(2,1)S(1)}, bf16[8,256,128]{2,1,0:T(8,128)(2,1)S(1)}, u32[]{:S(2)}, u32[]{:S(2)}) %collective-permute-start.3) | collective-permute-done | bytes 524320 | tf_op jit(solution)/shard_map/ppermute | solution.py:18
  59.3 3.4 %second_outer.1 = (bf16[40,256,128]{2,1,0:T(8,128)(2,1)S(1)}, bf16[8,2,32,512]{3,2,1,0:T(8,128)(2,1)S(1)}, f32[32,128]{1,0:T(8,128)S(1)}) custom-call(s32[6,32]{1,0:T(8,128)S(1)} %bitcast.11, bf16[8,2,32,512]{3,2,1,0:T(8,128)(2,1)S(1)} %all_to_all.32.res_ref.refs_10_, ...), custom_call_target="tpu_custom_call", output_to_operand_aliasing={{0}: (10, {}), {1}: (11, {}), {2}: (12, {})} | custom-call | flops 6442450944 | bytes 12582912 | tf_op jit(solution)/shard_map/second_outer/pallas_call | solution.py:385
  62.7 14.1 %all_to_all.33.y_ref = bf16[8,2,32,512]{3,2,1,0:T(8,128)(2,1)S(1)} all-to-all(bf16[8,2,32,512]{3,2,1,0:T(8,128)(2,1)S(1)} %get-tuple-element.41), channel_id=1, replica_groups=mesh['tile'=16,'mem'=8] {'mem'}, dimensions={0} | all-to-all | bytes 1048576 | tf_op jit(solution)/shard_map/all_to_all | solution.py:404
  76.8 0.3 residual_second.1
  77.1 13.1 %all_to_all.34.res_ref.refs_11_ = bf16[8,2,32,512]{3,2,1,0:T(8,128)(2,1)S(1)} all-to-all(bf16[8,2,32,512]{3,2,1,0:T(8,128)(2,1)S(1)} %get-tuple-element.44), channel_id=1, replica_groups=mesh['tile'=16,'mem'=8] {'mem'}, dimensions={0} | all-to-all | bytes 1048576 | tf_op jit(solution)/shard_map/all_to_all | solution.py:404
  90.2 6.0 %adjoint_all.1 = (f32[40,256,128]{2,1,0:T(8,128)S(1)}, bf16[4,256,128]{2,1,0:T(8,128)(2,1)S(1)}, bf16[4,256,128]{2,1,0:T(8,128)(2,1)S(1)}, f32[128,128]{1,0:T(8,128)S(1)}) custom-call(s32[6,32]{1,0:T(8,128)S(1)} %bitcast.12, bf16[8,2,32,512]{3,2,1,0:T(8,128)(2,1)S(1)} %all_to_all.34.res_ref.refs_11_, ...), custom_call_target="tpu_custom_call", output_to_operand_aliasing={{3}: (4, {})} | custom-call | flops 12884901888 | bytes 25165824 | tf_op jit(solution)/shard_map/adjoint_all/pallas_call | solution.py:385
  96.2 2.6 %collective-permute-start.4 = (bf16[4,256,128]{2,1,0:T(8,128)(2,1)S(1)}, bf16[4,256,128]{2,1,0:T(8,128)(2,1)S(1)}, u32[]{:S(2)}, u32[]{:S(2)}) collective-permute-start(bf16[4,256,128]{2,1,0:T(8,128)(2,1)S(1)} %get-tuple-element.48), channel_id=1, source_target_pairs={{0,8},{8,16},{16,24},{24,32},{32,40},{40,48},{48,56},{56,64},{64,7... | collective-permute-start | bytes 786440 | tf_op jit(solution)/shard_map/ppermute | solution.py:18
  98.8 0.0 collective-permute-start.5
  98.8 15.4 %all_to_all.35 = f32[128,1,128]{2,1,0:T(1,128)S(1)} all-to-all(f32[128,1,128]{2,1,0:T(1,128)S(1)} %bitcast.6), channel_id=1, replica_groups=mesh['tile'=16,'mem'=8] {'tile','mem'}, dimensions={0} | all-to-all | bytes 131072 | tf_op jit(solution)/shard_map/all_to_all | solution.py:458
  114.2 0.0 collective-permute-done.4.refs_8_
  114.2 0.0 collective-permute-done.5.refs_9_
  114.2 5.7 %final.1 = (f32[8,32,4096]{2,1,0:T(8,128)}, f32[4,4096]{1,0:T(4,128)}, f32[8,32,4096]{2,1,0:T(8,128)}, f32[4,4096]{1,0:T(4,128)}) custom-call(f32[128,128]{1,0:T(8,128)S(1)} %bitcast.5, f32[8,32,4096]{2,1,0:T(8,128)S(1)} %get-tuple-element.33.alpha_ref.refs_1_, f32[4,4096]{1,0:T(4,128)S(1)} %copy-done.4, f32[4,4096]{1,0:T(4,128)S(1)} %copy-done.5, ...), custom_call_target="tpu_custom_call" | custom-call | tf_op jit(solution)/shard_map/final/pallas_call | solution.py:470
Async XLA Ops:
  0.6 4.5 %copy-start = (bf16[32,6,128,128]{3,2,1,0:T(8,128)(2,1)S(1)}, bf16[32,6,128,128]{3,2,1,0:T(8,128)(2,1)}, u32[]{:S(2)}) copy-start(bf16[32,6,128,128]{3,2,1,0:T(8,128)(2,1)} %coef_ref.11) | copy-start | bytes 18874372
  0.6 4.5 %copy-start.1 = (bf16[8,2,32,4096]{3,2,1,0:T(8,128)(2,1)S(1)}, bf16[8,2,32,4096]{3,2,1,0:T(8,128)(2,1)}, u32[]{:S(2)}) copy-start(bf16[8,2,32,4096]{3,2,1,0:T(8,128)(2,1)} %anom_ref.11) | copy-start | bytes 12582916
  0.7 4.5 %copy-start.5 = (f32[4,4096]{1,0:T(4,128)S(1)}, f32[4,4096]{1,0:T(4,128)}, u32[]{:S(2)}) copy-start(f32[4,4096]{1,0:T(4,128)} %refs_3_.1) | copy-start | bytes 196612
  0.7 4.5 %copy-start.4 = (f32[4,4096]{1,0:T(4,128)S(1)}, f32[4,4096]{1,0:T(4,128)}, u32[]{:S(2)}) copy-start(f32[4,4096]{1,0:T(4,128)} %refs_2_.1) | copy-start | bytes 196612
  0.7 4.5 %copy-start.6 = (s32[32,6]{0,1:T(8,128)S(1)}, s32[32,6]{0,1:T(8,128)}, u32[]{:S(2)}) copy-start(s32[32,6]{0,1:T(8,128)} %param.14) | copy-start | bytes 2308
  2.1 8.7 %collective-permute-start = (bf16[8,32,512]{2,1,0:T(8,128)(2,1)S(1)}, bf16[8,32,512]{2,1,0:T(8,128)(2,1)S(1)}, u32[]{:S(2)}, u32[]{:S(2)}) collective-permute-start(bf16[8,32,512]{2,1,0:T(8,128)(2,1)S(1)} %get-tuple-element.27), channel_id=1, source_target_pairs={{0,8},{8,16},{16,24},{24,32},{32,40},{40,48},{48,56},{56,64},{64,7... | collective-permute-start | bytes 786440 | tf_op jit(solution)/shard_map/ppermute | solution.py:18
  5.2 6.1 %collective-permute-start.1 = (bf16[8,32,512]{2,1,0:T(8,128)(2,1)S(1)}, bf16[8,32,512]{2,1,0:T(8,128)(2,1)S(1)}, u32[]{:S(2)}, u32[]{:S(2)}) collective-permute-start(bf16[8,32,512]{2,1,0:T(8,128)(2,1)S(1)} %get-tuple-element.28), channel_id=1, source_target_pairs={{0,120},{8,0},{16,8},{24,16},{32,24},{40,32},{48,40},{56,48},{64,5... | collective-permute-start | bytes 786440 | tf_op jit(solution)/shard_map/ppermute | solution.py:18
  11.3 17.8 %copy-start.2 = (f32[2,32,4096]{2,1,0:T(8,128)S(1)}, f32[2,32,4096]{2,1,0:T(8,128)}, u32[]{:S(2)}) copy-start(f32[2,32,4096]{2,1,0:T(8,128)} %rinv_ref.3) | copy-start | bytes 3145732
  11.3 17.8 %copy-start.3 = (f32[2,32,4096]{2,1,0:T(8,128)S(1)}, f32[2,32,4096]{2,1,0:T(8,128)}, u32[]{:S(2)}) copy-start(f32[2,32,4096]{2,1,0:T(8,128)} %innov_ref.3) | copy-start | bytes 3145732
  44.3 12.7 %collective-permute-start.2 = (bf16[8,256,128]{2,1,0:T(8,128)(2,1)S(1)}, bf16[8,256,128]{2,1,0:T(8,128)(2,1)S(1)}, u32[]{:S(2)}, u32[]{:S(2)}) collective-permute-start(bf16[8,256,128]{2,1,0:T(8,128)(2,1)S(1)} %get-tuple-element.36), channel_id=1, source_target_pairs={{0,8},{8,16},{16,24},{24,32},{32,40},{40,48},{48,56},{56,64},{64,7... | collective-permute-start | bytes 1572872 | tf_op jit(solution)/shard_map/ppermute | solution.py:18
  50.7 8.6 %collective-permute-start.3 = (bf16[8,256,128]{2,1,0:T(8,128)(2,1)S(1)}, bf16[8,256,128]{2,1,0:T(8,128)(2,1)S(1)}, u32[]{:S(2)}, u32[]{:S(2)}) collective-permute-start(bf16[8,256,128]{2,1,0:T(8,128)(2,1)S(1)} %get-tuple-element.37), channel_id=1, source_target_pairs={{0,120},{8,0},{16,8},{24,16},{32,24},{40,32},{48,40},{56,48},{64,5... | collective-permute-start | bytes 1572872 | tf_op jit(solution)/shard_map/ppermute | solution.py:18
  96.2 18.0 %collective-permute-start.4 = (bf16[4,256,128]{2,1,0:T(8,128)(2,1)S(1)}, bf16[4,256,128]{2,1,0:T(8,128)(2,1)S(1)}, u32[]{:S(2)}, u32[]{:S(2)}) collective-permute-start(bf16[4,256,128]{2,1,0:T(8,128)(2,1)S(1)} %get-tuple-element.48), channel_id=1, source_target_pairs={{0,8},{8,16},{16,24},{24,32},{32,40},{40,48},{48,56},{56,64},{64,7... | collective-permute-start | bytes 786440 | tf_op jit(solution)/shard_map/ppermute | solution.py:18
  98.8 15.4 %collective-permute-start.5 = (bf16[4,256,128]{2,1,0:T(8,128)(2,1)S(1)}, bf16[4,256,128]{2,1,0:T(8,128)(2,1)S(1)}, u32[]{:S(2)}, u32[]{:S(2)}) collective-permute-start(bf16[4,256,128]{2,1,0:T(8,128)(2,1)S(1)} %get-tuple-element.49), channel_id=1, source_target_pairs={{0,120},{8,0},{16,8},{24,16},{32,24},{40,32},{48,40},{56,48},{64,5... | collective-permute-start | bytes 786440 | tf_op jit(solution)/shard_map/ppermute | solution.py:18

commit v5 on v4

--- a/solution.py
+++ b/solution.py
@@ -197,7 +197,10 @@
         high_ref[b] = acc_ref[padded - halo + b].astype(BF16)
 
 
-def adjoint_all(cols, res_ref, anom_ref, coef_ref, sum_in, acc_ref, low_ref, high_ref, sum_ref):
+def adjoint_all(cols, res_ref, anom_ref, coef_ref, acc_ref, low_ref, high_ref, sum_ref):
+    groups = res_ref.shape[0]
+    code = functools.reduce(jnp.add, [res_ref[d, 0, :16, -B:].astype(F32) for d in range(groups)])
+    sum_ref[...] = jnp.broadcast_to(code[:1], sum_ref.shape)
     adjoint_edges(res_ref.shape[0] // 2, cols, res_ref, anom_ref, coef_ref, acc_ref, low_ref, high_ref)
 
 
@@ -274,19 +277,30 @@
 
 
 def residual_second(
-    y_ref, rinv_ref, innov_ref, inc_ref, old_ref, norm_ref, out_ref, sum_ref
+    y_ref, rinv_ref, innov_ref, inc_ref, old_ref, norm_ref, out_ref
 ):
     width = y_ref.shape[-1]
     cut = lanes(rank() * width, width)
     y = jnp.sum(y_ref[...].astype(F32), axis=0)
     r = (rinv_ref[:, :, cut] * (y - innov_ref[:, :, cut])).astype(BF16)
     for k in range(out_ref.shape[0]):
-        out_ref[k] = r
+        out_ref[k, :, :, :width] = r
     change = (old_ref[0].astype(F32) - r.astype(F32)) * (inc_ref[...] - y)
     change = jnp.sum(change.reshape(-1, 8, width), axis=0)
     norm = norm_ref[...].reshape(-1, 8, B).sum(axis=0)
-    lane = lax.broadcasted_iota(jnp.int32, sum_ref.shape, 1)
-    sum_ref[...] = jnp.where(lane == 0, jnp.sum(norm), jnp.where(lane == 1, jnp.sum(change), 0.0))
+    lane = lax.broadcasted_iota(jnp.int32, (16, B), 1)
+    code = jnp.zeros((16, B), F32)
+    for base, total in ((0, jnp.sum(norm)), (3, jnp.sum(change))):
+        rest = jnp.full((16, B), total, F32)
+        for k in range(3):
+            piece = rest.astype(BF16).astype(F32)
+            code = jnp.where(lane == base + k, piece, code)
+            rest = rest - piece
+    code = code.astype(BF16)
+    for k in range(out_ref.shape[0]):
+        for t in range(out_ref.shape[1]):
+            for h in range(0, out_ref.shape[2], 16):
+                out_ref[k, t, h : h + 16, width:] = code
 
 
 def final_kernel(
@@ -302,8 +316,8 @@
     cut = lanes(d * width, width)
     totals = sum(jnp.sum(s[...], axis=0, keepdims=True) for s in sums_ref)
     lane = lax.broadcasted_iota(jnp.int32, totals.shape, 1)
-    norm = jnp.sum(jnp.where(lane == 0, totals, 0.0), axis=1, keepdims=True)
-    prod = norm + jnp.sum(jnp.where(lane == 1, totals, 0.0), axis=1, keepdims=True)
+    norm = jnp.sum(jnp.where(lane < 3, totals, 0.0), axis=1, keepdims=True)
+    prod = jnp.sum(jnp.where(lane < 6, totals, 0.0), axis=1, keepdims=True)
     step = norm / prod
 
     def rows_out(extra1, extra2):
@@ -341,7 +355,7 @@
     def own_sum(res):
         parts = []
         for h in range(streams):
-            s = res[h][d, 0].astype(F32) + res[h][d, 1].astype(F32)
+            s = res[h][d, 0, :, :width].astype(F32) + res[h][d, 1, :, :width].astype(F32)
             parts.append(gathered(masked(s, rank(), share, h * levels), share))
         return functools.reduce(jnp.add, parts)
 
@@ -443,19 +457,19 @@
         [xs_out, pieces, norm_out], alias={9: 0, 10: 1, 11: 2}, rows=16,
     )
     got2 = exchanged(part2)
-    r2, sums = call(
+    (r2,) = call(
         residual_second, "residual_second", [], [got2, rinv, innov, inc1, r1, norm],
-        [pieces, sds((groups * tiles, B), F32)],
+        [sds((groups, slot_count, levels, width + B), BF16)],
     )
     res2 = exchanged(r2)
     edge = sds((W, ml, B), BF16)
     acc2, low2, high2, sums = call(
-        adjoint_all, "adjoint_all", [cols], [res2, anom, coef, sums],
-        [acc_out, edge, edge, sds(sums.shape, F32)], alias={3: 3}, rows=32,
+        adjoint_all, "adjoint_all", [cols], [res2, anom, coef], [acc_out, edge, edge, sds((tiles, B), F32)],
+        rows=32,
     )
     prev2 = shifted(high2, "tile", 1)
     next2 = shifted(low2, "tile", -1)
-    sums = lax.all_to_all(sums, ("tile", "mem"), 0, 0, tiled=True)
+    sums = lax.all_to_all(sums, "tile", 0, 0, tiled=True)
     operands = [
         [sums], alpha, chi0, sigma, [acc1], [acc2], [prev1], [next1], [prev2], [next2], [res1], [res2]
     ]

time: 120 us -> 117 us (0.975)
  blocking collectives: 70.1 us -> 67.6 us
    all_to_all x1, blocking collectives: 15.4 us -> 11.1 us  [body(): sums = lax.all_to_all(sums, 'tile', 0, 0, tiled=True)]
    all_to_all x4, blocking collectives: 54.7 us -> 56.5 us  [exchanged(): return lax.all_to_all(x, 'mem', 0, 0)]
where the time goes in v5:
time: 117 us
  blocking collectives  67.6 us (58%)
  Pallas kernels  34.1 us (29%)
  starting transfers between devices  11.8 us (10%)
  waiting for transfers between devices  2.85 us (2%)
    all_to_all x4, blocking collectives, exchanged(): return lax.all_to_all(x, 'mem', 0, 0)  56.5 us
    pallas_call x9, Pallas kernels, call(): pl.pallas_call(kernel, in_specs=[sm] * len(scalars) + [anywhere] * hbm +...  28.5 us
    ppermute x6, starting transfers between devices, shifted(): lax.ppermute(array, axis, [(i, (i + by) % size) for i in range(size)])  11.8 us
    all_to_all x1, blocking collectives, body(): sums = lax.all_to_all(sums, 'tile', 0, 0, tiled=True)  11.1 us
    pallas_call x1, Pallas kernels, body(): pl.pallas_call(final, grid=(groups,), in_specs=[vm] * count, out_specs=[a...  5.6 us
    ppermute x6, waiting for transfers between devices, shifted(): lax.ppermute(array, axis, [(i, (i + by) % size) for i in range(size)])  2.85 us
  transfers between devices with their start and end apart: 6, of which 2 were waited for; matrix products, arithmetic and copies ran while one was open for 0% of the time, Pallas kernels for 10%

profile of v5, /device:TPU:1, one launch (start us, length us, event | category | flops | bytes accessed | tf_op | source)
XLA Modules:
  0.0 117.1 jit_solution(8036175899186332765)
XLA Ops:
  0.6 0.0 copy-start
  0.6 0.0 copy-start.1
  0.7 0.0 copy-start.5
  0.7 0.0 copy-start.4
  0.7 0.0 copy-start.6
  0.7 1.4 %edges.1 = (bf16[8,32,512]{2,1,0:T(8,128)(2,1)S(1)}, bf16[8,32,512]{2,1,0:T(8,128)(2,1)S(1)}) custom-call(f32[8,32,4096]{2,1,0:T(8,128)} %alpha_hbm.3), custom_call_target="tpu_custom_call" | custom-call | flops 38654705664 | bytes 75497472 | tf_op jit(solution)/shard_map/edges/pallas_call | solution.py:399
  2.1 3.1 %collective-permute-start = (bf16[8,32,512]{2,1,0:T(8,128)(2,1)S(1)}, bf16[8,32,512]{2,1,0:T(8,128)(2,1)S(1)}, u32[]{:S(2)}, u32[]{:S(2)}) collective-permute-start(bf16[8,32,512]{2,1,0:T(8,128)(2,1)S(1)} %get-tuple-element.25), channel_id=1, source_target_pairs={{0,8},{8,16},{16,24},{24,32},{32,40},{40,48},{48,56},{56,64},{64,7... | collective-permute-start | bytes 786440 | tf_op jit(solution)/shard_map/ppermute | solution.py:18
  5.2 0.0 collective-permute-start.1
  5.2 0.0 copy-done
  5.2 0.0 copy-done.1
  5.2 0.0 copy-done.5
  5.2 0.0 copy-done.4
  5.2 0.0 copy-done.6
  5.2 5.6 %first_inner.1 = (f32[8,32,4096]{2,1,0:T(8,128)S(1)}, bf16[40,256,128]{2,1,0:T(8,128)(2,1)S(1)}, bf16[8,2,32,512]{3,2,1,0:T(8,128)(2,1)S(1)}) custom-call(s32[6,32]{1,0:T(8,128)S(1)} %bitcast.6, f32[8,32,4096]{2,1,0:T(8,128)} %alpha_hbm.3, bf16[32,6,128,128]{3,2,1,0:T(8,128)(2,1)S(1)} %copy-done, bf16[8,2,32,4096]{3,2,1,0:T(8,128)(2,1)S(1)} %copy-done.1, ...), custom_call_target="tpu_custom_call" | custom-call | flops 9663676416 | bytes 18874368 | tf_op jit(solution)/shard_map/first_inner/pallas_call | solution.py:399
  10.8 0.0 collective-permute-done.low_ref
  10.8 0.5 collective-permute-done.1.high_ref
  11.3 0.0 copy-start.2
  11.3 0.0 copy-start.3
  11.3 1.9 %first_outer.1 = (bf16[40,256,128]{2,1,0:T(8,128)(2,1)S(1)}, bf16[8,2,32,512]{3,2,1,0:T(8,128)(2,1)S(1)}) custom-call(s32[6,32]{1,0:T(8,128)S(1)} %bitcast.7, bf16[8,32,512]{2,1,0:T(8,128)(2,1)S(1)} %collective-permute-done.low_ref, bf16[8,32,512]{2,1,0:T(8,128)(2,1)S(1)} %collective-permute-done.1.high_ref, ...), custom_call_target="tpu_custom_call", output_to_operand_aliasing={{0}: (7, {}), {1}: (8, {})} | custom-call | flops 3221225472 | bytes 6291456 | tf_op jit(solution)/shard_map/first_outer/pallas_call | solution.py:399
  13.1 15.9 %all_to_all.31.y_ref = bf16[8,2,32,512]{3,2,1,0:T(8,128)(2,1)S(1)} all-to-all(bf16[8,2,32,512]{3,2,1,0:T(8,128)(2,1)S(1)} %get-tuple-element.29), channel_id=1, replica_groups=mesh['tile'=16,'mem'=8] {'mem'}, dimensions={0} | all-to-all | bytes 1048576 | tf_op jit(solution)/shard_map/all_to_all | solution.py:418
  29.1 0.0 copy-done.2
  29.1 0.0 copy-done.3
  29.1 0.1 residual_first.1
  29.2 11.5 %all_to_all.32.res_ref.refs_10_ = bf16[8,2,32,512]{3,2,1,0:T(8,128)(2,1)S(1)} all-to-all(bf16[8,2,32,512]{3,2,1,0:T(8,128)(2,1)S(1)} %get-tuple-element.30.old_ref), channel_id=1, replica_groups=mesh['tile'=16,'mem'=8] {'mem'}, dimensions={0} | all-to-all | bytes 1048576 | tf_op jit(solution)/shard_map/all_to_all | solution.py:418
  40.7 3.6 %adjoint_edges.1 = (f32[40,256,128]{2,1,0:T(8,128)S(1)}, bf16[8,256,128]{2,1,0:T(8,128)(2,1)S(1)}, bf16[8,256,128]{2,1,0:T(8,128)(2,1)S(1)}) custom-call(s32[6,32]{1,0:T(8,128)S(1)} %bitcast.8, bf16[8,2,32,512]{3,2,1,0:T(8,128)(2,1)S(1)} %all_to_all.32.res_ref.refs_10_, bf16[8,2,32,4096]{3,2,1,0:T(8,128)(2,1)S(1)} %copy-done.1, ...), custom_call_target="tpu_custom_call" | custom-call | flops 6442450944 | bytes 12582912 | tf_op jit(solution)/shard_map/adjoint_edges/pallas_call | solution.py:399
  44.3 6.4 %collective-permute-start.2 = (bf16[8,256,128]{2,1,0:T(8,128)(2,1)S(1)}, bf16[8,256,128]{2,1,0:T(8,128)(2,1)S(1)}, u32[]{:S(2)}, u32[]{:S(2)}) collective-permute-start(bf16[8,256,128]{2,1,0:T(8,128)(2,1)S(1)} %get-tuple-element.34), channel_id=1, source_target_pairs={{0,8},{8,16},{16,24},{24,32},{32,40},{40,48},{48,56},{56,64},{64,7... | collective-permute-start | bytes 1572872 | tf_op jit(solution)/shard_map/ppermute | solution.py:18
  50.7 0.0 collective-permute-start.3
  50.7 6.2 %second_inner.1 = (f32[40,256,128]{2,1,0:T(8,128)S(1)}, bf16[40,256,128]{2,1,0:T(8,128)(2,1)S(1)}, bf16[8,2,32,512]{3,2,1,0:T(8,128)(2,1)S(1)}, f32[32,128]{1,0:T(8,128)S(1)}) custom-call(s32[6,32]{1,0:T(8,128)S(1)} %bitcast.9, bf16[8,2,32,512]{3,2,1,0:T(8,128)(2,1)S(1)} %all_to_all.32.res_ref.refs_10_, ...), custom_call_target="tpu_custom_call", output_to_operand_aliasing={{0}: (7, {})} | custom-call | flops 12884901888 | bytes 25165824 | tf_op jit(solution)/shard_map/second_inner/pallas_call | solution.py:399
  56.9 0.0 collective-permute-done.2.prev_ref.refs_6_
  57.0 2.4 %collective-permute-done.3.next_ref.refs_7_ = bf16[8,256,128]{2,1,0:T(8,128)(2,1)S(1)} collective-permute-done((bf16[8,256,128]{2,1,0:T(8,128)(2,1)S(1)}, bf16[8,256,128]{2,1,0:T(8,128)(2,1)S(1)}, u32[]{:S(2)}, u32[]{:S(2)}) %collective-permute-start.3) | collective-permute-done | bytes 524320 | tf_op jit(solution)/shard_map/ppermute | solution.py:18
  59.3 3.3 %second_outer.1 = (bf16[40,256,128]{2,1,0:T(8,128)(2,1)S(1)}, bf16[8,2,32,512]{3,2,1,0:T(8,128)(2,1)S(1)}, f32[32,128]{1,0:T(8,128)S(1)}) custom-call(s32[6,32]{1,0:T(8,128)S(1)} %bitcast.10, bf16[8,2,32,512]{3,2,1,0:T(8,128)(2,1)S(1)} %all_to_all.32.res_ref.refs_10_, ...), custom_call_target="tpu_custom_call", output_to_operand_aliasing={{0}: (10, {}), {1}: (11, {}), {2}: (12, {})} | custom-call | flops 6442450944 | bytes 12582912 | tf_op jit(solution)/shard_map/second_outer/pallas_call | solution.py:399
  62.7 14.1 %all_to_all.33.y_ref = bf16[8,2,32,512]{3,2,1,0:T(8,128)(2,1)S(1)} all-to-all(bf16[8,2,32,512]{3,2,1,0:T(8,128)(2,1)S(1)} %get-tuple-element.39), channel_id=1, replica_groups=mesh['tile'=16,'mem'=8] {'mem'}, dimensions={0} | all-to-all | bytes 1048576 | tf_op jit(solution)/shard_map/all_to_all | solution.py:418
  76.8 0.3 residual_second.1
  77.1 14.9 %all_to_all.34.res_ref.refs_11_ = bf16[8,2,32,640]{3,2,1,0:T(8,128)(2,1)S(1)} all-to-all(bf16[8,2,32,640]{3,2,1,0:T(8,128)(2,1)S(1)} %residual_second.1), channel_id=1, replica_groups=mesh['tile'=16,'mem'=8] {'mem'}, dimensions={0} | all-to-all | bytes 1310720 | tf_op jit(solution)/shard_map/all_to_all | solution.py:418
  92.0 6.1 %adjoint_all.1 = (f32[40,256,128]{2,1,0:T(8,128)S(1)}, bf16[4,256,128]{2,1,0:T(8,128)(2,1)S(1)}, bf16[4,256,128]{2,1,0:T(8,128)(2,1)S(1)}, f32[16,128]{1,0:T(8,128)S(1)}) custom-call(s32[6,32]{1,0:T(8,128)S(1)} %bitcast.11, bf16[8,2,32,640]{3,2,1,0:T(8,128)(2,1)S(1)} %all_to_all.34.res_ref.refs_11_, bf16[8,2,32,4096]{3,2,1,0:T(8,128)(2,1)S(1)} %copy-done.1, ...), custom_call_target="tpu_custom_call" | custom-call | flops 12884901888 | bytes 25165824 | tf_op jit(solution)/shard_map/adjoint_all/pallas_call | solution.py:399
  98.1 2.2 %collective-permute-start.4 = (bf16[4,256,128]{2,1,0:T(8,128)(2,1)S(1)}, bf16[4,256,128]{2,1,0:T(8,128)(2,1)S(1)}, u32[]{:S(2)}, u32[]{:S(2)}) collective-permute-start(bf16[4,256,128]{2,1,0:T(8,128)(2,1)S(1)} %get-tuple-element.44), channel_id=1, source_target_pairs={{0,8},{8,16},{16,24},{24,32},{32,40},{40,48},{48,56},{56,64},{64,7... | collective-permute-start | bytes 786440 | tf_op jit(solution)/shard_map/ppermute | solution.py:18
  100.3 0.0 collective-permute-start.5
  100.3 11.1 %all_to_all.35 = f32[16,1,128]{2,1,0:T(1,128)S(1)} all-to-all(f32[16,1,128]{2,1,0:T(1,128)S(1)} %bitcast.12), channel_id=1, replica_groups=mesh['tile'=16,'mem'=8] {'tile'}, dimensions={0} | all-to-all | bytes 16384 | tf_op jit(solution)/shard_map/all_to_all | solution.py:472
  111.5 0.0 collective-permute-done.4.refs_8_
  111.5 0.0 collective-permute-done.5.refs_9_
  111.5 5.6 %final.1 = (f32[8,32,4096]{2,1,0:T(8,128)}, f32[4,4096]{1,0:T(4,128)}, f32[8,32,4096]{2,1,0:T(8,128)}, f32[4,4096]{1,0:T(4,128)}) custom-call(f32[16,128]{1,0:T(8,128)S(1)} %bitcast.5, f32[8,32,4096]{2,1,0:T(8,128)S(1)} %get-tuple-element.31.alpha_ref.refs_1_, f32[4,4096]{1,0:T(4,128)S(1)} %copy-done.4, f32[4,4096]{1,0:T(4,128)S(1)} %copy-done.5, ...), custom_call_target="tpu_custom_call" | custom-call | tf_op jit(solution)/shard_map/final/pallas_call | solution.py:484
Async XLA Ops:
  0.6 4.5 %copy-start = (bf16[32,6,128,128]{3,2,1,0:T(8,128)(2,1)S(1)}, bf16[32,6,128,128]{3,2,1,0:T(8,128)(2,1)}, u32[]{:S(2)}) copy-start(bf16[32,6,128,128]{3,2,1,0:T(8,128)(2,1)} %coef_ref.11) | copy-start | bytes 18874372
  0.6 4.5 %copy-start.1 = (bf16[8,2,32,4096]{3,2,1,0:T(8,128)(2,1)S(1)}, bf16[8,2,32,4096]{3,2,1,0:T(8,128)(2,1)}, u32[]{:S(2)}) copy-start(bf16[8,2,32,4096]{3,2,1,0:T(8,128)(2,1)} %anom_ref.11) | copy-start | bytes 12582916
  0.7 4.5 %copy-start.5 = (f32[4,4096]{1,0:T(4,128)S(1)}, f32[4,4096]{1,0:T(4,128)}, u32[]{:S(2)}) copy-start(f32[4,4096]{1,0:T(4,128)} %refs_3_.1) | copy-start | bytes 196612
  0.7 4.5 %copy-start.4 = (f32[4,4096]{1,0:T(4,128)S(1)}, f32[4,4096]{1,0:T(4,128)}, u32[]{:S(2)}) copy-start(f32[4,4096]{1,0:T(4,128)} %refs_2_.1) | copy-start | bytes 196612
  0.7 4.5 %copy-start.6 = (s32[32,6]{0,1:T(8,128)S(1)}, s32[32,6]{0,1:T(8,128)}, u32[]{:S(2)}) copy-start(s32[32,6]{0,1:T(8,128)} %param.14) | copy-start | bytes 2308
  2.1 8.7 %collective-permute-start = (bf16[8,32,512]{2,1,0:T(8,128)(2,1)S(1)}, bf16[8,32,512]{2,1,0:T(8,128)(2,1)S(1)}, u32[]{:S(2)}, u32[]{:S(2)}) collective-permute-start(bf16[8,32,512]{2,1,0:T(8,128)(2,1)S(1)} %get-tuple-element.25), channel_id=1, source_target_pairs={{0,8},{8,16},{16,24},{24,32},{32,40},{40,48},{48,56},{56,64},{64,7... | collective-permute-start | bytes 786440 | tf_op jit(solution)/shard_map/ppermute | solution.py:18
  5.2 6.1 %collective-permute-start.1 = (bf16[8,32,512]{2,1,0:T(8,128)(2,1)S(1)}, bf16[8,32,512]{2,1,0:T(8,128)(2,1)S(1)}, u32[]{:S(2)}, u32[]{:S(2)}) collective-permute-start(bf16[8,32,512]{2,1,0:T(8,128)(2,1)S(1)} %get-tuple-element.26), channel_id=1, source_target_pairs={{0,120},{8,0},{16,8},{24,16},{32,24},{40,32},{48,40},{56,48},{64,5... | collective-permute-start | bytes 786440 | tf_op jit(solution)/shard_map/ppermute | solution.py:18
  11.3 17.8 %copy-start.2 = (f32[2,32,4096]{2,1,0:T(8,128)S(1)}, f32[2,32,4096]{2,1,0:T(8,128)}, u32[]{:S(2)}) copy-start(f32[2,32,4096]{2,1,0:T(8,128)} %rinv_ref.3) | copy-start | bytes 3145732
  11.3 17.8 %copy-start.3 = (f32[2,32,4096]{2,1,0:T(8,128)S(1)}, f32[2,32,4096]{2,1,0:T(8,128)}, u32[]{:S(2)}) copy-start(f32[2,32,4096]{2,1,0:T(8,128)} %innov_ref.3) | copy-start | bytes 3145732
  44.3 12.7 %collective-permute-start.2 = (bf16[8,256,128]{2,1,0:T(8,128)(2,1)S(1)}, bf16[8,256,128]{2,1,0:T(8,128)(2,1)S(1)}, u32[]{:S(2)}, u32[]{:S(2)}) collective-permute-start(bf16[8,256,128]{2,1,0:T(8,128)(2,1)S(1)} %get-tuple-element.34), channel_id=1, source_target_pairs={{0,8},{8,16},{16,24},{24,32},{32,40},{40,48},{48,56},{56,64},{64,7... | collective-permute-start | bytes 1572872 | tf_op jit(solution)/shard_map/ppermute | solution.py:18
  50.7 8.6 %collective-permute-start.3 = (bf16[8,256,128]{2,1,0:T(8,128)(2,1)S(1)}, bf16[8,256,128]{2,1,0:T(8,128)(2,1)S(1)}, u32[]{:S(2)}, u32[]{:S(2)}) collective-permute-start(bf16[8,256,128]{2,1,0:T(8,128)(2,1)S(1)} %get-tuple-element.35), channel_id=1, source_target_pairs={{0,120},{8,0},{16,8},{24,16},{32,24},{40,32},{48,40},{56,48},{64,5... | collective-permute-start | bytes 1572872 | tf_op jit(solution)/shard_map/ppermute | solution.py:18
  98.1 13.3 %collective-permute-start.4 = (bf16[4,256,128]{2,1,0:T(8,128)(2,1)S(1)}, bf16[4,256,128]{2,1,0:T(8,128)(2,1)S(1)}, u32[]{:S(2)}, u32[]{:S(2)}) collective-permute-start(bf16[4,256,128]{2,1,0:T(8,128)(2,1)S(1)} %get-tuple-element.44), channel_id=1, source_target_pairs={{0,8},{8,16},{16,24},{24,32},{32,40},{40,48},{48,56},{56,64},{64,7... | collective-permute-start | bytes 786440 | tf_op jit(solution)/shard_map/ppermute | solution.py:18
  100.3 11.1 %collective-permute-start.5 = (bf16[4,256,128]{2,1,0:T(8,128)(2,1)S(1)}, bf16[4,256,128]{2,1,0:T(8,128)(2,1)S(1)}, u32[]{:S(2)}, u32[]{:S(2)}) collective-permute-start(bf16[4,256,128]{2,1,0:T(8,128)(2,1)S(1)} %get-tuple-element.45), channel_id=1, source_target_pairs={{0,120},{8,0},{16,8},{24,16},{32,24},{40,32},{48,40},{56,48},{64,5... | collective-permute-start | bytes 786440 | tf_op jit(solution)/shard_map/ppermute | solution.py:18

commit v6 on v5

--- a/solution.py
+++ b/solution.py
@@ -106,7 +106,9 @@
         out[...] = buf[0 if out is low_ref else 1].astype(BF16)
 
 
-def first_inner(cols, alpha_hbm, coef_ref, anom_ref, chi_ref, sig_ref, alpha_ref, xs, out_ref, sem):
+def first_inner(
+    cols, alpha_hbm, coef_ref, anom_ref, chi_ref, sig_ref, alpha_ref, xs, out_ref, zero_a, zero_b, sem
+):
     members, levels, columns = alpha_ref.shape
     groups = out_ref.shape[0]
     width = columns // groups
@@ -119,6 +121,13 @@
 
     for d in range(groups):
         copy(d).start()
+
+    def clear(b, carry):
+        zero_a[b] = jnp.zeros(zero_a.shape[1:], F32)
+        zero_b[b] = jnp.zeros(zero_b.shape[1:], F32)
+        return carry
+
+    lax.fori_loop(0, zero_a.shape[0], clear, 0)
 
     def load(d):
         copy(d).wait()
@@ -155,6 +164,13 @@
     lax.fori_loop(0, 2, step, 0)
 
 
+def res_block(res_ref, d, t, r, rows, levels):
+    if len(res_ref.shape) == 4:
+        return res_ref[d, t, :, r * B : (r + 1) * B].astype(F32)
+    base = (t * rows + r) * levels
+    return res_ref[d, base : base + levels].astype(F32)
+
+
 def adjoint_group(d, cols, res_ref, anom_ref, coef_ref, acc_ref):
     groups = res_ref.shape[0]
     nblocks, slots = coef_ref.shape[:2]
@@ -166,7 +182,8 @@
         w = functools.reduce(
             jnp.add,
             [
-                anom_ref[:, t, :, lanes(i * B, B)].astype(F32) * res_ref[d, t, :, sl].astype(F32)[None]
+                anom_ref[:, t, :, lanes(i * B, B)].astype(F32)
+                * res_block(res_ref, d, t, r, rows, levels)[None]
                 for t in range(slot_count)
             ],
         )
@@ -175,15 +192,9 @@
             acc_ref[column(cols, i, s)] += jnp.dot(w, coef_ref[i, s], preferred_element_type=F32)
 
 
-def adjoint_edges(outer, cols, res_ref, anom_ref, coef_ref, acc_ref, low_ref, high_ref):
+def adjoint_edges(outer, cols, res_ref, anom_ref, coef_ref, acc_in, acc_ref, low_ref, high_ref):
     groups = res_ref.shape[0]
     padded = acc_ref.shape[0]
-
-    def clear(b, carry):
-        acc_ref[b] = jnp.zeros(acc_ref.shape[1:], F32)
-        return carry
-
-    lax.fori_loop(0, padded, clear, 0)
 
     def step(k, carry):
         d = jnp.where(k < outer, k, groups - 2 * outer + k)
@@ -197,11 +208,12 @@
         high_ref[b] = acc_ref[padded - halo + b].astype(BF16)
 
 
-def adjoint_all(cols, res_ref, anom_ref, coef_ref, acc_ref, low_ref, high_ref, sum_ref):
+def adjoint_all(cols, res_ref, anom_ref, coef_ref, acc_in, acc_ref, low_ref, high_ref, sum_ref):
     groups = res_ref.shape[0]
-    code = functools.reduce(jnp.add, [res_ref[d, 0, :16, -B:].astype(F32) for d in range(groups)])
+    code = functools.reduce(jnp.add, [res_ref[d, res_ref.shape[1] - 16 :].astype(F32) for d in range(groups)])
     sum_ref[...] = jnp.broadcast_to(code[:1], sum_ref.shape)
-    adjoint_edges(res_ref.shape[0] // 2, cols, res_ref, anom_ref, coef_ref, acc_ref, low_ref, high_ref)
+    outer = res_ref.shape[0] // 2
+    adjoint_edges(outer, cols, res_ref, anom_ref, coef_ref, acc_in, acc_ref, low_ref, high_ref)
 
 
 def adjoint_rest(outer, cols, res_ref, anom_ref, coef_ref, acc_in, acc_ref):
@@ -283,8 +295,10 @@
     cut = lanes(rank() * width, width)
     y = jnp.sum(y_ref[...].astype(F32), axis=0)
     r = (rinv_ref[:, :, cut] * (y - innov_ref[:, :, cut])).astype(BF16)
+    blocks = [r[t, :, q * B : (q + 1) * B] for t in range(r.shape[0]) for q in range(width // B)]
     for k in range(out_ref.shape[0]):
-        out_ref[k, :, :, :width] = r
+        for q, block in enumerate(blocks):
+            out_ref[k, q * r.shape[1] : (q + 1) * r.shape[1]] = block
     change = (old_ref[0].astype(F32) - r.astype(F32)) * (inc_ref[...] - y)
     change = jnp.sum(change.reshape(-1, 8, width), axis=0)
     norm = norm_ref[...].reshape(-1, 8, B).sum(axis=0)
@@ -298,9 +312,7 @@
             rest = rest - piece
     code = code.astype(BF16)
     for k in range(out_ref.shape[0]):
-        for t in range(out_ref.shape[1]):
-            for h in range(0, out_ref.shape[2], 16):
-                out_ref[k, t, h : h + 16, width:] = code
+        out_ref[k, out_ref.shape[1] - 16 :] = code
 
 
 def final_kernel(
@@ -355,7 +367,13 @@
     def own_sum(res):
         parts = []
         for h in range(streams):
-            s = res[h][d, 0, :, :width].astype(F32) + res[h][d, 1, :, :width].astype(F32)
+            s = jnp.concatenate(
+                [
+                    res_block(res[h], d, 0, r, rows, levels) + res_block(res[h], d, 1, r, rows, levels)
+                    for r in range(rows)
+                ],
+                axis=1,
+            )
             parts.append(gathered(masked(s, rank(), share, h * levels), share))
         return functools.reduce(jnp.add, parts)
 
@@ -424,9 +442,9 @@
     )
     low = shifted(low, "tile", 1)
     high = shifted(high, "tile", -1)
-    alpha, xs1, part1 = call(
+    alpha, xs1, part1, acc1, acc2 = call(
         first_inner, "first_inner", [cols], [alpha0, taper_coef, anomalies, chi0, sigma],
-        [sds(alpha0.shape, F32), xs_out, pieces],
+        [sds(alpha0.shape, F32), xs_out, pieces, acc_out, acc_out],
         [pltpu.SemaphoreType.DMA((groups,))], hbm=1, rows=24,
     )
     coef, anom = taper_coef, anomalies
@@ -441,8 +459,8 @@
     outer = 2 * W // (width // B)
     edge = sds((2 * W, ml, B), BF16)
     acc1, low1, high1 = call(
-        part(adjoint_edges, outer), "adjoint_edges", [cols], [res1, anom, coef], [acc_out, edge, edge],
-        rows=16,
+        part(adjoint_edges, outer), "adjoint_edges", [cols], [res1, anom, coef, acc1],
+        [acc_out, edge, edge], alias={3: 0}, rows=16,
     )
     prev1 = shifted(high1, "tile", 1)
     next1 = shifted(low1, "tile", -1)
@@ -459,13 +477,13 @@
     got2 = exchanged(part2)
     (r2,) = call(
         residual_second, "residual_second", [], [got2, rinv, innov, inc1, r1, norm],
-        [sds((groups, slot_count, levels, width + B), BF16)],
+        [sds((groups, slot_count * levels * width // B + 16, B), BF16)],
     )
     res2 = exchanged(r2)
     edge = sds((W, ml, B), BF16)
     acc2, low2, high2, sums = call(
-        adjoint_all, "adjoint_all", [cols], [res2, anom, coef], [acc_out, edge, edge, sds((tiles, B), F32)],
-        rows=32,
+        adjoint_all, "adjoint_all", [cols], [res2, anom, coef, acc2],
+        [acc_out, edge, edge, sds((tiles, B), F32)], alias={3: 0}, rows=32,
     )
     prev2 = shifted(high2, "tile", 1)
     next2 = shifted(low2, "tile", -1)

time: 117 us -> 116 us (level)
  blocking collectives: 67.6 us -> 66.1 us
    all_to_all x4, blocking collectives: 56.5 us -> 54.9 us  [exchanged(): return lax.all_to_all(x, 'mem', 0, 0)]
where the time goes in v6:
time: 116 us; the launch traced here: 115 us
  blocking collectives  66.1 us (57%)
  Pallas kernels  33.2 us (29%)
  starting transfers between devices  12.4 us (11%)
  waiting for transfers between devices  2.86 us (2%)
    all_to_all x4, blocking collectives, exchanged(): return lax.all_to_all(x, 'mem', 0, 0)  54.9 us
    pallas_call x9, Pallas kernels, call(): pl.pallas_call(kernel, in_specs=[sm] * len(scalars) + [anywhere] * hbm +...  27.6 us
    ppermute x6, starting transfers between devices, shifted(): lax.ppermute(array, axis, [(i, (i + by) % size) for i in range(size)])  12.4 us
    all_to_all x1, blocking collectives, body(): sums = lax.all_to_all(sums, 'tile', 0, 0, tiled=True)  11.1 us
    pallas_call x1, Pallas kernels, body(): pl.pallas_call(final, grid=(groups,), in_specs=[vm] * count, out_specs=[a...  5.59 us
    ppermute x6, waiting for transfers between devices, shifted(): lax.ppermute(array, axis, [(i, (i + by) % size) for i in range(size)])  2.86 us
  transfers between devices with their start and end apart: 6, of which 2 were waited for; matrix products, arithmetic and copies ran while one was open for 0% of the time, Pallas kernels for 10%

profile of v6, /device:TPU:1, one launch (start us, length us, event | category | flops | bytes accessed | tf_op | source)
XLA Modules:
  0.0 115.3 jit_solution(107106929865005771)
XLA Ops:
  0.6 0.0 copy-start
  0.6 0.0 copy-start.1
  0.7 0.0 copy-start.5
  0.7 0.0 copy-start.4
  0.7 0.0 copy-start.6
  0.7 1.4 %edges.1 = (bf16[8,32,512]{2,1,0:T(8,128)(2,1)S(1)}, bf16[8,32,512]{2,1,0:T(8,128)(2,1)S(1)}) custom-call(f32[8,32,4096]{2,1,0:T(8,128)} %alpha_hbm.3), custom_call_target="tpu_custom_call" | custom-call | flops 38654705664 | bytes 75497472 | tf_op jit(solution)/shard_map/edges/pallas_call | solution.py:417
  2.1 3.1 %collective-permute-start = (bf16[8,32,512]{2,1,0:T(8,128)(2,1)S(1)}, bf16[8,32,512]{2,1,0:T(8,128)(2,1)S(1)}, u32[]{:S(2)}, u32[]{:S(2)}) collective-permute-start(bf16[8,32,512]{2,1,0:T(8,128)(2,1)S(1)} %get-tuple-element.27), channel_id=1, source_target_pairs={{0,8},{8,16},{16,24},{24,32},{32,40},{40,48},{48,56},{56,64},{64,7... | collective-permute-start | bytes 786440 | tf_op jit(solution)/shard_map/ppermute | solution.py:18
  5.2 0.0 collective-permute-start.1
  5.2 0.0 copy-done
  5.2 0.0 copy-done.1
  5.2 0.0 copy-done.5
  5.2 0.0 copy-done.4
  5.2 0.0 copy-done.6
  5.2 5.6 %first_inner.1 = (f32[8,32,4096]{2,1,0:T(8,128)S(1)}, bf16[40,256,128]{2,1,0:T(8,128)(2,1)S(1)}, bf16[8,2,32,512]{3,2,1,0:T(8,128)(2,1)S(1)}, f32[40,256,128]{2,1,0:T(8,128)S(1)}, f32[40,256,128]{2,1,0:T(8,128)S(1)}) custom-call(s32[6,32]{1,0:T(8,128)S(1)} %bitcast.6, f32[8,32,4096]{2,1,0:T(8,128)} %alpha_hbm.3, bf16[32,6,128,128]{3,2,1,0:T(8,128)(2,1)S(1)} %copy-done, ...), custom_call_target="tpu_custom_call" | custom-call | flops 9663676416 | bytes 18874368 | tf_op jit(solution)/shard_map/first_inner/pallas_call | solution.py:417
  10.8 0.0 collective-permute-done.low_ref
  10.8 0.5 collective-permute-done.1.high_ref
  11.3 0.0 copy-start.2
  11.3 0.0 copy-start.3
  11.3 1.9 %first_outer.1 = (bf16[40,256,128]{2,1,0:T(8,128)(2,1)S(1)}, bf16[8,2,32,512]{3,2,1,0:T(8,128)(2,1)S(1)}) custom-call(s32[6,32]{1,0:T(8,128)S(1)} %bitcast.7, bf16[8,32,512]{2,1,0:T(8,128)(2,1)S(1)} %collective-permute-done.low_ref, bf16[8,32,512]{2,1,0:T(8,128)(2,1)S(1)} %collective-permute-done.1.high_ref, ...), custom_call_target="tpu_custom_call", output_to_operand_aliasing={{0}: (7, {}), {1}: (8, {})} | custom-call | flops 3221225472 | bytes 6291456 | tf_op jit(solution)/shard_map/first_outer/pallas_call | solution.py:417
  13.1 15.9 %all_to_all.31.y_ref = bf16[8,2,32,512]{3,2,1,0:T(8,128)(2,1)S(1)} all-to-all(bf16[8,2,32,512]{3,2,1,0:T(8,128)(2,1)S(1)} %get-tuple-element.31), channel_id=1, replica_groups=mesh['tile'=16,'mem'=8] {'mem'}, dimensions={0} | all-to-all | bytes 1048576 | tf_op jit(solution)/shard_map/all_to_all | solution.py:436
  29.1 0.0 copy-done.2
  29.1 0.0 copy-done.3
  29.1 0.1 residual_first.1
  29.1 11.5 %all_to_all.32.res_ref.refs_10_ = bf16[8,2,32,512]{3,2,1,0:T(8,128)(2,1)S(1)} all-to-all(bf16[8,2,32,512]{3,2,1,0:T(8,128)(2,1)S(1)} %get-tuple-element.32.old_ref), channel_id=1, replica_groups=mesh['tile'=16,'mem'=8] {'mem'}, dimensions={0} | all-to-all | bytes 1048576 | tf_op jit(solution)/shard_map/all_to_all | solution.py:436
  40.6 3.2 %adjoint_edges.1 = (f32[40,256,128]{2,1,0:T(8,128)S(1)}, bf16[8,256,128]{2,1,0:T(8,128)(2,1)S(1)}, bf16[8,256,128]{2,1,0:T(8,128)(2,1)S(1)}) custom-call(s32[6,32]{1,0:T(8,128)S(1)} %bitcast.8, bf16[8,2,32,512]{3,2,1,0:T(8,128)(2,1)S(1)} %all_to_all.32.res_ref.refs_10_, bf16[8,2,32,4096]{3,2,1,0:T(8,128)(2,1)S(1)} %copy-done.1, ...), custom_call_target="tpu_custom_call", output_to_operand_aliasing={{0}: (4, {})} | custom-call | flops 6442450944 | bytes 12582912 | tf_op jit(solution)/shard_map/adjoint_edges/pallas_call | solution.py:417
  43.8 6.5 %collective-permute-start.2 = (bf16[8,256,128]{2,1,0:T(8,128)(2,1)S(1)}, bf16[8,256,128]{2,1,0:T(8,128)(2,1)S(1)}, u32[]{:S(2)}, u32[]{:S(2)}) collective-permute-start(bf16[8,256,128]{2,1,0:T(8,128)(2,1)S(1)} %get-tuple-element.37), channel_id=1, source_target_pairs={{0,8},{8,16},{16,24},{24,32},{32,40},{40,48},{48,56},{56,64},{64,7... | collective-permute-start | bytes 1572872 | tf_op jit(solution)/shard_map/ppermute | solution.py:18
  50.3 0.0 collective-permute-start.3
  50.3 6.2 %second_inner.1 = (f32[40,256,128]{2,1,0:T(8,128)S(1)}, bf16[40,256,128]{2,1,0:T(8,128)(2,1)S(1)}, bf16[8,2,32,512]{3,2,1,0:T(8,128)(2,1)S(1)}, f32[32,128]{1,0:T(8,128)S(1)}) custom-call(s32[6,32]{1,0:T(8,128)S(1)} %bitcast.9, bf16[8,2,32,512]{3,2,1,0:T(8,128)(2,1)S(1)} %all_to_all.32.res_ref.refs_10_, ...), custom_call_target="tpu_custom_call", output_to_operand_aliasing={{0}: (7, {})} | custom-call | flops 12884901888 | bytes 25165824 | tf_op jit(solution)/shard_map/second_inner/pallas_call | solution.py:417
  56.5 0.0 collective-permute-done.2.prev_ref.refs_6_
  56.5 2.4 %collective-permute-done.3.next_ref.refs_7_ = bf16[8,256,128]{2,1,0:T(8,128)(2,1)S(1)} collective-permute-done((bf16[8,256,128]{2,1,0:T(8,128)(2,1)S(1)}, bf16[8,256,128]{2,1,0:T(8,128)(2,1)S(1)}, u32[]{:S(2)}, u32[]{:S(2)}) %collective-permute-start.3) | collective-permute-done | bytes 524320 | tf_op jit(solution)/shard_map/ppermute | solution.py:18
  58.9 3.3 %second_outer.1 = (bf16[40,256,128]{2,1,0:T(8,128)(2,1)S(1)}, bf16[8,2,32,512]{3,2,1,0:T(8,128)(2,1)S(1)}, f32[32,128]{1,0:T(8,128)S(1)}) custom-call(s32[6,32]{1,0:T(8,128)S(1)} %bitcast.10, bf16[8,2,32,512]{3,2,1,0:T(8,128)(2,1)S(1)} %all_to_all.32.res_ref.refs_10_, ...), custom_call_target="tpu_custom_call", output_to_operand_aliasing={{0}: (10, {}), {1}: (11, {}), {2}: (12, {})} | custom-call | flops 6442450944 | bytes 12582912 | tf_op jit(solution)/shard_map/second_outer/pallas_call | solution.py:417
  62.3 14.1 %all_to_all.33.y_ref = bf16[8,2,32,512]{3,2,1,0:T(8,128)(2,1)S(1)} all-to-all(bf16[8,2,32,512]{3,2,1,0:T(8,128)(2,1)S(1)} %get-tuple-element.42), channel_id=1, replica_groups=mesh['tile'=16,'mem'=8] {'mem'}, dimensions={0} | all-to-all | bytes 1048576 | tf_op jit(solution)/shard_map/all_to_all | solution.py:436
  76.4 0.3 residual_second.1
  76.7 13.4 %all_to_all.34.res_ref.refs_11_ = bf16[8,272,128]{2,1,0:T(8,128)(2,1)S(1)} all-to-all(bf16[8,272,128]{2,1,0:T(8,128)(2,1)S(1)} %residual_second.1), channel_id=1, replica_groups=mesh['tile'=16,'mem'=8] {'mem'}, dimensions={0} | all-to-all | bytes 1114112 | tf_op jit(solution)/shard_map/all_to_all | solution.py:436
  90.1 5.6 %adjoint_all.1 = (f32[40,256,128]{2,1,0:T(8,128)S(1)}, bf16[4,256,128]{2,1,0:T(8,128)(2,1)S(1)}, bf16[4,256,128]{2,1,0:T(8,128)(2,1)S(1)}, f32[16,128]{1,0:T(8,128)S(1)}) custom-call(s32[6,32]{1,0:T(8,128)S(1)} %bitcast.11, bf16[8,272,128]{2,1,0:T(8,128)(2,1)S(1)} %all_to_all.34.res_ref.refs_11_, ...), custom_call_target="tpu_custom_call", output_to_operand_aliasing={{0}: (4, {})} | custom-call | flops 12884901888 | bytes 25165824 | tf_op jit(solution)/shard_map/adjoint_all/pallas_call | solution.py:417
  95.7 2.9 %collective-permute-start.4 = (bf16[4,256,128]{2,1,0:T(8,128)(2,1)S(1)}, bf16[4,256,128]{2,1,0:T(8,128)(2,1)S(1)}, u32[]{:S(2)}, u32[]{:S(2)}) collective-permute-start(bf16[4,256,128]{2,1,0:T(8,128)(2,1)S(1)} %get-tuple-element.48), channel_id=1, source_target_pairs={{0,8},{8,16},{16,24},{24,32},{32,40},{40,48},{48,56},{56,64},{64,7... | collective-permute-start | bytes 786440 | tf_op jit(solution)/shard_map/ppermute | solution.py:18
  98.6 0.0 collective-permute-start.5
  98.6 11.1 %all_to_all.35 = f32[16,1,128]{2,1,0:T(1,128)S(1)} all-to-all(f32[16,1,128]{2,1,0:T(1,128)S(1)} %bitcast.12), channel_id=1, replica_groups=mesh['tile'=16,'mem'=8] {'tile'}, dimensions={0} | all-to-all | bytes 16384 | tf_op jit(solution)/shard_map/all_to_all | solution.py:490
  109.7 0.0 collective-permute-done.4.refs_8_
  109.7 0.0 collective-permute-done.5.refs_9_
  109.7 5.6 %final.1 = (f32[8,32,4096]{2,1,0:T(8,128)}, f32[4,4096]{1,0:T(4,128)}, f32[8,32,4096]{2,1,0:T(8,128)}, f32[4,4096]{1,0:T(4,128)}) custom-call(f32[16,128]{1,0:T(8,128)S(1)} %bitcast.5, f32[8,32,4096]{2,1,0:T(8,128)S(1)} %get-tuple-element.33.alpha_ref.refs_1_, f32[4,4096]{1,0:T(4,128)S(1)} %copy-done.4, f32[4,4096]{1,0:T(4,128)S(1)} %copy-done.5, ...), custom_call_target="tpu_custom_call" | custom-call | tf_op jit(solution)/shard_map/final/pallas_call | solution.py:502
Async XLA Ops:
  0.6 4.5 %copy-start = (bf16[32,6,128,128]{3,2,1,0:T(8,128)(2,1)S(1)}, bf16[32,6,128,128]{3,2,1,0:T(8,128)(2,1)}, u32[]{:S(2)}) copy-start(bf16[32,6,128,128]{3,2,1,0:T(8,128)(2,1)} %coef_ref.11) | copy-start | bytes 18874372
  0.6 4.5 %copy-start.1 = (bf16[8,2,32,4096]{3,2,1,0:T(8,128)(2,1)S(1)}, bf16[8,2,32,4096]{3,2,1,0:T(8,128)(2,1)}, u32[]{:S(2)}) copy-start(bf16[8,2,32,4096]{3,2,1,0:T(8,128)(2,1)} %anom_ref.11) | copy-start | bytes 12582916
  0.7 4.5 %copy-start.5 = (f32[4,4096]{1,0:T(4,128)S(1)}, f32[4,4096]{1,0:T(4,128)}, u32[]{:S(2)}) copy-start(f32[4,4096]{1,0:T(4,128)} %refs_3_.1) | copy-start | bytes 196612
  0.7 4.5 %copy-start.4 = (f32[4,4096]{1,0:T(4,128)S(1)}, f32[4,4096]{1,0:T(4,128)}, u32[]{:S(2)}) copy-start(f32[4,4096]{1,0:T(4,128)} %refs_2_.1) | copy-start | bytes 196612
  0.7 4.5 %copy-start.6 = (s32[32,6]{0,1:T(8,128)S(1)}, s32[32,6]{0,1:T(8,128)}, u32[]{:S(2)}) copy-start(s32[32,6]{0,1:T(8,128)} %param.14) | copy-start | bytes 2308
  2.1 8.7 %collective-permute-start = (bf16[8,32,512]{2,1,0:T(8,128)(2,1)S(1)}, bf16[8,32,512]{2,1,0:T(8,128)(2,1)S(1)}, u32[]{:S(2)}, u32[]{:S(2)}) collective-permute-start(bf16[8,32,512]{2,1,0:T(8,128)(2,1)S(1)} %get-tuple-element.27), channel_id=1, source_target_pairs={{0,8},{8,16},{16,24},{24,32},{32,40},{40,48},{48,56},{56,64},{64,7... | collective-permute-start | bytes 786440 | tf_op jit(solution)/shard_map/ppermute | solution.py:18
  5.2 6.1 %collective-permute-start.1 = (bf16[8,32,512]{2,1,0:T(8,128)(2,1)S(1)}, bf16[8,32,512]{2,1,0:T(8,128)(2,1)S(1)}, u32[]{:S(2)}, u32[]{:S(2)}) collective-permute-start(bf16[8,32,512]{2,1,0:T(8,128)(2,1)S(1)} %get-tuple-element.28), channel_id=1, source_target_pairs={{0,120},{8,0},{16,8},{24,16},{32,24},{40,32},{48,40},{56,48},{64,5... | collective-permute-start | bytes 786440 | tf_op jit(solution)/shard_map/ppermute | solution.py:18
  11.3 17.8 %copy-start.2 = (f32[2,32,4096]{2,1,0:T(8,128)S(1)}, f32[2,32,4096]{2,1,0:T(8,128)}, u32[]{:S(2)}) copy-start(f32[2,32,4096]{2,1,0:T(8,128)} %rinv_ref.3) | copy-start | bytes 3145732
  11.3 17.8 %copy-start.3 = (f32[2,32,4096]{2,1,0:T(8,128)S(1)}, f32[2,32,4096]{2,1,0:T(8,128)}, u32[]{:S(2)}) copy-start(f32[2,32,4096]{2,1,0:T(8,128)} %innov_ref.3) | copy-start | bytes 3145732
  43.8 12.7 %collective-permute-start.2 = (bf16[8,256,128]{2,1,0:T(8,128)(2,1)S(1)}, bf16[8,256,128]{2,1,0:T(8,128)(2,1)S(1)}, u32[]{:S(2)}, u32[]{:S(2)}) collective-permute-start(bf16[8,256,128]{2,1,0:T(8,128)(2,1)S(1)} %get-tuple-element.37), channel_id=1, source_target_pairs={{0,8},{8,16},{16,24},{24,32},{32,40},{40,48},{48,56},{56,64},{64,7... | collective-permute-start | bytes 1572872 | tf_op jit(solution)/shard_map/ppermute | solution.py:18
  50.3 8.6 %collective-permute-start.3 = (bf16[8,256,128]{2,1,0:T(8,128)(2,1)S(1)}, bf16[8,256,128]{2,1,0:T(8,128)(2,1)S(1)}, u32[]{:S(2)}, u32[]{:S(2)}) collective-permute-start(bf16[8,256,128]{2,1,0:T(8,128)(2,1)S(1)} %get-tuple-element.38), channel_id=1, source_target_pairs={{0,120},{8,0},{16,8},{24,16},{32,24},{40,32},{48,40},{56,48},{64,5... | collective-permute-start | bytes 1572872 | tf_op jit(solution)/shard_map/ppermute | solution.py:18
  95.7 14.0 %collective-permute-start.4 = (bf16[4,256,128]{2,1,0:T(8,128)(2,1)S(1)}, bf16[4,256,128]{2,1,0:T(8,128)(2,1)S(1)}, u32[]{:S(2)}, u32[]{:S(2)}) collective-permute-start(bf16[4,256,128]{2,1,0:T(8,128)(2,1)S(1)} %get-tuple-element.48), channel_id=1, source_target_pairs={{0,8},{8,16},{16,24},{24,32},{32,40},{40,48},{48,56},{56,64},{64,7... | collective-permute-start | bytes 786440 | tf_op jit(solution)/shard_map/ppermute | solution.py:18
  98.6 11.1 %collective-permute-start.5 = (bf16[4,256,128]{2,1,0:T(8,128)(2,1)S(1)}, bf16[4,256,128]{2,1,0:T(8,128)(2,1)S(1)}, u32[]{:S(2)}, u32[]{:S(2)}) collective-permute-start(bf16[4,256,128]{2,1,0:T(8,128)(2,1)S(1)} %get-tuple-element.49), channel_id=1, source_target_pairs={{0,120},{8,0},{16,8},{24,16},{32,24},{40,32},{48,40},{56,48},{64,5... | collective-permute-start | bytes 786440 | tf_op jit(solution)/shard_map/ppermute | solution.py:18

commit v7 on v6

--- a/solution.py
+++ b/solution.py
@@ -161,7 +161,7 @@
         localize_group(d, levels, 0, cols, xs, coef_ref, anom_ref, out_ref, static)
         return carry
 
-    lax.fori_loop(0, 2, step, 0)
+    lax.fori_loop(0, 2, step, 0, unroll=2)
 
 
 def res_block(res_ref, d, t, r, rows, levels):
@@ -201,7 +201,7 @@
         adjoint_group(d, cols, res_ref, anom_ref, coef_ref, acc_ref)
         return carry
 
-    lax.fori_loop(0, 2 * outer, step, 0)
+    lax.fori_loop(0, 2 * outer, step, 0, unroll=2)
     halo = low_ref.shape[0]
     for b in range(halo):
         low_ref[b] = acc_ref[b].astype(BF16)
@@ -221,7 +221,7 @@
         adjoint_group(d, cols, res_ref, anom_ref, coef_ref, acc_ref)
         return carry
 
-    lax.fori_loop(outer, res_ref.shape[0] - outer, step, 0)
+    lax.fori_loop(outer, res_ref.shape[0] - outer, step, 0, unroll=2)
 
 
 def second_block(b, adj, alpha_ref, xs, norm_ref, own):
@@ -254,7 +254,7 @@
         localize_group(d, levels, 0, cols, xs, coef_ref, anom_ref, out_ref, static)
         return carry
 
-    lax.fori_loop(outer, groups - outer, step, 0)
+    lax.fori_loop(outer, groups - outer, step, 0, unroll=2)
 
 
 def second_outer(
@@ -275,7 +275,7 @@
         localize_group(d, levels, 0, cols, xs, coef_ref, anom_ref, out_ref, static)
         return carry
 
-    lax.fori_loop(0, 2 * outer, step, 0)
+    lax.fori_loop(0, 2 * outer, step, 0, unroll=2)
 
 
 def residual_first(y_ref, rinv_ref, innov_ref, out_ref, inc_ref):

time: 116 us -> 115 us (level)
  transfers between devices with their start and end apart: 6 -> 6, of which waited for: 2 -> 3; matrix products, arithmetic and copies ran while one was open for 0% -> 0% of each run, Pallas kernels for 10% -> 10%
where the time goes in v7:
time: 115 us
  blocking collectives  66.1 us (57%)
  Pallas kernels  32.3 us (28%)
  starting transfers between devices  12.4 us (11%)
  waiting for transfers between devices  3.12 us (3%)
    all_to_all x4, blocking collectives, exchanged(): return lax.all_to_all(x, 'mem', 0, 0)  54.9 us
    pallas_call x9, Pallas kernels, call(): pl.pallas_call(kernel, in_specs=[sm] * len(scalars) + [anywhere] * hbm +...  26.7 us
    ppermute x6, starting transfers between devices, shifted(): lax.ppermute(array, axis, [(i, (i + by) % size) for i in range(size)])  12.4 us
    all_to_all x1, blocking collectives, body(): sums = lax.all_to_all(sums, 'tile', 0, 0, tiled=True)  11.1 us
    pallas_call x1, Pallas kernels, body(): pl.pallas_call(final, grid=(groups,), in_specs=[vm] * count, out_specs=[a...  5.59 us
    ppermute x6, waiting for transfers between devices, shifted(): lax.ppermute(array, axis, [(i, (i + by) % size) for i in range(size)])  3.12 us
  transfers between devices with their start and end apart: 6, of which 3 were waited for; matrix products, arithmetic and copies ran while one was open for 0% of the time, Pallas kernels for 10%

profile of v7, /device:TPU:1, one launch (start us, length us, event | category | flops | bytes accessed | tf_op | source)
XLA Modules:
  0.0 114.7 jit_solution(14524748233972149128)
XLA Ops:
  0.6 0.0 copy-start
  0.6 0.0 copy-start.1
  0.7 0.0 copy-start.5
  0.7 0.0 copy-start.4
  0.7 0.0 copy-start.6
  0.7 1.4 %edges.1 = (bf16[8,32,512]{2,1,0:T(8,128)(2,1)S(1)}, bf16[8,32,512]{2,1,0:T(8,128)(2,1)S(1)}) custom-call(f32[8,32,4096]{2,1,0:T(8,128)} %alpha_hbm.3), custom_call_target="tpu_custom_call" | custom-call | flops 38654705664 | bytes 75497472 | tf_op jit(solution)/shard_map/edges/pallas_call | solution.py:417
  2.1 3.1 %collective-permute-start = (bf16[8,32,512]{2,1,0:T(8,128)(2,1)S(1)}, bf16[8,32,512]{2,1,0:T(8,128)(2,1)S(1)}, u32[]{:S(2)}, u32[]{:S(2)}) collective-permute-start(bf16[8,32,512]{2,1,0:T(8,128)(2,1)S(1)} %get-tuple-element.27), channel_id=1, source_target_pairs={{0,8},{8,16},{16,24},{24,32},{32,40},{40,48},{48,56},{56,64},{64,7... | collective-permute-start | bytes 786440 | tf_op jit(solution)/shard_map/ppermute | solution.py:18
  5.2 0.0 collective-permute-start.1
  5.2 0.0 copy-done
  5.2 0.0 copy-done.1
  5.2 0.0 copy-done.5
  5.2 0.0 copy-done.4
  5.2 0.0 copy-done.6
  5.2 5.6 %first_inner.1 = (f32[8,32,4096]{2,1,0:T(8,128)S(1)}, bf16[40,256,128]{2,1,0:T(8,128)(2,1)S(1)}, bf16[8,2,32,512]{3,2,1,0:T(8,128)(2,1)S(1)}, f32[40,256,128]{2,1,0:T(8,128)S(1)}, f32[40,256,128]{2,1,0:T(8,128)S(1)}) custom-call(s32[6,32]{1,0:T(8,128)S(1)} %bitcast.6, f32[8,32,4096]{2,1,0:T(8,128)} %alpha_hbm.3, bf16[32,6,128,128]{3,2,1,0:T(8,128)(2,1)S(1)} %copy-done, ...), custom_call_target="tpu_custom_call" | custom-call | flops 9663676416 | bytes 18874368 | tf_op jit(solution)/shard_map/first_inner/pallas_call | solution.py:417
  10.8 0.0 collective-permute-done.low_ref
  10.8 0.5 collective-permute-done.1.high_ref
  11.3 0.0 copy-start.2
  11.3 0.0 copy-start.3
  11.3 1.7 %first_outer.1 = (bf16[40,256,128]{2,1,0:T(8,128)(2,1)S(1)}, bf16[8,2,32,512]{3,2,1,0:T(8,128)(2,1)S(1)}) custom-call(s32[6,32]{1,0:T(8,128)S(1)} %bitcast.7, bf16[8,32,512]{2,1,0:T(8,128)(2,1)S(1)} %collective-permute-done.low_ref, bf16[8,32,512]{2,1,0:T(8,128)(2,1)S(1)} %collective-permute-done.1.high_ref, ...), custom_call_target="tpu_custom_call", output_to_operand_aliasing={{0}: (7, {}), {1}: (8, {})} | custom-call | flops 3221225472 | bytes 6291456 | tf_op jit(solution)/shard_map/first_outer/pallas_call | solution.py:417
  12.9 15.9 %all_to_all.31.y_ref = bf16[8,2,32,512]{3,2,1,0:T(8,128)(2,1)S(1)} all-to-all(bf16[8,2,32,512]{3,2,1,0:T(8,128)(2,1)S(1)} %get-tuple-element.31), channel_id=1, replica_groups=mesh['tile'=16,'mem'=8] {'mem'}, dimensions={0} | all-to-all | bytes 1048576 | tf_op jit(solution)/shard_map/all_to_all | solution.py:436
  28.8 0.0 copy-done.2
  28.8 0.0 copy-done.3
  28.8 0.1 residual_first.1
  28.9 11.5 %all_to_all.32.res_ref.refs_10_ = bf16[8,2,32,512]{3,2,1,0:T(8,128)(2,1)S(1)} all-to-all(bf16[8,2,32,512]{3,2,1,0:T(8,128)(2,1)S(1)} %get-tuple-element.32.old_ref), channel_id=1, replica_groups=mesh['tile'=16,'mem'=8] {'mem'}, dimensions={0} | all-to-all | bytes 1048576 | tf_op jit(solution)/shard_map/all_to_all | solution.py:436
  40.4 3.0 %adjoint_edges.1 = (f32[40,256,128]{2,1,0:T(8,128)S(1)}, bf16[8,256,128]{2,1,0:T(8,128)(2,1)S(1)}, bf16[8,256,128]{2,1,0:T(8,128)(2,1)S(1)}) custom-call(s32[6,32]{1,0:T(8,128)S(1)} %bitcast.8, bf16[8,2,32,512]{3,2,1,0:T(8,128)(2,1)S(1)} %all_to_all.32.res_ref.refs_10_, bf16[8,2,32,4096]{3,2,1,0:T(8,128)(2,1)S(1)} %copy-done.1, ...), custom_call_target="tpu_custom_call", output_to_operand_aliasing={{0}: (4, {})} | custom-call | flops 6442450944 | bytes 12582912 | tf_op jit(solution)/shard_map/adjoint_edges/pallas_call | solution.py:417
  43.5 6.5 %collective-permute-start.2 = (bf16[8,256,128]{2,1,0:T(8,128)(2,1)S(1)}, bf16[8,256,128]{2,1,0:T(8,128)(2,1)S(1)}, u32[]{:S(2)}, u32[]{:S(2)}) collective-permute-start(bf16[8,256,128]{2,1,0:T(8,128)(2,1)S(1)} %get-tuple-element.37), channel_id=1, source_target_pairs={{0,8},{8,16},{16,24},{24,32},{32,40},{40,48},{48,56},{56,64},{64,7... | collective-permute-start | bytes 1572872 | tf_op jit(solution)/shard_map/ppermute | solution.py:18
  49.9 0.0 collective-permute-start.3
  49.9 6.0 %second_inner.1 = (f32[40,256,128]{2,1,0:T(8,128)S(1)}, bf16[40,256,128]{2,1,0:T(8,128)(2,1)S(1)}, bf16[8,2,32,512]{3,2,1,0:T(8,128)(2,1)S(1)}, f32[32,128]{1,0:T(8,128)S(1)}) custom-call(s32[6,32]{1,0:T(8,128)S(1)} %bitcast.9, bf16[8,2,32,512]{3,2,1,0:T(8,128)(2,1)S(1)} %all_to_all.32.res_ref.refs_10_, ...), custom_call_target="tpu_custom_call", output_to_operand_aliasing={{0}: (7, {})} | custom-call | flops 12884901888 | bytes 25165824 | tf_op jit(solution)/shard_map/second_inner/pallas_call | solution.py:417
  55.9 0.2 collective-permute-done.2.prev_ref.refs_6_
  56.0 2.5 %collective-permute-done.3.next_ref.refs_7_ = bf16[8,256,128]{2,1,0:T(8,128)(2,1)S(1)} collective-permute-done((bf16[8,256,128]{2,1,0:T(8,128)(2,1)S(1)}, bf16[8,256,128]{2,1,0:T(8,128)(2,1)S(1)}, u32[]{:S(2)}, u32[]{:S(2)}) %collective-permute-start.3) | collective-permute-done | bytes 524320 | tf_op jit(solution)/shard_map/ppermute | solution.py:18
  58.5 3.1 %second_outer.1 = (bf16[40,256,128]{2,1,0:T(8,128)(2,1)S(1)}, bf16[8,2,32,512]{3,2,1,0:T(8,128)(2,1)S(1)}, f32[32,128]{1,0:T(8,128)S(1)}) custom-call(s32[6,32]{1,0:T(8,128)S(1)} %bitcast.10, bf16[8,2,32,512]{3,2,1,0:T(8,128)(2,1)S(1)} %all_to_all.32.res_ref.refs_10_, ...), custom_call_target="tpu_custom_call", output_to_operand_aliasing={{0}: (10, {}), {1}: (11, {}), {2}: (12, {})} | custom-call | flops 6442450944 | bytes 12582912 | tf_op jit(solution)/shard_map/second_outer/pallas_call | solution.py:417
  61.6 14.1 %all_to_all.33.y_ref = bf16[8,2,32,512]{3,2,1,0:T(8,128)(2,1)S(1)} all-to-all(bf16[8,2,32,512]{3,2,1,0:T(8,128)(2,1)S(1)} %get-tuple-element.42), channel_id=1, replica_groups=mesh['tile'=16,'mem'=8] {'mem'}, dimensions={0} | all-to-all | bytes 1048576 | tf_op jit(solution)/shard_map/all_to_all | solution.py:436
  75.8 0.3 residual_second.1
  76.0 13.4 %all_to_all.34.res_ref.refs_11_ = bf16[8,272,128]{2,1,0:T(8,128)(2,1)S(1)} all-to-all(bf16[8,272,128]{2,1,0:T(8,128)(2,1)S(1)} %residual_second.1), channel_id=1, replica_groups=mesh['tile'=16,'mem'=8] {'mem'}, dimensions={0} | all-to-all | bytes 1114112 | tf_op jit(solution)/shard_map/all_to_all | solution.py:436
  89.4 5.7 %adjoint_all.1 = (f32[40,256,128]{2,1,0:T(8,128)S(1)}, bf16[4,256,128]{2,1,0:T(8,128)(2,1)S(1)}, bf16[4,256,128]{2,1,0:T(8,128)(2,1)S(1)}, f32[16,128]{1,0:T(8,128)S(1)}) custom-call(s32[6,32]{1,0:T(8,128)S(1)} %bitcast.11, bf16[8,272,128]{2,1,0:T(8,128)(2,1)S(1)} %all_to_all.34.res_ref.refs_11_, ...), custom_call_target="tpu_custom_call", output_to_operand_aliasing={{0}: (4, {})} | custom-call | flops 12884901888 | bytes 25165824 | tf_op jit(solution)/shard_map/adjoint_all/pallas_call | solution.py:417
  95.1 2.9 %collective-permute-start.4 = (bf16[4,256,128]{2,1,0:T(8,128)(2,1)S(1)}, bf16[4,256,128]{2,1,0:T(8,128)(2,1)S(1)}, u32[]{:S(2)}, u32[]{:S(2)}) collective-permute-start(bf16[4,256,128]{2,1,0:T(8,128)(2,1)S(1)} %get-tuple-element.48), channel_id=1, source_target_pairs={{0,8},{8,16},{16,24},{24,32},{32,40},{40,48},{48,56},{56,64},{64,7... | collective-permute-start | bytes 786440 | tf_op jit(solution)/shard_map/ppermute | solution.py:18
  98.0 0.0 collective-permute-start.5
  98.0 11.1 %all_to_all.35 = f32[16,1,128]{2,1,0:T(1,128)S(1)} all-to-all(f32[16,1,128]{2,1,0:T(1,128)S(1)} %bitcast.12), channel_id=1, replica_groups=mesh['tile'=16,'mem'=8] {'tile'}, dimensions={0} | all-to-all | bytes 16384 | tf_op jit(solution)/shard_map/all_to_all | solution.py:490
  109.1 0.0 collective-permute-done.4.refs_8_
  109.1 0.0 collective-permute-done.5.refs_9_
  109.1 5.6 %final.1 = (f32[8,32,4096]{2,1,0:T(8,128)}, f32[4,4096]{1,0:T(4,128)}, f32[8,32,4096]{2,1,0:T(8,128)}, f32[4,4096]{1,0:T(4,128)}) custom-call(f32[16,128]{1,0:T(8,128)S(1)} %bitcast.5, f32[8,32,4096]{2,1,0:T(8,128)S(1)} %get-tuple-element.33.alpha_ref.refs_1_, f32[4,4096]{1,0:T(4,128)S(1)} %copy-done.4, f32[4,4096]{1,0:T(4,128)S(1)} %copy-done.5, ...), custom_call_target="tpu_custom_call" | custom-call | tf_op jit(solution)/shard_map/final/pallas_call | solution.py:502
Async XLA Ops:
  0.6 4.5 %copy-start = (bf16[32,6,128,128]{3,2,1,0:T(8,128)(2,1)S(1)}, bf16[32,6,128,128]{3,2,1,0:T(8,128)(2,1)}, u32[]{:S(2)}) copy-start(bf16[32,6,128,128]{3,2,1,0:T(8,128)(2,1)} %coef_ref.11) | copy-start | bytes 18874372
  0.6 4.5 %copy-start.1 = (bf16[8,2,32,4096]{3,2,1,0:T(8,128)(2,1)S(1)}, bf16[8,2,32,4096]{3,2,1,0:T(8,128)(2,1)}, u32[]{:S(2)}) copy-start(bf16[8,2,32,4096]{3,2,1,0:T(8,128)(2,1)} %anom_ref.11) | copy-start | bytes 12582916
  0.7 4.5 %copy-start.5 = (f32[4,4096]{1,0:T(4,128)S(1)}, f32[4,4096]{1,0:T(4,128)}, u32[]{:S(2)}) copy-start(f32[4,4096]{1,0:T(4,128)} %refs_3_.1) | copy-start | bytes 196612
  0.7 4.5 %copy-start.4 = (f32[4,4096]{1,0:T(4,128)S(1)}, f32[4,4096]{1,0:T(4,128)}, u32[]{:S(2)}) copy-start(f32[4,4096]{1,0:T(4,128)} %refs_2_.1) | copy-start | bytes 196612
  0.7 4.5 %copy-start.6 = (s32[32,6]{0,1:T(8,128)S(1)}, s32[32,6]{0,1:T(8,128)}, u32[]{:S(2)}) copy-start(s32[32,6]{0,1:T(8,128)} %param.14) | copy-start | bytes 2308
  2.1 8.7 %collective-permute-start = (bf16[8,32,512]{2,1,0:T(8,128)(2,1)S(1)}, bf16[8,32,512]{2,1,0:T(8,128)(2,1)S(1)}, u32[]{:S(2)}, u32[]{:S(2)}) collective-permute-start(bf16[8,32,512]{2,1,0:T(8,128)(2,1)S(1)} %get-tuple-element.27), channel_id=1, source_target_pairs={{0,8},{8,16},{16,24},{24,32},{32,40},{40,48},{48,56},{56,64},{64,7... | collective-permute-start | bytes 786440 | tf_op jit(solution)/shard_map/ppermute | solution.py:18
  5.2 6.1 %collective-permute-start.1 = (bf16[8,32,512]{2,1,0:T(8,128)(2,1)S(1)}, bf16[8,32,512]{2,1,0:T(8,128)(2,1)S(1)}, u32[]{:S(2)}, u32[]{:S(2)}) collective-permute-start(bf16[8,32,512]{2,1,0:T(8,128)(2,1)S(1)} %get-tuple-element.28), channel_id=1, source_target_pairs={{0,120},{8,0},{16,8},{24,16},{32,24},{40,32},{48,40},{56,48},{64,5... | collective-permute-start | bytes 786440 | tf_op jit(solution)/shard_map/ppermute | solution.py:18
  11.3 17.6 %copy-start.2 = (f32[2,32,4096]{2,1,0:T(8,128)S(1)}, f32[2,32,4096]{2,1,0:T(8,128)}, u32[]{:S(2)}) copy-start(f32[2,32,4096]{2,1,0:T(8,128)} %rinv_ref.3) | copy-start | bytes 3145732
  11.3 17.6 %copy-start.3 = (f32[2,32,4096]{2,1,0:T(8,128)S(1)}, f32[2,32,4096]{2,1,0:T(8,128)}, u32[]{:S(2)}) copy-start(f32[2,32,4096]{2,1,0:T(8,128)} %innov_ref.3) | copy-start | bytes 3145732
  43.5 12.6 %collective-permute-start.2 = (bf16[8,256,128]{2,1,0:T(8,128)(2,1)S(1)}, bf16[8,256,128]{2,1,0:T(8,128)(2,1)S(1)}, u32[]{:S(2)}, u32[]{:S(2)}) collective-permute-start(bf16[8,256,128]{2,1,0:T(8,128)(2,1)S(1)} %get-tuple-element.37), channel_id=1, source_target_pairs={{0,8},{8,16},{16,24},{24,32},{32,40},{40,48},{48,56},{56,64},{64,7... | collective-permute-start | bytes 1572872 | tf_op jit(solution)/shard_map/ppermute | solution.py:18
  49.9 8.6 %collective-permute-start.3 = (bf16[8,256,128]{2,1,0:T(8,128)(2,1)S(1)}, bf16[8,256,128]{2,1,0:T(8,128)(2,1)S(1)}, u32[]{:S(2)}, u32[]{:S(2)}) collective-permute-start(bf16[8,256,128]{2,1,0:T(8,128)(2,1)S(1)} %get-tuple-element.38), channel_id=1, source_target_pairs={{0,120},{8,0},{16,8},{24,16},{32,24},{40,32},{48,40},{56,48},{64,5... | collective-permute-start | bytes 1572872 | tf_op jit(solution)/shard_map/ppermute | solution.py:18
  95.1 14.0 %collective-permute-start.4 = (bf16[4,256,128]{2,1,0:T(8,128)(2,1)S(1)}, bf16[4,256,128]{2,1,0:T(8,128)(2,1)S(1)}, u32[]{:S(2)}, u32[]{:S(2)}) collective-permute-start(bf16[4,256,128]{2,1,0:T(8,128)(2,1)S(1)} %get-tuple-element.48), channel_id=1, source_target_pairs={{0,8},{8,16},{16,24},{24,32},{32,40},{40,48},{48,56},{56,64},{64,7... | collective-permute-start | bytes 786440 | tf_op jit(solution)/shard_map/ppermute | solution.py:18
  98.0 11.1 %collective-permute-start.5 = (bf16[4,256,128]{2,1,0:T(8,128)(2,1)S(1)}, bf16[4,256,128]{2,1,0:T(8,128)(2,1)S(1)}, u32[]{:S(2)}, u32[]{:S(2)}) collective-permute-start(bf16[4,256,128]{2,1,0:T(8,128)(2,1)S(1)} %get-tuple-element.49), channel_id=1, source_target_pairs={{0,120},{8,0},{16,8},{24,16},{32,24},{40,32},{48,40},{56,48},{64,5... | collective-permute-start | bytes 786440 | tf_op jit(solution)/shard_map/ppermute | solution.py:18
